TPU v7x, 32 devices: a whole 2x2x4 slice. The times are simulated.
32 devices in a mesh: groups: 2 (over x), tx: 16 (over z, y, core).
Axes of the slice: x: 2, y: 2, z: 4, core: 2. Of those that a mesh axis runs over, the one named last changes fastest.
Arguments:
- masters: float32 [128, 1024], P(('groups', 'tx')), parts along dimension 0, may hold values from 0 to 1
- velocity: float32 [128, 1024], P(('groups', 'tx')), parts along dimension 0, may hold values from -4 to 4
- place_owner: int32 [4096, 1], P(('groups', 'tx')), parts along dimension 0, may hold values from 0 to 15; in each aligned block of 128 rows (0 to 127, 128 to 255, ...) at most 16 rows name the same one
- place_local: int32 [4096], P(('groups', 'tx')), parts along dimension 0, may hold values from 0 to 3
- place_row: int32 [4096], P(('groups', 'tx')), parts along dimension 0, may hold values from 0 to 32
- place_col: int32 [4096], P(('groups', 'tx')), parts along dimension 0, may hold values from 0 to 224
- row_taps: bfloat16 [12, 4, 2, 63], replicated, may hold values from -0.75 to 0.75
- col_taps: bfloat16 [12, 4, 2, 63], replicated, may hold values from -0.25 to 0.25
- mode_weights: float32 [12], replicated, may hold values from 0.02 to 0.2
- target: bfloat16 [2048, 256], P(('groups', 'tx')), parts along dimension 0, may hold values from 0 to 1
Outputs:
- resist_residual: float32 [2048, 256], P(('groups', 'tx')), parts along dimension 0
- velocity_new: float32 [128, 1024], P(('groups', 'tx')), parts along dimension 0
- masters_new: float32 [128, 1024], P(('groups', 'tx')), parts along dimension 0
There are 2 independent parts, one for each index of `groups`. A program takes and returns all parts, laid end to end along the dimension named above; an argument that names none is the same for every part. Nothing has to cross between parts.
Inputs may be any that keep to these rules, and one draw needn't show every extreme that they name: `place_owner`: among the placements of one device (aligned blocks of 128), at most 16 name any one owner, a bound that some block reaches.
All inputs are finite; a program needn't handle non-finite values.
Results may differ from a plain program's by a relative error of at most 0.0012.
Values may be sent and summed in bfloat16 or wider, within the bound.
No kernel may reach another device: no remote copies, remote signals or barrier semaphores. Data moves between devices by JAX's collectives and lax.ppermute only.
A program may use at most 192 MiB of HBM per device.

v0:
```python
import jax
import jax.numpy as jnp
from jax import lax
from jax.sharding import PartitionSpec as P

W = 256
MS = 32
TAPS = 63
HALF = 31
TERMS = 4
MODES = 12


steepness = 0.5
threshold = 8.0
momentum = 0.9
step_size = 0.05


def extended(block, sides, width):
    for axis, dim in sides:
        count = lax.axis_size(axis)
        forward = [(i, i + 1) for i in range(count - 1)]
        backward = [(target, source) for source, target in forward]
        low = lax.ppermute(
            lax.slice_in_dim(block, block.shape[dim] - width, None, axis=dim), axis, forward
        )
        high = lax.ppermute(lax.slice_in_dim(block, 0, width, axis=dim), axis, backward)
        block = jnp.concatenate([low, block, high], axis=dim)
    return block


def from_behind(value, axis, steps):
    count = lax.axis_size(axis)
    initial, last = (max(0, -steps), min(count, count - steps))
    return lax.ppermute(value, axis, [(source, source + steps) for source in range(initial, last)])


def all_row_bands(row_taps, rows_here):
    out_rows = jnp.arange(rows_here, dtype=jnp.int32)
    in_rows = jnp.arange(rows_here + 2 * HALF, dtype=jnp.int32)
    tap_iota = jnp.arange(TAPS, dtype=jnp.int32)
    picker = (in_rows[None, :, None] - out_rows[:, None, None] == tap_iota[None, None, :]).astype(
        jnp.bfloat16
    )
    filters = row_taps.reshape(MODES, 2 * TERMS, TAPS)
    return jnp.einsum("kct,rst->kcrs", filters, picker, preferred_element_type=jnp.float32).astype(
        jnp.bfloat16
    )


def all_column_bands(col_taps):
    cells = jnp.arange(W, dtype=jnp.int32)
    tap_iota = jnp.arange(TAPS, dtype=jnp.int32)
    picker = (cells[:, None, None] - cells[None, :, None] + HALF == tap_iota[None, None, :]).astype(
        jnp.bfloat16
    )
    bands = jnp.einsum(
        "kxpt,wot->kxpwo", col_taps, picker, preferred_element_type=jnp.float32
    ).astype(jnp.bfloat16)
    real_band = bands[:, :, 0]
    imag_band = bands[:, :, 1]
    from_real = jnp.concatenate([real_band, imag_band], axis=-1)
    from_imag = jnp.concatenate([-imag_band, real_band], axis=-1)
    return jnp.stack([from_real, from_imag], axis=2).reshape(MODES, 2 * TERMS, W, 2 * W)


def on_device(
    masters,
    velocity,
    place_owner,
    place_local,
    place_row,
    place_col,
    row_taps,
    col_taps,
    mode_weights,
    target,
):
    rows_here = target.shape[0]
    places = place_local.shape[0]
    owners_count = lax.axis_size("tx")
    owner_dev = place_owner[:, 0]
    master_half = masters.astype(jnp.bfloat16)
    master_count = masters.shape[0]
    offsets = jnp.arange(MS, dtype=jnp.int32)
    row_chosen = (
        place_row[:, None, None] + offsets[None, :, None]
        == jnp.arange(rows_here, dtype=jnp.int32)[None, None, :]
    )
    col_chosen = (
        place_col[:, None, None] + offsets[None, :, None]
        == jnp.arange(W, dtype=jnp.int32)[None, None, :]
    )
    capacity = 2 * places // owners_count
    place_iota = jnp.arange(places, dtype=jnp.int32)
    same_owner = (owner_dev[:, None] == owner_dev[None, :]) & (
        place_iota[None, :] < place_iota[:, None]
    )
    slot_rank = jnp.sum(same_owner.astype(jnp.int32), axis=1)
    slot_index = owner_dev * capacity + slot_rank
    slot_chosen = (
        slot_index[:, None] == jnp.arange(owners_count * capacity, dtype=jnp.int32)[None, :]
    )
    requests = jnp.sum(jnp.where(slot_chosen, (place_local + 1)[:, None], 0), axis=0).reshape(
        owners_count, capacity
    )
    received = lax.all_to_all(requests, "tx", split_axis=0, concat_axis=0, tiled=True)
    lookup = (received[..., None] - 1 == jnp.arange(master_count, dtype=jnp.int32)).astype(
        jnp.bfloat16
    )
    replies = jnp.einsum(
        "scm,mf->scf", lookup, master_half, preferred_element_type=jnp.float32
    ).astype(jnp.bfloat16)
    replies, asked = (replies, received)
    returned = lax.all_to_all(replies, "tx", split_axis=0, concat_axis=0, tiled=True)
    patterns = jnp.dot(
        slot_chosen.astype(jnp.bfloat16),
        returned.reshape(owners_count * capacity, MS * MS),
        preferred_element_type=jnp.float32,
    )
    pattern_half = patterns.reshape(places, MS, MS).astype(jnp.bfloat16)
    spread = jnp.einsum(
        "pab,pbj->paj",
        pattern_half,
        col_chosen.astype(jnp.bfloat16),
        preferred_element_type=jnp.float32,
    ).astype(jnp.bfloat16)
    mask = jnp.einsum(
        "pai,paj->ij", row_chosen.astype(jnp.bfloat16), spread, preferred_element_type=jnp.float32
    ).astype(jnp.bfloat16)
    padded_mask = extended(mask, (("tx", 0),), HALF)
    row_stack = all_row_bands(row_taps, rows_here)
    column_stack = all_column_bands(col_taps)

    def forward_mode(running, pair):
        row_band, column_band = pair
        field_y = jnp.einsum(
            "crs,sw->crw", row_band, padded_mask, preferred_element_type=jnp.float32
        ).astype(jnp.bfloat16)
        field_e = jnp.einsum(
            "crw,cwo->ro", field_y, column_band, preferred_element_type=jnp.float32
        )
        return (running, field_e)

    _, fields = lax.scan(forward_mode, jnp.zeros((), jnp.float32), (row_stack, column_stack))
    field_re = fields[:, :, :W]
    field_im = fields[:, :, W:]
    intensity = jnp.sum(
        mode_weights[:, None, None] * (field_re * field_re + field_im * field_im), 0
    )
    resist = jax.nn.sigmoid(steepness * (intensity - threshold))
    resist_residual = resist - target.astype(jnp.float32)
    grad_intensity = resist_residual * steepness * resist * (1.0 - resist)
    doubled = jnp.concatenate([grad_intensity, grad_intensity], axis=-1)
    grad_fields = (2.0 * mode_weights[:, None, None] * doubled[None] * fields).astype(jnp.bfloat16)

    def adjoint_mode(running, inputs):
        row_band, column_band, grad_field = inputs
        grad_y = jnp.einsum(
            "ro,cwo->crw", grad_field, column_band, preferred_element_type=jnp.float32
        ).astype(jnp.bfloat16)
        return (
            running
            + jnp.einsum("crs,crw->sw", row_band, grad_y, preferred_element_type=jnp.float32),
            None,
        )

    grad_padded, _ = lax.scan(
        adjoint_mode,
        jnp.zeros((rows_here + 2 * HALF, W), jnp.float32),
        (row_stack, column_stack, grad_fields),
    )
    top_rim = grad_padded[:HALF]
    bottom_rim = grad_padded[HALF + rows_here :]
    from_above = from_behind(bottom_rim, "tx", 1)
    from_below = from_behind(top_rim, "tx", -1)
    grad_mask = grad_padded[HALF : HALF + rows_here]
    grad_mask = grad_mask + jnp.pad(from_above, ((0, rows_here - HALF), (0, 0)))
    grad_mask = grad_mask + jnp.pad(from_below, ((rows_here - HALF, 0), (0, 0)))
    row_rows = jnp.einsum(
        "pai,ij->paj", row_chosen.astype(jnp.float32), grad_mask, precision=lax.Precision.HIGHEST
    )
    grad_patch = jnp.einsum(
        "paj,pcj->pac", row_rows, col_chosen.astype(jnp.float32), precision=lax.Precision.HIGHEST
    ).reshape(places, MS * MS)
    slot_grads = jnp.dot(
        slot_chosen.astype(jnp.float32).T, grad_patch, precision=lax.Precision.HIGHEST
    ).reshape(owners_count, capacity, MS * MS)
    arrived = lax.all_to_all(slot_grads, "tx", split_axis=0, concat_axis=0, tiled=True)
    lookup = (
        asked.reshape(-1)[None, :] - 1 == jnp.arange(master_count, dtype=jnp.int32)[:, None]
    ).astype(jnp.float32)
    master_grad = jnp.dot(
        lookup, arrived.reshape(owners_count * capacity, MS * MS), precision=lax.Precision.HIGHEST
    )
    velocity_new = momentum * velocity + master_grad
    masters_new = masters - step_size * velocity_new
    return (resist_residual, velocity_new, masters_new)


def solution(mesh):
    return jax.shard_map(
        on_device,
        mesh=mesh,
        in_specs=(
            P(("groups", "tx"), None),
            P(("groups", "tx"), None),
            P(("groups", "tx"), None),
            P(("groups", "tx")),
            P(("groups", "tx")),
            P(("groups", "tx")),
            P(),
            P(),
            P(),
            P(("groups", "tx"), None),
        ),
        out_specs=(P(("groups", "tx"), None), P(("groups", "tx"), None), P(("groups", "tx"), None)),
        check_vma=False,
    )
```

profile of v0, /device:TPU:0, one launch (start us, length us, event | category | flops | bytes accessed | tf_op | source)
XLA Modules:
  0.0 254.9 jit_solution(10167865873663665052)
XLA Ops:
  3.7 7.4 %all-to-all-start = ((s32[16,1,16]{2,1,0:T(1,128)}), s32[16,1,16]{2,1,0:T(1,128)S(1)}, u32[]{:S(2)}, u32[]{:S(2)}) async-start(s32[16,1,16]{2,1,0:T(1,128)} %all_to_all.12), calls=%async_computation | async-start | bytes 16384 | tf_op jit(solution)/shard_map/all_to_all | solution.py:108
  11.1 8.9 %convert_bitcast_fusion = bf16[12,4,2,256,256]{4,0,2,1,3:T(8,128)(2,1)} fusion(s32[256,256]{1,0:T(8,128)S(1)} %subtract_add_fusion, bf16[12,4,2,63]{3,2,1,0:T(2,128)(2,1)} %param.21), kind=kOutput, calls=%fused_computation.26 | convolution fusion | flops 803143680 | bytes 12857152 | tf_op jit(solution)/shard_map/kxpt,wot->kxpwo/dot_general | solution.py:58
  20.0 12.0 %slice_bitcast_fusion = (bf16[12,4,256,256]{3,0,1,2:T(8,128)(2,1)}, bf16[12,4,256,256]{3,0,1,2:T(8,128)(2,1)}) fusion(bf16[12,4,2,256,256]{4,0,2,1,3:T(8,128)(2,1)} %convert_bitcast_fusion), kind=kLoop, calls=%fused_computation.30 | loop fusion | bytes 25165824 | tf_op jit(solution)/shard_map/squeeze | solution.py:62
  32.0 7.2 %fusion.96 = bf16[12,4,256,256]{3,0,1,2:T(8,128)(2,1)} fusion(bf16[12,4,2,256,256]{4,0,2,1,3:T(8,128)(2,1)} %convert_bitcast_fusion), kind=kLoop, calls=%fused_computation.101 | loop fusion | flops 3145728 | bytes 12582912 | tf_op jit(solution)/shard_map/neg | solution.py:64
  40.0 25.1 %maximum_bitcast_fusion = (bf16[12,4,1,256,512]{4,0,1,3,2:T(8,128)(2,1)}, bf16[12,4,1,256,512]{4,0,1,3,2:T(8,128)(2,1)}) fusion(bf16[12,4,256,256]{3,0,1,2:T(8,128)(2,1)} %get-tuple-element.139, bf16[12,4,256,256]{3,0,1,2:T(8,128)(2,1)} %get-tuple-element.140, bf16[12,4,256,256]{3,0,1,2:T(8,128)(2,1)} %fusion.96), kind=kLoop, calls=%fused_computation.24 | loop fusion | flops 50331648 | bytes 44040192 | tf_op jit(solution)/shard_map/stack | solution.py:65
  67.1 6.0 %all-to-all-start.1 = ((bf16[16,16,1024]{2,1,0:T(8,128)(2,1)}), bf16[16,16,1024]{2,1,0:T(8,128)(2,1)S(1)}, u32[]{:S(2)}, u32[]{:S(2)}) async-start(bf16[16,16,1024]{2,1,0:T(8,128)(2,1)} %convolution_convert_fusion.1), calls=%async_computation.1 | async-start | bytes 1048576 | tf_op jit(solution)/shard_map/all_to_all | solution.py:116
  73.1 22.5 %pad_maximum_fusion = bf16[12,4,2,256,512]{4,0,1,3,2:T(8,128)(2,1)} fusion(bf16[12,4,1,256,512]{4,0,1,3,2:T(8,128)(2,1)} %get-tuple-element.142, bf16[12,4,1,256,512]{4,0,1,3,2:T(8,128)(2,1)} %get-tuple-element.141), kind=kLoop, calls=%fused_computation.23 | loop fusion | flops 12582912 | bytes 50331648 | tf_op jit(solution)/shard_map/stack | solution.py:65
  104.7 28.4 %copy.44 = bf16[12,4,2,256,512]{4,3,2,1,0:T(8,128)(2,1)} copy(bf16[12,4,2,256,512]{4,0,1,3,2:T(8,128)(2,1)} %pad_maximum_fusion) | data formatting | bytes 50331648 | tf_op jit(solution)/shard_map/stack | solution.py:65
  135.4 34.9 %while.21 = (s32[]{:T(128)}, f32[12,64,512]{2,1,0:T(8,128)}, bf16[12,8,64,126]{3,2,1,0:T(8,128)(2,1)}, bf16[126,256]{1,0:T(8,128)(2,1)S(1)}, bf16[12,8,256,512]{3,2,1,0:T(8,128)(2,1)}, /*index=5*/s32[]{:T(128)}) while((s32[]{:T(128)}, f32[12,64,512]{2,1,0:T(8,128)}, bf16[12,8,64,126]{3,2,1,0:T(8,128)(2,1)}, bf16[126,256]{1,0:T(8,128)(2,1)S(1)}, ...), condition=%wide.region_3.4_spmd, body=%wide.region_2.3_spmd.sunk | while | flops 167378944 | bytes 2425413 | solution.py:146
  135.4 2.9 %fusion.115 = f32[12,64,512]{2,1,0:T(8,128)} fusion(f32[12,64,512]{2,1,0:T(8,128)} %get-tuple-element.222, s32[]{:T(128)} %get-tuple-element.221, bf16[12,8,256,512]{3,2,1,0:T(8,128)(2,1)} %get-tuple-element.231, bf16[12,8,64,126]{3,2,1,0:T(8,128)(2,1)} %get-tuple-element.229, bf16[126,256]{1,0:T(8,128)(2,1)S(1)} %get-tuple-element.230), kind=kOutput, calls=%fused_computation.5.clone.1 | convolution fusion | flops 167378944 | bytes 2425344 | tf_op jit(solution)/shard_map/while/body/eval_jaxpr/crw,cwo->ro/dot_general | solution.py:141
  141.2 2.9 %fusion.115 = f32[12,64,512]{2,1,0:T(8,128)} fusion(f32[12,64,512]{2,1,0:T(8,128)} %get-tuple-element.222, s32[]{:T(128)} %get-tuple-element.221, bf16[12,8,256,512]{3,2,1,0:T(8,128)(2,1)} %get-tuple-element.231, bf16[12,8,64,126]{3,2,1,0:T(8,128)(2,1)} %get-tuple-element.229, bf16[126,256]{1,0:T(8,128)(2,1)S(1)} %get-tuple-element.230), kind=kOutput, calls=%fused_computation.5.clone.1 | convolution fusion | flops 167378944 | bytes 2425344 | tf_op jit(solution)/shard_map/while/body/eval_jaxpr/crw,cwo->ro/dot_general | solution.py:141
  147.0 2.9 %fusion.115 = f32[12,64,512]{2,1,0:T(8,128)} fusion(f32[12,64,512]{2,1,0:T(8,128)} %get-tuple-element.222, s32[]{:T(128)} %get-tuple-element.221, bf16[12,8,256,512]{3,2,1,0:T(8,128)(2,1)} %get-tuple-element.231, bf16[12,8,64,126]{3,2,1,0:T(8,128)(2,1)} %get-tuple-element.229, bf16[126,256]{1,0:T(8,128)(2,1)S(1)} %get-tuple-element.230), kind=kOutput, calls=%fused_computation.5.clone.1 | convolution fusion | flops 167378944 | bytes 2425344 | tf_op jit(solution)/shard_map/while/body/eval_jaxpr/crw,cwo->ro/dot_general | solution.py:141
  149.9 2.9 %fusion.115 = f32[12,64,512]{2,1,0:T(8,128)} fusion(f32[12,64,512]{2,1,0:T(8,128)} %get-tuple-element.222, s32[]{:T(128)} %get-tuple-element.221, bf16[12,8,256,512]{3,2,1,0:T(8,128)(2,1)} %get-tuple-element.231, bf16[12,8,64,126]{3,2,1,0:T(8,128)(2,1)} %get-tuple-element.229, bf16[126,256]{1,0:T(8,128)(2,1)S(1)} %get-tuple-element.230), kind=kOutput, calls=%fused_computation.5.clone.1 | convolution fusion | flops 167378944 | bytes 2425344 | tf_op jit(solution)/shard_map/while/body/eval_jaxpr/crw,cwo->ro/dot_general | solution.py:141
  152.8 2.9 %fusion.115 = f32[12,64,512]{2,1,0:T(8,128)} fusion(f32[12,64,512]{2,1,0:T(8,128)} %get-tuple-element.222, s32[]{:T(128)} %get-tuple-element.221, bf16[12,8,256,512]{3,2,1,0:T(8,128)(2,1)} %get-tuple-element.231, bf16[12,8,64,126]{3,2,1,0:T(8,128)(2,1)} %get-tuple-element.229, bf16[126,256]{1,0:T(8,128)(2,1)S(1)} %get-tuple-element.230), kind=kOutput, calls=%fused_computation.5.clone.1 | convolution fusion | flops 167378944 | bytes 2425344 | tf_op jit(solution)/shard_map/while/body/eval_jaxpr/crw,cwo->ro/dot_general | solution.py:141
  155.7 2.9 %fusion.115 = f32[12,64,512]{2,1,0:T(8,128)} fusion(f32[12,64,512]{2,1,0:T(8,128)} %get-tuple-element.222, s32[]{:T(128)} %get-tuple-element.221, bf16[12,8,256,512]{3,2,1,0:T(8,128)(2,1)} %get-tuple-element.231, bf16[12,8,64,126]{3,2,1,0:T(8,128)(2,1)} %get-tuple-element.229, bf16[126,256]{1,0:T(8,128)(2,1)S(1)} %get-tuple-element.230), kind=kOutput, calls=%fused_computation.5.clone.1 | convolution fusion | flops 167378944 | bytes 2425344 | tf_op jit(solution)/shard_map/while/body/eval_jaxpr/crw,cwo->ro/dot_general | solution.py:141
  158.7 2.9 %fusion.115 = f32[12,64,512]{2,1,0:T(8,128)} fusion(f32[12,64,512]{2,1,0:T(8,128)} %get-tuple-element.222, s32[]{:T(128)} %get-tuple-element.221, bf16[12,8,256,512]{3,2,1,0:T(8,128)(2,1)} %get-tuple-element.231, bf16[12,8,64,126]{3,2,1,0:T(8,128)(2,1)} %get-tuple-element.229, bf16[126,256]{1,0:T(8,128)(2,1)S(1)} %get-tuple-element.230), kind=kOutput, calls=%fused_computation.5.clone.1 | convolution fusion | flops 167378944 | bytes 2425344 | tf_op jit(solution)/shard_map/while/body/eval_jaxpr/crw,cwo->ro/dot_general | solution.py:141
  164.5 2.9 %fusion.115 = f32[12,64,512]{2,1,0:T(8,128)} fusion(f32[12,64,512]{2,1,0:T(8,128)} %get-tuple-element.222, s32[]{:T(128)} %get-tuple-element.221, bf16[12,8,256,512]{3,2,1,0:T(8,128)(2,1)} %get-tuple-element.231, bf16[12,8,64,126]{3,2,1,0:T(8,128)(2,1)} %get-tuple-element.229, bf16[126,256]{1,0:T(8,128)(2,1)S(1)} %get-tuple-element.230), kind=kOutput, calls=%fused_computation.5.clone.1 | convolution fusion | flops 167378944 | bytes 2425344 | tf_op jit(solution)/shard_map/while/body/eval_jaxpr/crw,cwo->ro/dot_general | solution.py:141
  167.4 2.9 %fusion.115 = f32[12,64,512]{2,1,0:T(8,128)} fusion(f32[12,64,512]{2,1,0:T(8,128)} %get-tuple-element.222, s32[]{:T(128)} %get-tuple-element.221, bf16[12,8,256,512]{3,2,1,0:T(8,128)(2,1)} %get-tuple-element.231, bf16[12,8,64,126]{3,2,1,0:T(8,128)(2,1)} %get-tuple-element.229, bf16[126,256]{1,0:T(8,128)(2,1)S(1)} %get-tuple-element.230), kind=kOutput, calls=%fused_computation.5.clone.1 | convolution fusion | flops 167378944 | bytes 2425344 | tf_op jit(solution)/shard_map/while/body/eval_jaxpr/crw,cwo->ro/dot_general | solution.py:141
  174.2 31.6 %while.22 = (s32[]{:T(128)}, f32[126,256]{1,0:T(8,128)S(1)}, bf16[12,8,64,126]{3,2,1,0:T(8,128)(2,1)}, bf16[12,8,256,512]{3,2,1,0:T(8,128)(2,1)}, bf16[12,64,512]{2,1,0:T(8,128)(2,1)S(1)}, /*index=5*/s32[]{:T(128)}, s32[]{:T(128)}) while((s32[]{:T(128)}, f32[126,256]{1,0:T(8,128)S(1)}, bf16[12,8,64,126]{3,2,1,0:T(8,128)(2,1)}, ...), condition=%wide.region_6.7_spmd.clone, body=%wide.region_5.6_spmd.clone.sunk | while | flops 167443456 | bytes 2555479 | solution.py:169
  205.8 4.2 %collective-permute-start.2 = (f32[31,256]{1,0:T(8,128)S(1)}, f32[31,256]{1,0:T(8,128)S(1)}, u32[]{:S(2)}, u32[]{:S(2)}) collective-permute-start(f32[31,256]{1,0:T(8,128)S(1)} %get-tuple-element.143), channel_id=1, source_target_pairs={{0,1},{1,2},{2,3},{3,4},{4,5},{5,6},{6,7},{7,8},{8,9},{9,10},{10,1... | collective-permute-start | bytes 95240 | tf_op jit(solution)/shard_map/ppermute | solution.py:36
  211.3 3.0 %collective-permute-done.3 = f32[31,256]{1,0:T(8,128)S(1)} collective-permute-done((f32[31,256]{1,0:T(8,128)S(1)}, f32[31,256]{1,0:T(8,128)S(1)}, u32[]{:S(2)}, u32[]{:S(2)}) %collective-permute-start.3) | collective-permute-done | bytes 31776 | tf_op jit(solution)/shard_map/ppermute | solution.py:36
  216.3 3.1 %fusion.49 = f32[128,32,32]{2,1,0:T(8,128)S(1)} fusion(f32[128,32,256]{2,1,0:T(8,128)S(1)} %fusion.56, s32[128,32]{1,0:T(8,128)S(1)} %get-tuple-element.151), kind=kOutput, calls=%fused_computation.34 | convolution fusion | flops 403701760 | bytes 4734976 | tf_op jit(solution)/shard_map/paj,pcj->pac/dot_general | solution.py:184
  222.3 8.7 %all-to-all-start.2 = ((f32[16,16,1024]{2,1,0:T(8,128)}), f32[16,16,1024]{2,1,0:T(8,128)S(1)}, u32[]{:S(2)}, u32[]{:S(2)}) async-start(f32[16,16,1024]{2,1,0:T(8,128)} %fusion.73), calls=%async_computation.2 | async-start | bytes 2097152 | tf_op jit(solution)/shard_map/all_to_all | solution.py:190
  231.1 22.8 %all-to-all-done.2 = f32[16,16,1024]{2,1,0:T(8,128)S(1)} async-done(((f32[16,16,1024]{2,1,0:T(8,128)}), f32[16,16,1024]{2,1,0:T(8,128)S(1)}, u32[]{:S(2)}, u32[]{:S(2)}) %all-to-all-start.2) | async-done | bytes 1048608 | tf_op jit(solution)/shard_map/all_to_all | solution.py:190
  (75 shorter events, 68.2 us)
Async XLA Ops:
  2.2 0.7 copy-start.5
  3.7 61.6 %all-to-all-start = ((s32[16,1,16]{2,1,0:T(1,128)}), s32[16,1,16]{2,1,0:T(1,128)S(1)}, u32[]{:S(2)}, u32[]{:S(2)}) async-start(s32[16,1,16]{2,1,0:T(1,128)} %all_to_all.12), calls=%async_computation | async-start | bytes 16384 | tf_op jit(solution)/shard_map/all_to_all | solution.py:108
  32.0 7.2 %copy-start.1 = (bf16[12,4,2,63]{3,2,1,0:T(2,128)(2,1)S(1)}, bf16[12,4,2,63]{3,2,1,0:T(2,128)(2,1)}, u32[]{:S(2)}) copy-start(bf16[12,4,2,63]{3,2,1,0:T(2,128)(2,1)} %param.20) | copy-start | bytes 36292
  40.0 25.2 %copy-start.7 = (s32[128]{0:T(128)S(1)}, s32[128]{0:T(128)}, u32[]{:S(2)}) copy-start(s32[128]{0:T(128)} %param.19) | copy-start | bytes 1540
  40.0 25.2 %copy-start.8 = (s32[128]{0:T(128)S(1)}, s32[128]{0:T(128)}, u32[]{:S(2)}) copy-start(s32[128]{0:T(128)} %param.18) | copy-start | bytes 1540
  40.0 25.9 %copy-start = (f32[4,1024]{1,0:T(4,128)S(1)}, f32[4,1024]{1,0:T(4,128)}, u32[]{:S(2)}) copy-start(f32[4,1024]{1,0:T(4,128)} %param.14) | copy-start | bytes 49156
  67.1 28.5 %all-to-all-start.1 = ((bf16[16,16,1024]{2,1,0:T(8,128)(2,1)}), bf16[16,16,1024]{2,1,0:T(8,128)(2,1)S(1)}, u32[]{:S(2)}, u32[]{:S(2)}) async-start(bf16[16,16,1024]{2,1,0:T(8,128)(2,1)} %convolution_convert_fusion.1), calls=%async_computation.1 | async-start | bytes 1048576 | tf_op jit(solution)/shard_map/all_to_all | solution.py:116
  100.2 35.1 %collective-permute-start = (bf16[31,256]{1,0:T(8,128)(2,1)S(1)}, bf16[31,256]{1,0:T(8,128)(2,1)S(1)}, u32[]{:S(2)}, u32[]{:S(2)}) collective-permute-start(bf16[31,256]{1,0:T(8,128)(2,1)S(1)} %get-tuple-element.145), channel_id=1, source_target_pairs={{0,1},{1,2},{2,3},{3,4},{4,5},{5,6},{6,7},{7,8},{8,9},{9,10},{10,1... | collective-permute-start | bytes 47624 | tf_op jit(solution)/shard_map/ppermute | solution.py:25
  102.6 32.7 %collective-permute-start.1 = (bf16[31,256]{1,0:T(8,128)(2,1)S(1)}, bf16[31,256]{1,0:T(8,128)(2,1)S(1)}, u32[]{:S(2)}, u32[]{:S(2)}) collective-permute-start(bf16[31,256]{1,0:T(8,128)(2,1)S(1)} %get-tuple-element.146), channel_id=1, source_target_pairs={{1,0},{2,1},{3,2},{4,3},{5,4},{6,5},{7,6},{8,7},{9,8},{10,9},{11,1... | collective-permute-start | bytes 47624 | tf_op jit(solution)/shard_map/ppermute | solution.py:28
  135.3 35.0 %copy-start.9 = (f32[12]{0:T(128)S(1)}, f32[12]{0:T(128)}, u32[]{:S(2)}) copy-start(f32[12]{0:T(128)} %param.22) | copy-start | bytes 148
  135.3 36.5 %copy-start.2 = (bf16[64,256]{1,0:T(8,128)(2,1)S(1)}, bf16[64,256]{1,0:T(8,128)(2,1)}, u32[]{:S(2)}) copy-start(bf16[64,256]{1,0:T(8,128)(2,1)} %param.23) | copy-start | bytes 98308
  205.8 5.5 %collective-permute-start.2 = (f32[31,256]{1,0:T(8,128)S(1)}, f32[31,256]{1,0:T(8,128)S(1)}, u32[]{:S(2)}, u32[]{:S(2)}) collective-permute-start(f32[31,256]{1,0:T(8,128)S(1)} %get-tuple-element.143), channel_id=1, source_target_pairs={{0,1},{1,2},{2,3},{3,4},{4,5},{5,6},{6,7},{7,8},{8,9},{9,10},{10,1... | collective-permute-start | bytes 95240 | tf_op jit(solution)/shard_map/ppermute | solution.py:36
  210.0 4.3 %collective-permute-start.3 = (f32[31,256]{1,0:T(8,128)S(1)}, f32[31,256]{1,0:T(8,128)S(1)}, u32[]{:S(2)}, u32[]{:S(2)}) collective-permute-start(f32[31,256]{1,0:T(8,128)S(1)} %get-tuple-element.144), channel_id=1, source_target_pairs={{1,0},{2,1},{3,2},{4,3},{5,4},{6,5},{7,6},{8,7},{9,8},{10,9},{11,1... | collective-permute-start | bytes 95240 | tf_op jit(solution)/shard_map/ppermute | solution.py:36
  216.2 4.4 %copy-start.6 = (s32[128]{0:T(128)S(1)}, s32[128]{0:T(128)}, u32[]{:S(2)}) copy-start(s32[128]{0:T(128)} %copy-done.5) | copy-start | bytes 1540
  219.4 11.6 %copy-start.3 = (s32[16,16]{1,0:T(8,128)S(1)}, s32[16,16]{1,0:T(8,128)}, u32[]{:S(2)}) copy-start(s32[16,16]{1,0:T(8,128)} %get-tuple-element.147) | copy-start | bytes 3076
  219.4 34.5 %copy-start.4 = (f32[4,1024]{1,0:T(4,128)S(1)}, f32[4,1024]{1,0:T(4,128)}, u32[]{:S(2)}) copy-start(f32[4,1024]{1,0:T(4,128)} %param.15) | copy-start | bytes 49156
  222.3 31.6 %all-to-all-start.2 = ((f32[16,16,1024]{2,1,0:T(8,128)}), f32[16,16,1024]{2,1,0:T(8,128)S(1)}, u32[]{:S(2)}, u32[]{:S(2)}) async-start(f32[16,16,1024]{2,1,0:T(8,128)} %fusion.73), calls=%async_computation.2 | async-start | bytes 2097152 | tf_op jit(solution)/shard_map/all_to_all | solution.py:190
where the time goes:
time: 258 us; the launch traced here: 255 us
  matrix products  87.7 us (34%)
  other arithmetic  62.5 us (24%)
  local copies, waits for them, and re-layouts  46.4 us (18%)
  starting transfers between devices  31.3 us (12%)
  waiting for transfers between devices  25.8 us (10%)
    another operation x2, other arithmetic, all_column_bands(): jnp.stack([from_real, from_imag], axis=2)  47.6 us
    dot_general x12, matrix products, forward_mode(): jnp.einsum('crw,cwo->ro', field_y, column_band, preferred_element_type=jn...  34.9 us
    dot_general x12, matrix products, adjoint_mode(): jnp.einsum('crs,crw->sw', row_band, grad_y, preferred_element_type=jnp.fl...  31.3 us
    another operation x1, local copies, waits for them, and re-layouts, all_column_bands(): jnp.stack([from_real, from_imag], axis=2)  28.4 us
    all_to_all x1, waiting for transfers between devices, on_device(): lax.all_to_all(slot_grads, 'tx', split_axis=0, concat_axis=0, tiled=True)  22.8 us
    squeeze x1, local copies, waits for them, and re-layouts, all_column_bands(): imag_band = bands[:, :, 1]  12 us
    dot_general x1, matrix products, all_column_bands(): jnp.einsum('kxpt,wot->kxpwo', col_taps, picker, preferred_element_type=jn...  8.91 us
    all_to_all x1, starting transfers between devices, on_device(): lax.all_to_all(slot_grads, 'tx', split_axis=0, concat_axis=0, tiled=True)  8.69 us
  transfers between devices with their start and end apart: 7, of which 2 were waited for; matrix products, arithmetic and copies ran while one was open for 42% of the time, Pallas kernels for 0%

commit v1 on v0

v1 whole, which is shorter than its diff:
```python
import jax
import jax.numpy as jnp
from jax import lax
from jax.experimental import pallas as pl
from jax.experimental.pallas import tpu as pltpu
from jax.sharding import PartitionSpec as P

W = 256
MS = 32
TAPS = 63
HALF = 31
TERMS = 4
MODES = 12
CH = 2 * TERMS
LANES = 128
BLK = 64
NBLK = W // BLK
EXT = 128
PAD = 40
CROWS = 72

steepness = 0.5
threshold = 8.0
momentum = 0.9
step_size = 0.05


def lane_iota(shape):
    return lax.broadcasted_iota(jnp.int32, shape, len(shape) - 1)


def skew(row, shift, rows):
    return pltpu.roll(
        jnp.broadcast_to(row, (rows, LANES)), shift, 1, stride=1, stride_axis=0
    )


def bands_kernel(taps_ref, r_ref, rt_ref, cf_ref, ca_ref):
    low = lane_iota((EXT, LANES)) < BLK

    def step(n, carry):
        k = n // 2
        half = n % 2
        first = k * CH + half * 4
        for f in range(4):
            r_ref[pl.ds((first + f) * BLK, BLK), :] = skew(
                taps_ref[0, pl.ds(first + f, 1), :], 0, BLK
            ).astype(jnp.bfloat16)
        for par in range(2):
            lo = skew(taps_ref[1, pl.ds(first + par, 1), :], 0, EXT)
            hi = skew(taps_ref[1, pl.ds(first + 2 + par, 1), :], BLK, EXT)
            rt_ref[n, par * EXT : (par + 1) * EXT, :] = jnp.where(low, lo, hi).astype(
                jnp.bfloat16
            )
        for t in range(2):
            c0 = taps_ref[2, pl.ds(first + 2 * t, 1), :]
            c1 = taps_ref[2, pl.ds(first + 2 * t + 1, 1), :]
            a0, a1 = skew(c0, 0, EXT), skew(c1, 0, EXT)
            b0, b1 = skew(c0, BLK, EXT), skew(c1, BLK, EXT)
            at = (half * 2 + t) * 2 * EXT
            cf_ref[k, pl.ds(at, EXT), :] = jnp.where(low, a0, b1).astype(jnp.bfloat16)
            cf_ref[k, pl.ds(at + EXT, EXT), :] = jnp.where(low, -a1, b0).astype(jnp.bfloat16)
            c0 = taps_ref[3, pl.ds(first + 2 * t, 1), :]
            c1 = taps_ref[3, pl.ds(first + 2 * t + 1, 1), :]
            a0, a1 = skew(c0, 0, EXT), skew(c1, 0, EXT)
            b0, b1 = skew(c0, BLK, EXT), skew(c1, BLK, EXT)
            ca_ref[n * 2 + t, :EXT, :] = jnp.where(low, a0, -b1).astype(jnp.bfloat16)
            ca_ref[n * 2 + t, EXT:, :] = jnp.where(low, a1, b0).astype(jnp.bfloat16)
        return carry

    lax.fori_loop(0, 2 * MODES, step, 0)


def build_bands(row_taps, col_taps):
    row = row_taps.reshape(MODES * CH, TAPS).astype(jnp.float32)
    col = col_taps.reshape(MODES * CH, TAPS).astype(jnp.float32)
    gap = LANES - TAPS

    def reversed_taps(v):
        return jnp.concatenate(
            [v[:, :1], jnp.zeros((v.shape[0], gap), jnp.float32), v[:, :0:-1]], axis=1
        )

    from_last = jnp.concatenate(
        [col[:, TAPS - 1 :], jnp.zeros((col.shape[0], gap), jnp.float32), col[:, : TAPS - 1]],
        axis=1,
    )
    taps = jnp.stack(
        [jnp.pad(row, ((0, 0), (0, gap))), reversed_taps(row), reversed_taps(col), from_last]
    )
    return pl.pallas_call(
        bands_kernel,
        out_shape=(
            jax.ShapeDtypeStruct((MODES * CH * BLK, LANES), jnp.bfloat16),
            jax.ShapeDtypeStruct((2 * MODES, 2 * EXT, LANES), jnp.bfloat16),
            jax.ShapeDtypeStruct((MODES, CH * EXT, LANES), jnp.bfloat16),
            jax.ShapeDtypeStruct((4 * MODES, 2 * EXT, LANES), jnp.bfloat16),
        ),
        in_specs=[pl.BlockSpec(memory_space=pltpu.VMEM)],
        out_specs=[pl.BlockSpec(memory_space=pltpu.VMEM)] * 4,
        name="bands",
    )(taps)


def main_kernel(
    own_ref,
    above_ref,
    below_ref,
    weight_ref,
    masters_ref,
    target_ref,
    r_ref,
    rt_ref,
    cf_ref,
    ca_ref,
    resid_ref,
    grads_ref,
    canvas_own,
    canvas_above,
    canvas_below,
    window,
    fields,
    gys,
    grad,
    acc_above,
    acc_below,
):
    places = own_ref.shape[1]
    rows = BLK
    canvases = ((own_ref, canvas_own), (above_ref, canvas_above), (below_ref, canvas_below))
    for _, canvas in canvases:
        canvas[...] = jnp.zeros_like(canvas)
    lanes8 = lane_iota((8, LANES))

    def place(q, carry):
        for ids, canvas in canvases:
            master = masters_ref[ids[0, q]].astype(jnp.float32)
            top = ids[1, q] + 7
            col = ids[2, q] + HALF
            side = col // LANES
            shift = col % LANES
            for k in range(4):
                moved = pltpu.roll(master, (shift + LANES - 32 * k) % LANES, 1)
                here = (lanes8 >= shift) & (lanes8 < shift + MS)
                after = lanes8 < shift + MS - LANES
                at = pl.ds(top + k, 8, stride=4)
                canvas[side, at, :] += jnp.where(here, moved, 0.0)
                canvas[side + 1, at, :] += jnp.where(after, moved, 0.0)
        return carry

    lax.fori_loop(0, places, place, 0)

    sides = []
    for h in range(3):
        a, o, b = canvas_above[h], canvas_own[h], canvas_below[h]
        sides.append(
            jnp.concatenate(
                [a[40:64], a[64:72] + o[0:8], o[8:64], o[64:72] + b[0:8], b[8:40]], axis=0
            )
        )
    low = lane_iota((EXT, LANES)) < BLK
    turned = [pltpu.roll(s, BLK, 1) for s in sides]
    window[:, 0:128] = sides[0].astype(jnp.bfloat16)
    window[:, 128:256] = jnp.where(low, turned[0], turned[1]).astype(jnp.bfloat16)
    window[:, 256:384] = sides[1].astype(jnp.bfloat16)
    window[:, 384:512] = jnp.where(low, turned[1], turned[2]).astype(jnp.bfloat16)

    intensity = jnp.zeros((NBLK * rows, LANES), jnp.float32)
    for k in range(MODES):
        field_y = jnp.dot(
            r_ref[k * CH * rows : (k + 1) * CH * rows, :],
            window[...],
            preferred_element_type=jnp.float32,
        ).astype(jnp.bfloat16)
        lhs = jnp.concatenate(
            [
                jnp.concatenate(
                    [
                        field_y[c * rows : (c + 1) * rows, b * LANES : (b + 1) * LANES]
                        for c in range(CH)
                    ],
                    axis=1,
                )
                for b in range(NBLK)
            ],
            axis=0,
        )
        e = jnp.dot(lhs, cf_ref[k], preferred_element_type=jnp.float32)
        fields[k] = e
        intensity = intensity + weight_ref[k] * (e * e)
    intensity = intensity + pltpu.roll(intensity, BLK, 1)
    low_rows = lane_iota((rows, LANES)) < BLK
    goal = []
    for h in range(2):
        t = target_ref[:, h * LANES : (h + 1) * LANES].astype(jnp.float32)
        other = pltpu.roll(t, BLK, 1)
        goal += [jnp.where(low_rows, t, other), jnp.where(low_rows, other, t)]
    resist = jax.nn.sigmoid(steepness * (intensity - threshold))
    resid = resist - jnp.concatenate(goal, axis=0)
    for h in range(2):
        first = resid[2 * h * rows : (2 * h + 1) * rows]
        second = resid[(2 * h + 1) * rows : (2 * h + 2) * rows]
        resid_ref[:, h * LANES : (h + 1) * LANES] = jnp.where(low_rows, first, second)
    grad_intensity = resid * steepness * resist * (1.0 - resist)

    lanes = lane_iota((rows, LANES))
    middle = (lanes >= HALF) & (lanes < HALF + BLK)
    left = lanes < HALF
    nothing = jnp.zeros((rows, LANES), jnp.float32)
    for k in range(MODES):
        g = 2.0 * weight_ref[k] * grad_intensity * fields[k]
        r31 = pltpu.roll(g, HALF, 1)
        r95 = pltpu.roll(g, HALF + BLK, 1)

        def part(v, b):
            return v[b * rows : (b + 1) * rows] if 0 <= b < NBLK else nothing

        parts = []
        for b in range(NBLK):
            re = jnp.where(
                middle, part(r31, b), jnp.where(left, part(r95, b - 1), part(r95, b + 1))
            )
            im = jnp.where(
                middle, part(r95, b), jnp.where(left, part(r31, b - 1), part(r31, b + 1))
            )
            parts.append(jnp.concatenate([re, im], axis=1))
        gw = jnp.concatenate(parts, axis=0).astype(jnp.bfloat16)
        for t in range(TERMS):
            gy = jnp.dot(
                gw, ca_ref[k * TERMS + t], preferred_element_type=jnp.float32
            ).astype(jnp.bfloat16)
            at = (k * TERMS + t) * rows
            for b in range(NBLK):
                gys[at : at + rows, b * LANES : (b + 1) * LANES] = gy[b * rows : (b + 1) * rows]

    total = jnp.zeros((2 * EXT, NBLK * LANES), jnp.float32)
    for n in range(2 * MODES):
        total = total + jnp.dot(
            rt_ref[n], gys[n * LANES : (n + 1) * LANES, :], preferred_element_type=jnp.float32
        )
    zeros = jnp.zeros((PAD, LANES), jnp.float32)
    for h in range(2):
        v0 = total[:EXT, 2 * h * LANES : (2 * h + 1) * LANES]
        v1 = total[:EXT, (2 * h + 1) * LANES : (2 * h + 2) * LANES]
        u0 = total[EXT:, 2 * h * LANES : (2 * h + 1) * LANES]
        u1 = total[EXT:, (2 * h + 1) * LANES : (2 * h + 2) * LANES]
        grad[h, PAD : PAD + EXT, :] = jnp.where(
            low, v0 + pltpu.roll(u0, BLK, 1), pltpu.roll(v1, BLK, 1) + u1
        )
        grad[h, :PAD, :] = zeros
        grad[h, PAD + EXT :, :] = zeros

    sums = (
        (own_ref, grads_ref, PAD + HALF),
        (above_ref, acc_above, PAD + HALF - rows),
        (below_ref, acc_below, PAD + HALF + rows),
    )
    for _, acc, _ in sums:
        acc[...] = jnp.zeros_like(acc)

    def gather(q, carry):
        for ids, acc, base in sums:
            m = ids[0, q]
            top = ids[1, q] + base
            col = ids[2, q]
            side = col // LANES
            after = jnp.minimum(side + 1, 1)
            shift = col % LANES
            patch = jnp.zeros((8, LANES), jnp.float32)
            for k in range(4):
                at = pl.ds(top + k, 8, stride=4)
                both = jnp.where(lanes8 >= shift, grad[side, at, :], grad[after, at, :])
                moved = pltpu.roll(both, (LANES + 32 * k - shift) % LANES, 1)
                patch = jnp.where((lanes8 >= 32 * k) & (lanes8 < 32 * k + MS), moved, patch)
            acc[m] += patch
        return carry

    lax.fori_loop(0, places, gather, 0)
    grads_ref[...] += acc_above[...] + acc_below[...]


def main_step(own, above, below, weights, masters, target, bands):
    count = masters.shape[0]
    smem = pl.BlockSpec(memory_space=pltpu.SMEM)
    vmem = pl.BlockSpec(memory_space=pltpu.VMEM)
    return pl.pallas_call(
        main_kernel,
        out_shape=(
            jax.ShapeDtypeStruct(target.shape, jnp.float32),
            jax.ShapeDtypeStruct((count, 8, LANES), jnp.float32),
        ),
        in_specs=[smem] * 4 + [vmem] * 6,
        out_specs=[vmem] * 2,
        scratch_shapes=[
            pltpu.VMEM((3, CROWS, LANES), jnp.float32),
            pltpu.VMEM((3, CROWS, LANES), jnp.float32),
            pltpu.VMEM((3, CROWS, LANES), jnp.float32),
            pltpu.VMEM((EXT, NBLK * LANES), jnp.bfloat16),
            pltpu.VMEM((MODES, NBLK * BLK, LANES), jnp.float32),
            pltpu.VMEM((MODES * TERMS * BLK, NBLK * LANES), jnp.bfloat16),
            pltpu.VMEM((2, 2 * PAD + EXT, LANES), jnp.float32),
            pltpu.VMEM((count, 8, LANES), jnp.float32),
            pltpu.VMEM((count, 8, LANES), jnp.float32),
        ],
        name="imaging",
    )(own, above, below, weights, masters, target, *bands)


def update_kernel(sent_ref, velocity_ref, masters_ref, velocity_out, masters_out, sums):
    count = velocity_ref.shape[0]
    total = sent_ref[0]
    for d in range(1, sent_ref.shape[0]):
        total = total + sent_ref[d]
    sums[...] = total.reshape(count * 8, LANES)
    for s in range(8):
        at = slice(s * LANES, (s + 1) * LANES)
        gradient = sums[pl.ds(s, count, stride=8), :]
        velocity = momentum * velocity_ref[:, at] + gradient
        velocity_out[:, at] = velocity
        masters_out[:, at] = masters_ref[:, at] - step_size * velocity


def update(sent, velocity, masters):
    vmem = pl.BlockSpec(memory_space=pltpu.VMEM)
    return pl.pallas_call(
        update_kernel,
        out_shape=(jax.ShapeDtypeStruct(velocity.shape, jnp.float32),) * 2,
        in_specs=[vmem] * 3,
        out_specs=[vmem] * 2,
        scratch_shapes=[pltpu.VMEM((8 * velocity.shape[0], LANES), jnp.float32)],
        name="update",
    )(sent, velocity, masters)


def on_device(
    masters,
    velocity,
    place_owner,
    place_local,
    place_row,
    place_col,
    row_taps,
    col_taps,
    mode_weights,
    target,
):
    devices = lax.axis_size("tx")
    count = masters.shape[0]
    master_id = place_owner[:, 0] * count + place_local
    own = jnp.stack([master_id, place_row, place_col])
    flipped = jnp.stack([master_id, (BLK - MS) - place_row, place_col])
    forward = [(i, i + 1) for i in range(devices - 1)]
    backward = [(i + 1, i) for i in range(devices - 1)]
    above = lax.ppermute(own, "tx", forward)
    below = lax.ppermute(flipped, "tx", backward)
    below = below * jnp.array([1, -1, 1], jnp.int32)[:, None] + jnp.array(
        [0, BLK - MS, 0], jnp.int32
    )[:, None]
    half = masters.astype(jnp.bfloat16).reshape(count, 8, LANES)
    everywhere = jnp.broadcast_to(half[None], (devices, count, 8, LANES))
    gathered = lax.all_to_all(everywhere, "tx", split_axis=0, concat_axis=0, tiled=True)
    gathered = gathered.reshape(devices * count, 8, LANES)
    bands = build_bands(row_taps, col_taps)
    resid, grads = main_step(own, above, below, mode_weights, gathered, target, bands)
    sent = lax.all_to_all(
        grads.reshape(devices, count, 8, LANES), "tx", split_axis=0, concat_axis=0, tiled=True
    )
    velocity_new, masters_new = update(sent, velocity, masters)
    return resid, velocity_new, masters_new


def solution(mesh):
    return jax.shard_map(
        on_device,
        mesh=mesh,
        in_specs=(
            P(("groups", "tx"), None),
            P(("groups", "tx"), None),
            P(("groups", "tx"), None),
            P(("groups", "tx")),
            P(("groups", "tx")),
            P(("groups", "tx")),
            P(),
            P(),
            P(),
            P(("groups", "tx"), None),
        ),
        out_specs=(P(("groups", "tx"), None), P(("groups", "tx"), None), P(("groups", "tx"), None)),
        check_vma=False,
    )
```

time: 258 us -> 95.5 us (0.37)
  matrix products: 87.7 us -> 0 us
  other arithmetic: 62.5 us -> 4.93 us
  Pallas kernels: 0 us -> 55.8 us
  local copies, waits for them, and re-layouts: 46.4 us -> 4.87 us
  waiting for transfers between devices: 25.8 us -> 0.01 us
  starting transfers between devices: 31.3 us -> 12.3 us
  blocking collectives: 0 us -> 16.1 us
    dot_general x33 -> x0, matrix products: 87.7 us -> none  [the longest x12 34.9 us: forward_mode(): jnp.einsum('crw,cwo->ro', field_y, column_band, preferred_element_type=jn...]
    pallas_call x0 -> x3, Pallas kernels: none -> 55.8 us  [the longest x1 44.3 us: main_step(): pl.pallas_call(main_kernel, out_shape=(jax.ShapeDtypeStruct(target.shape,...]
    another operation x2 -> x4, other arithmetic: 47.6 us -> 2.19 us  [the longest x2 0.81 us: build_bands(): jnp.stack([jnp.pad(row, ((0, 0), (0, gap))), reversed_taps(row), reversed...]
    another operation x1, local copies, waits for them, and re-layouts: 28.4 us -> 0.01 us  [all_column_bands(): jnp.stack([from_real, from_imag], axis=2)]
    all_to_all x3 -> x1, waiting for transfers between devices: 22.8 us -> 0.01 us  [on_device(): lax.all_to_all(everywhere, 'tx', split_axis=0, concat_axis=0, tiled=True)]
    all_to_all x0 -> x1, blocking collectives: none -> 16.1 us  [on_device(): lax.all_to_all(grads.reshape(devices, count, 8, LANES), 'tx', split_axis=...]
    all_to_all x3 -> x1, starting transfers between devices: 22.1 us -> 7.98 us  [on_device(): lax.all_to_all(everywhere, 'tx', split_axis=0, concat_axis=0, tiled=True)]
    squeeze x1 -> x0, local copies, waits for them, and re-layouts: 12 us -> none  [all_column_bands(): imag_band = bands[:, :, 1]]
  transfers between devices with their start and end apart: 7 -> 3, of which waited for: 2 -> 0; matrix products, arithmetic and copies ran while one was open for 42% -> 8% of each run, Pallas kernels for 0% -> 10%
where the time goes in v1:
time: 95.5 us; the launch traced here: 94.7 us
  Pallas kernels  55.8 us (58%)
  blocking collectives  16.1 us (17%)
  starting transfers between devices  12.3 us (13%)
  other arithmetic  4.93 us (5%)
  local copies, waits for them, and re-layouts  4.87 us (5%)
    pallas_call x1, Pallas kernels, main_step(): pl.pallas_call(main_kernel, out_shape=(jax.ShapeDtypeStruct(target.shape,...  44.3 us
    all_to_all x1, blocking collectives, on_device(): lax.all_to_all(grads.reshape(devices, count, 8, LANES), 'tx', split_axis=...  16.1 us
    pallas_call x1, Pallas kernels, build_bands(): pl.pallas_call(bands_kernel, out_shape=(jax.ShapeDtypeStruct((MODES * CH...  9.89 us
    all_to_all x1, starting transfers between devices, on_device(): lax.all_to_all(everywhere, 'tx', split_axis=0, concat_axis=0, tiled=True)  7.98 us
    ppermute x1, starting transfers between devices, on_device(): above = lax.ppermute(own, 'tx', forward)  3.03 us
  transfers between devices with their start and end apart: 3, of which 0 were waited for; matrix products, arithmetic and copies ran while one was open for 8% of the time, Pallas kernels for 10%

profile of v1, /device:TPU:0, one launch (start us, length us, event | category | flops | bytes accessed | tf_op | source)
XLA Modules:
  0.0 94.7 jit_solution(11560691518825816269)
XLA Ops:
  0.6 0.7 fusion
  1.3 0.7 pad_add_fusion
  2.0 1.3 %collective-permute-start.1 = (s32[3,128]{1,0:T(4,128)S(1)}, s32[3,128]{1,0:T(4,128)S(1)}, u32[]{:S(2)}, u32[]{:S(2)}) collective-permute-start(s32[3,128]{1,0:T(4,128)S(1)} %get-tuple-element.23), channel_id=1, source_target_pairs={{1,0},{2,1},{3,2},{4,3},{5,4},{6,5},{7,6},{8,7},{9,8},{10,9},{11,1... | collective-permute-start | bytes 4616 | tf_op jit(solution)/shard_map/ppermute | solution.py:355
  3.3 3.0 %collective-permute-start = (s32[3,128]{1,0:T(4,128)S(1)}, s32[3,128]{1,0:T(4,128)S(1)}, u32[]{:S(2)}, u32[]{:S(2)}) collective-permute-start(s32[3,128]{1,0:T(4,128)S(1)} %get-tuple-element.24.own_ref), channel_id=1, source_target_pairs={{0,1},{1,2},{2,3},{3,4},{4,5},{5,6},{6,7},{7,8},{8,9},{9,10},{10,1... | collective-permute-start | bytes 4616 | tf_op jit(solution)/shard_map/ppermute | solution.py:354
  6.3 0.7 convert_bitcast_fusion
  7.1 0.7 broadcast_in_dim.10
  7.7 8.0 %all-to-all-start = ((bf16[16,4,8,128]{3,2,1,0:T(8,128)(2,1)}), bf16[16,4,8,128]{3,2,1,0:T(8,128)(2,1)S(1)}, u32[]{:S(2)}, u32[]{:S(2)}) async-start(bf16[16,4,8,128]{3,2,1,0:T(8,128)(2,1)} %broadcast_in_dim.10), calls=%async_computation | async-start | bytes 262144 | tf_op jit(solution)/shard_map/all_to_all | solution.py:361
  15.7 0.7 slice.24
  16.5 0.8 slice.25
  17.3 0.7 convert.2
  18.0 0.9 fusion.2
  18.9 0.9 fusion.1
  19.8 0.1 rev.6
  19.9 0.1 rev.7
  20.0 0.1 pad.16.clone
  20.0 0.1 maximum_bitcast_fusion
  20.2 0.7 pad_maximum_fusion.taps_ref
  20.9 9.9 %bands.1 = (bf16[6144,128]{1,0:T(8,128)(2,1)}, bf16[24,256,128]{2,1,0:T(8,128)(2,1)}, bf16[12,1024,128]{2,1,0:T(8,128)(2,1)}, bf16[48,256,128]{2,1,0:T(8,128)(2,1)}) custom-call(f32[4,96,128]{2,1,0:T(8,128)} %pad_maximum_fusion.taps_ref), custom_call_target="tpu_custom_call" | custom-call | tf_op jit(solution)/shard_map/bands/pallas_call | solution.py:91
  30.7 1.3 %multiply_add_fusion.below_ref = s32[3,128]{1,0:T(4,128)} fusion(s32[3,128]{1,0:T(4,128)S(1)} %collective-permute-done.1, s32[3]{0:T(128)} %constant.13.clone, s32[3]{0:T(128)} %constant.12.clone), kind=kLoop, calls=%fused_computation.11 | loop fusion | flops 768 | bytes 3096 | tf_op jit(solution)/shard_map/add | solution.py:356
  32.1 0.6 copy-done.2
  32.6 0.1 copy-done
  32.7 44.3 %imaging.1 = (f32[64,256]{1,0:T(8,128)}, f32[64,8,128]{2,1,0:T(8,128)}) custom-call(s32[3,128]{1,0:T(4,128)} %copy-done.1, s32[3,128]{1,0:T(4,128)} %copy-done.2, s32[3,128]{1,0:T(4,128)} %multiply_add_fusion.below_ref, f32[12]{0:T(128)} %weight_ref.1, bf16[64,8,128]{2,1,0:T(8,128)(2,1)} %bitcast.34, bf16[64,256]{1,0:T(8,128)(2,1)} %target_ref.1, ...), custom_call_target="tpu_custom_call" | custom-call | tf_op jit(solution)/shard_map/imaging/pallas_call | solution.py:286
  77.0 16.1 %all_to_all.10.sent_ref = f32[16,4,8,128]{3,2,1,0:T(8,128)} all-to-all(f32[16,4,8,128]{3,2,1,0:T(8,128)} %bitcast.35), channel_id=1, replica_groups=mesh['groups'=2,'tx'=16] {'tx'}, dimensions={0} | all-to-all | bytes 524288 | tf_op jit(solution)/shard_map/all_to_all | solution.py:365
  93.1 1.6 %update.1 = (f32[4,1024]{1,0:T(4,128)}, f32[4,1024]{1,0:T(4,128)}) custom-call(f32[16,4,8,128]{3,2,1,0:T(8,128)} %all_to_all.10.sent_ref, f32[4,1024]{1,0:T(4,128)} %velocity_ref.1, f32[4,1024]{1,0:T(4,128)} %masters_ref.1), custom_call_target="tpu_custom_call" | custom-call | tf_op jit(solution)/shard_map/update/pallas_call | solution.py:325
  (9 shorter events, 0.0 us)
Async XLA Ops:
  2.0 30.0 %copy-start.1 = (s32[3,128]{1,0:T(4,128)}, s32[3,128]{1,0:T(4,128)S(1)}, u32[]{:S(2)}) copy-start(s32[3,128]{1,0:T(4,128)S(1)} %get-tuple-element.24.own_ref) | copy-start | bytes 4612
  2.0 28.7 %collective-permute-start.1 = (s32[3,128]{1,0:T(4,128)S(1)}, s32[3,128]{1,0:T(4,128)S(1)}, u32[]{:S(2)}, u32[]{:S(2)}) collective-permute-start(s32[3,128]{1,0:T(4,128)S(1)} %get-tuple-element.23), channel_id=1, source_target_pairs={{1,0},{2,1},{3,2},{4,3},{5,4},{6,5},{7,6},{8,7},{9,8},{10,9},{11,1... | collective-permute-start | bytes 4616 | tf_op jit(solution)/shard_map/ppermute | solution.py:355
  3.3 28.7 %collective-permute-start = (s32[3,128]{1,0:T(4,128)S(1)}, s32[3,128]{1,0:T(4,128)S(1)}, u32[]{:S(2)}, u32[]{:S(2)}) collective-permute-start(s32[3,128]{1,0:T(4,128)S(1)} %get-tuple-element.24.own_ref), channel_id=1, source_target_pairs={{0,1},{1,2},{2,3},{3,4},{4,5},{5,6},{6,7},{7,8},{8,9},{9,10},{10,1... | collective-permute-start | bytes 4616 | tf_op jit(solution)/shard_map/ppermute | solution.py:354
  7.7 24.3 %all-to-all-start = ((bf16[16,4,8,128]{3,2,1,0:T(8,128)(2,1)}), bf16[16,4,8,128]{3,2,1,0:T(8,128)(2,1)S(1)}, u32[]{:S(2)}, u32[]{:S(2)}) async-start(bf16[16,4,8,128]{3,2,1,0:T(8,128)(2,1)} %broadcast_in_dim.10), calls=%async_computation | async-start | bytes 262144 | tf_op jit(solution)/shard_map/all_to_all | solution.py:361
  32.0 0.6 copy-start.2
  32.0 0.7 copy-start

commit v2 on v1

v2 whole, which is shorter than its diff:
```python
import jax
import jax.numpy as jnp
from jax import lax
from jax.experimental import pallas as pl
from jax.experimental.pallas import tpu as pltpu
from jax.sharding import PartitionSpec as P

W = 256
MS = 32
TAPS = 63
HALF = 31
TERMS = 4
MODES = 12
CH = 2 * TERMS
LANES = 128
BLK = 64
NBLK = W // BLK
EXT = 128
PAD = 40
CROWS = 72

steepness = 0.5
threshold = 8.0
momentum = 0.9
step_size = 0.05


def in_vmem(x):
    return pltpu.with_memory_space_constraint(x, pltpu.VMEM)


def lane_iota(shape):
    return lax.broadcasted_iota(jnp.int32, shape, len(shape) - 1)


def skew(row, shift):
    return pltpu.roll(
        jnp.broadcast_to(row, (BLK, LANES)), shift, 1, stride=1, stride_axis=0
    )


def pair(first, second):
    return (skew(first, 0), skew(first, BLK), skew(second, 0), skew(second, BLK))


def half_band(x):
    return x.astype(jnp.bfloat16)


def low_lanes():
    return lane_iota((BLK, LANES)) < BLK


def row_bands_kernel(row_ref, col_ref, r_ref, taps):
    count = MODES * CH
    taps[...] = jnp.zeros_like(taps)
    for k in range(MODES):
        for t in range(TERMS):
            at = k * CH + 2 * t
            taps[at : at + 2, :TAPS] = row_ref[k, t].astype(jnp.float32)
            taps[count + at : count + at + 2, :TAPS] = col_ref[k, t].astype(jnp.float32)
    source = lax.broadcasted_iota(jnp.int32, (LANES, LANES), 0)
    mirror = (source + lane_iota((LANES, LANES))) % LANES == 0
    taps[2 * count :, :] = jnp.dot(
        taps[: 2 * count, :].astype(jnp.bfloat16),
        mirror.astype(jnp.bfloat16),
        preferred_element_type=jnp.float32,
    )
    taps[count : 2 * count, :] = pltpu.roll(taps[count : 2 * count, :], LANES - (TAPS - 1), 1)

    def step(n, carry):
        for f in range(4):
            at = n * 4 + f
            r_ref[pl.ds(at * BLK, BLK), :] = half_band(skew(taps[pl.ds(at, 1), :], 0))
        return carry

    lax.fori_loop(0, 2 * MODES, step, 0)


def row_adjoint_kernel(taps, rt_ref):
    count = MODES * CH
    low = low_lanes()

    def step(n, carry):
        first = 2 * count + 4 * n
        for par in range(2):
            a, a_far, b, b_far = pair(
                taps[pl.ds(first + par, 1), :], taps[pl.ds(first + 2 + par, 1), :]
            )
            rt_ref[n, par * EXT : par * EXT + BLK, :] = half_band(jnp.where(low, a, b_far))
            rt_ref[n, par * EXT + BLK : (par + 1) * EXT, :] = half_band(jnp.where(low, a_far, b))
        return carry

    lax.fori_loop(0, 2 * MODES, step, 0)


def column_bands_kernel(taps, cf_ref):
    count = MODES * CH
    low = low_lanes()

    def step(n, carry):
        first = 3 * count + 4 * n
        for t in range(2):
            at = t * 2 * EXT
            a, a_far, b, b_far = pair(
                taps[pl.ds(first + 2 * t, 1), :], taps[pl.ds(first + 2 * t + 1, 1), :]
            )
            cf_ref[n, at : at + BLK, :] = half_band(jnp.where(low, a, b_far))
            cf_ref[n, at + BLK : at + EXT, :] = half_band(jnp.where(low, a_far, b))
            cf_ref[n, at + EXT : at + EXT + BLK, :] = half_band(jnp.where(low, -b, a_far))
            cf_ref[n, at + EXT + BLK : at + 2 * EXT, :] = half_band(jnp.where(low, -b_far, a))
        return carry

    lax.fori_loop(0, 2 * MODES, step, 0)


def column_adjoint_kernel(taps, ca_ref):
    count = MODES * CH
    low = low_lanes()

    def step(n, carry):
        first = count + 4 * n
        for t in range(2):
            a, a_far, b, b_far = pair(
                taps[pl.ds(first + 2 * t, 1), :], taps[pl.ds(first + 2 * t + 1, 1), :]
            )
            ca_ref[n * 2 + t, :BLK, :] = half_band(jnp.where(low, a, -b_far))
            ca_ref[n * 2 + t, BLK:EXT, :] = half_band(jnp.where(low, a_far, -b))
            ca_ref[n * 2 + t, EXT : EXT + BLK, :] = half_band(jnp.where(low, b, a_far))
            ca_ref[n * 2 + t, EXT + BLK :, :] = half_band(jnp.where(low, b_far, a))
        return carry

    lax.fori_loop(0, 2 * MODES, step, 0)


def build_bands(row_taps, col_taps):
    vmem = pl.BlockSpec(memory_space=pltpu.VMEM)
    small = pltpu.CompilerParams(vmem_limit_bytes=4 << 20)
    r, taps = pl.pallas_call(
        row_bands_kernel,
        out_shape=(
            pltpu.VMEM((MODES * CH * BLK, LANES), jnp.bfloat16),
            pltpu.VMEM((4 * MODES * CH, LANES), jnp.float32),
        ),
        in_specs=[vmem] * 2,
        out_specs=[vmem] * 2,
        compiler_params=small,
        name="row_bands",
    )(row_taps, col_taps)
    taps = in_vmem(taps)
    built = [
        pl.pallas_call(
            kernel,
            out_shape=pltpu.VMEM(shape, jnp.bfloat16),
            in_specs=[vmem],
            out_specs=vmem,
            compiler_params=small,
            name=name,
        )(taps)
        for kernel, shape, name in (
            (row_adjoint_kernel, (2 * MODES, 2 * EXT, LANES), "row_adjoint"),
            (column_bands_kernel, (2 * MODES, CH * EXT // 2, LANES), "column_bands"),
            (column_adjoint_kernel, (4 * MODES, 2 * EXT, LANES), "column_adjoint"),
        )
    ]
    return [r, *built]


def main_kernel(
    weight_ref,
    gathered_ref,
    target_ref,
    r_ref,
    rt_ref,
    cf_ref,
    ca_ref,
    resid_ref,
    grads_ref,
    canvas_own,
    canvas_above,
    canvas_below,
    window,
    fields,
    gys,
    grad,
    acc_own,
    acc_above,
    acc_below,
    table,
    ids,
    sem,
):
    devices, slabs = gathered_ref.shape[:2]
    count = slabs - 1
    places = LANES
    rows = BLK
    me = lax.axis_index("tx")
    bits = devices.bit_length() - 1
    for n, (other, missing) in enumerate(
        ((me, 0), (jnp.maximum(me - 1, 0), 0), (jnp.minimum(me + 1, devices - 1), BLK - MS))
    ):
        slab = gathered_ref[other ^ me, count].astype(jnp.float32).astype(jnp.int32)
        owner, local = slab[0:1] ^ me, slab[1:2]
        turned = sum(((owner >> b) & 1) << (bits - 1 - b) for b in range(bits))
        table[n, 0:1, :] = owner * slabs + local
        table[n, 1:2, :] = turned * count + local
        row = slab[2:3]
        table[n, 2:3, :] = row if n == 0 else jnp.where(other == me, missing, row)
        table[n, 3:4, :] = slab[3:4]
    to_scalar = pltpu.make_async_copy(table, ids, sem)
    to_scalar.start()
    canvases = ((0, canvas_own), (1, canvas_above), (2, canvas_below))
    for _, canvas in canvases:
        canvas[...] = jnp.zeros_like(canvas)
    lanes8 = lane_iota((8, LANES))
    to_scalar.wait()

    def place(q, carry):
        for n, canvas in canvases:
            at = ids[n, 0, q]
            master = gathered_ref[at // slabs, at % slabs].astype(jnp.float32)
            top = ids[n, 2, q] + 7
            col = ids[n, 3, q] + HALF
            side = col >> 7
            shift = col & 127
            for k in range(4):
                moved = pltpu.roll(master, (shift + LANES - 32 * k) & 127, 1)
                here = (lanes8 >= shift) & (lanes8 < shift + MS)
                after = lanes8 < shift + MS - LANES
                at = pl.ds(top + k, 8, stride=4)
                canvas[side, at, :] += jnp.where(here, moved, 0.0)
                canvas[side + 1, at, :] += jnp.where(after, moved, 0.0)
        return carry

    lax.fori_loop(0, places, place, 0, unroll=8)

    sides = []
    for h in range(3):
        a, o, b = canvas_above[h], canvas_own[h], canvas_below[h]
        sides.append(
            jnp.concatenate(
                [a[40:64], a[64:72] + o[0:8], o[8:64], o[64:72] + b[0:8], b[8:40]], axis=0
            )
        )
    low = lane_iota((EXT, LANES)) < BLK
    turned = [pltpu.roll(s, BLK, 1) for s in sides]
    window[:, 0:128] = sides[0].astype(jnp.bfloat16)
    window[:, 128:256] = jnp.where(low, turned[0], turned[1]).astype(jnp.bfloat16)
    window[:, 256:384] = sides[1].astype(jnp.bfloat16)
    window[:, 384:512] = jnp.where(low, turned[1], turned[2]).astype(jnp.bfloat16)

    intensity = jnp.zeros((NBLK * rows, LANES), jnp.float32)
    for k in range(MODES):
        field_y = jnp.dot(
            r_ref[k * CH * rows : (k + 1) * CH * rows, :],
            window[...],
            preferred_element_type=jnp.float32,
        ).astype(jnp.bfloat16)
        lhs = jnp.concatenate(
            [
                jnp.concatenate(
                    [
                        field_y[c * rows : (c + 1) * rows, b * LANES : (b + 1) * LANES]
                        for c in range(CH)
                    ],
                    axis=1,
                )
                for b in range(NBLK)
            ],
            axis=0,
        )
        e = jnp.dot(
            lhs,
            jnp.concatenate([cf_ref[2 * k], cf_ref[2 * k + 1]], axis=0),
            preferred_element_type=jnp.float32,
        )
        fields[k] = e
        intensity = intensity + weight_ref[k] * (e * e)
    intensity = intensity + pltpu.roll(intensity, BLK, 1)
    low_rows = lane_iota((rows, LANES)) < BLK
    goal = []
    for h in range(2):
        t = target_ref[:, h * LANES : (h + 1) * LANES].astype(jnp.float32)
        other = pltpu.roll(t, BLK, 1)
        goal += [jnp.where(low_rows, t, other), jnp.where(low_rows, other, t)]
    resist = jax.nn.sigmoid(steepness * (intensity - threshold))
    resid = resist - jnp.concatenate(goal, axis=0)
    for h in range(2):
        first = resid[2 * h * rows : (2 * h + 1) * rows]
        second = resid[(2 * h + 1) * rows : (2 * h + 2) * rows]
        resid_ref[:, h * LANES : (h + 1) * LANES] = jnp.where(low_rows, first, second)
    grad_intensity = resid * steepness * resist * (1.0 - resist)

    lanes = lane_iota((rows, LANES))
    middle = (lanes >= HALF) & (lanes < HALF + BLK)
    left = lanes < HALF
    nothing = jnp.zeros((rows, LANES), jnp.float32)
    for k in range(MODES):
        g = 2.0 * weight_ref[k] * grad_intensity * fields[k]
        r31 = pltpu.roll(g, HALF, 1)
        r95 = pltpu.roll(g, HALF + BLK, 1)

        def part(v, b):
            return v[b * rows : (b + 1) * rows] if 0 <= b < NBLK else nothing

        parts = []
        for b in range(NBLK):
            re = jnp.where(
                middle, part(r31, b), jnp.where(left, part(r95, b - 1), part(r95, b + 1))
            )
            im = jnp.where(
                middle, part(r95, b), jnp.where(left, part(r31, b - 1), part(r31, b + 1))
            )
            parts.append(jnp.concatenate([re, im], axis=1))
        gw = jnp.concatenate(parts, axis=0).astype(jnp.bfloat16)
        for t in range(TERMS):
            gy = jnp.dot(
                gw, ca_ref[k * TERMS + t], preferred_element_type=jnp.float32
            ).astype(jnp.bfloat16)
            at = (k * TERMS + t) * rows
            for b in range(NBLK):
                gys[at : at + rows, b * LANES : (b + 1) * LANES] = gy[b * rows : (b + 1) * rows]

    total = jnp.zeros((2 * EXT, NBLK * LANES), jnp.float32)
    for n in range(2 * MODES):
        total = total + jnp.dot(
            rt_ref[n], gys[n * LANES : (n + 1) * LANES, :], preferred_element_type=jnp.float32
        )
    zeros = jnp.zeros((PAD, LANES), jnp.float32)
    for h in range(2):
        v0 = total[:EXT, 2 * h * LANES : (2 * h + 1) * LANES]
        v1 = total[:EXT, (2 * h + 1) * LANES : (2 * h + 2) * LANES]
        u0 = total[EXT:, 2 * h * LANES : (2 * h + 1) * LANES]
        u1 = total[EXT:, (2 * h + 1) * LANES : (2 * h + 2) * LANES]
        grad[h, PAD : PAD + EXT, :] = jnp.where(
            low, v0 + pltpu.roll(u0, BLK, 1), pltpu.roll(v1, BLK, 1) + u1
        )
        grad[h, :PAD, :] = zeros
        grad[h, PAD + EXT :, :] = zeros

    sums = (
        (0, acc_own, PAD + HALF),
        (1, acc_above, PAD + HALF - rows),
        (2, acc_below, PAD + HALF + rows),
    )
    for _, acc, _ in sums:
        acc[...] = jnp.zeros_like(acc)

    def gather(q, carry):
        for n, acc, base in sums:
            m = ids[n, 1, q]
            top = ids[n, 2, q] + base
            col = ids[n, 3, q]
            side = col >> 7
            after = jnp.minimum(side + 1, 1)
            shift = col & 127
            patch = jnp.zeros((8, LANES), jnp.float32)
            for k in range(4):
                at = pl.ds(top + k, 8, stride=4)
                both = jnp.where(lanes8 >= shift, grad[side, at, :], grad[after, at, :])
                moved = pltpu.roll(both, (LANES + 32 * k - shift) & 127, 1)
                patch = jnp.where((lanes8 >= 32 * k) & (lanes8 < 32 * k + MS), moved, patch)
            acc[m] += patch
        return carry

    lax.fori_loop(0, places, gather, 0, unroll=8)
    grads_ref[...] = (acc_own[...] + acc_above[...] + acc_below[...]).reshape(grads_ref.shape)


def main_step(weights, gathered, target, bands):
    devices, slabs = gathered.shape[:2]
    count = slabs - 1
    vmem = pl.BlockSpec(memory_space=pltpu.VMEM)
    accumulator = pltpu.VMEM((devices * count, 8, LANES), jnp.float32)
    return pl.pallas_call(
        main_kernel,
        out_shape=(
            jax.ShapeDtypeStruct(target.shape, jnp.float32),
            pltpu.VMEM((devices, count, 8, LANES), jnp.float32),
        ),
        in_specs=[pl.BlockSpec(memory_space=pltpu.SMEM)] + [vmem] * 6,
        out_specs=[vmem] * 2,
        scratch_shapes=[
            pltpu.VMEM((3, CROWS, LANES), jnp.float32),
            pltpu.VMEM((3, CROWS, LANES), jnp.float32),
            pltpu.VMEM((3, CROWS, LANES), jnp.float32),
            pltpu.VMEM((EXT, NBLK * LANES), jnp.bfloat16),
            pltpu.VMEM((MODES, NBLK * BLK, LANES), jnp.float32),
            pltpu.VMEM((MODES * TERMS * BLK, NBLK * LANES), jnp.bfloat16),
            pltpu.VMEM((2, 2 * PAD + EXT, LANES), jnp.float32),
            accumulator,
            accumulator,
            accumulator,
            pltpu.VMEM((3, 8, LANES), jnp.int32),
            pltpu.SMEM((3, 8, LANES), jnp.int32),
            pltpu.SemaphoreType.DMA,
        ],
        compiler_params=pltpu.CompilerParams(vmem_limit_bytes=24 << 20),
        name="imaging",
    )(weights, in_vmem(gathered), target, *[in_vmem(b) for b in bands])


def pack_kernel(masters_ref, owner_ref, local_ref, row_ref, col_ref, out_ref, spread):
    count = masters_ref.shape[0]
    for s in range(8):
        spread[pl.ds(s, count, stride=8), :] = masters_ref[:, s * LANES : (s + 1) * LANES]
    spread[8 * count :, :] = jnp.zeros((8, LANES), jnp.float32)
    for n, ref in enumerate((owner_ref, local_ref, row_ref, col_ref)):
        spread[8 * count + n : 8 * count + n + 1, :] = ref[...].astype(jnp.float32)
    out_ref[...] = spread[...].reshape(out_ref.shape).astype(jnp.bfloat16)


def pack(masters, *places):
    count = masters.shape[0]
    vmem = pl.BlockSpec(memory_space=pltpu.VMEM)
    return pl.pallas_call(
        pack_kernel,
        out_shape=pltpu.VMEM((1, count + 1, 8, LANES), jnp.bfloat16),
        in_specs=[vmem] * 5,
        out_specs=vmem,
        scratch_shapes=[pltpu.VMEM((8 * count + 8, LANES), jnp.float32)],
        compiler_params=pltpu.CompilerParams(vmem_limit_bytes=4 << 20),
        name="pack",
    )(masters, *[p.reshape(1, LANES) for p in places])


def update_kernel(kept_ref, sent_ref, velocity_ref, masters_ref, velocity_out, masters_out, sums):
    count = velocity_ref.shape[0]
    sums[...] = (kept_ref[0] + sent_ref[0]).reshape(count * 8, LANES)
    for s in range(8):
        at = slice(s * LANES, (s + 1) * LANES)
        gradient = sums[pl.ds(s, count, stride=8), :]
        velocity = momentum * velocity_ref[:, at] + gradient
        velocity_out[:, at] = velocity
        masters_out[:, at] = masters_ref[:, at] - step_size * velocity


def update(kept, sent, velocity, masters):
    vmem = pl.BlockSpec(memory_space=pltpu.VMEM)
    return pl.pallas_call(
        update_kernel,
        out_shape=(jax.ShapeDtypeStruct(velocity.shape, jnp.float32),) * 2,
        in_specs=[vmem] * 4,
        out_specs=[vmem] * 2,
        scratch_shapes=[pltpu.VMEM((8 * velocity.shape[0], LANES), jnp.float32)],
        compiler_params=pltpu.CompilerParams(vmem_limit_bytes=4 << 20),
        name="update",
    )(kept, sent, velocity, masters)


def swap(value, bit, devices):
    return lax.ppermute(value, "tx", [(i, i ^ bit) for i in range(devices)])


def on_device(
    masters,
    velocity,
    place_owner,
    place_local,
    place_row,
    place_col,
    row_taps,
    col_taps,
    mode_weights,
    target,
):
    devices = lax.axis_size("tx")
    bits = devices.bit_length() - 1
    held = pack(masters, place_owner, place_local, place_row, place_col)
    for b in range(bits):
        held = jnp.concatenate([held, swap(held, 1 << b, devices)], axis=0)
    bands = build_bands(row_taps, col_taps)
    resid, grads = main_step(mode_weights, held, target, bands)
    for b in range(bits):
        half = grads.shape[0] // 2
        sent = swap(grads[half:], 1 << b, devices)
        if b < bits - 1:
            grads = grads[:half] + sent
    velocity_new, masters_new = update(grads, sent, velocity, masters)
    return resid, velocity_new, masters_new


def solution(mesh):
    return jax.shard_map(
        on_device,
        mesh=mesh,
        in_specs=(
            P(("groups", "tx"), None),
            P(("groups", "tx"), None),
            P(("groups", "tx"), None),
            P(("groups", "tx")),
            P(("groups", "tx")),
            P(("groups", "tx")),
            P(),
            P(),
            P(),
            P(("groups", "tx"), None),
        ),
        out_specs=(P(("groups", "tx"), None), P(("groups", "tx"), None), P(("groups", "tx"), None)),
        check_vma=False,
    )
```

time: 95.5 us -> 66.4 us (0.70)
  Pallas kernels: 55.8 us -> 31 us
  blocking collectives: 16.1 us -> 0 us
  waiting for transfers between devices: 0.01 us -> 13.6 us
  other arithmetic: 4.93 us -> 0.06 us
  starting transfers between devices: 12.3 us -> 15.7 us
    pallas_call x1, Pallas kernels: 44.3 us -> 19.8 us  [main_step(): pl.pallas_call(main_kernel, out_shape=(jax.ShapeDtypeStruct(target.shape,...]
    all_to_all x1 -> x0, blocking collectives: 16.1 us -> none  [on_device(): lax.all_to_all(grads.reshape(devices, count, 8, LANES), 'tx', split_axis=...]
    ppermute x2 -> x8, waiting for transfers between devices: 0.01 us -> 13.6 us  [swap(): return lax.ppermute(value, 'tx', [(i, i ^ bit) for i in range(devices)])]
    ppermute x2 -> x8, starting transfers between devices: 4.32 us -> 15.7 us  [swap(): return lax.ppermute(value, 'tx', [(i, i ^ bit) for i in range(devices)])]
    all_to_all x1 -> x0, starting transfers between devices: 7.98 us -> none  [on_device(): lax.all_to_all(everywhere, 'tx', split_axis=0, concat_axis=0, tiled=True)]
    unnamed x7 -> x26, local copies, waits for them, and re-layouts: 0.65 us -> 4.86 us
    slice x4, local copies, waits for them, and re-layouts: 3.34 us -> 0.03 us  [on_device(): sent = swap(grads[half:], 1 << b, devices)]
    another operation x4 -> x0, other arithmetic: 2.19 us -> none  [the longest x2 0.81 us: build_bands(): jnp.stack([jnp.pad(row, ((0, 0), (0, gap))), reversed_taps(row), reversed...]
  transfers between devices with their start and end apart: 3 -> 8, of which waited for: 0 -> 7; matrix products, arithmetic and copies ran while one was open for 8% -> 0% of each run, Pallas kernels for 10% -> 16%
where the time goes in v2:
time: 66.4 us; the launch traced here: 66 us
  Pallas kernels  31 us (47%)
  starting transfers between devices  15.7 us (24%)
  waiting for transfers between devices  13.6 us (20%)
  local copies, waits for them, and re-layouts  4.9 us (7%)
  between operations  0.81 us (1%)
    pallas_call x1, Pallas kernels, main_step(): pl.pallas_call(main_kernel, out_shape=(jax.ShapeDtypeStruct(target.shape,...  19.8 us
    ppermute x8, starting transfers between devices, swap(): return lax.ppermute(value, 'tx', [(i, i ^ bit) for i in range(devices)])  15.7 us
    ppermute x8, waiting for transfers between devices, swap(): return lax.ppermute(value, 'tx', [(i, i ^ bit) for i in range(devices)])  13.6 us
    pallas_call x3, Pallas kernels, build_bands(): pl.pallas_call(kernel, out_shape=pltpu.VMEM(shape, jnp.bfloat16), in_spec...  8.27 us
    unnamed x26, local copies, waits for them, and re-layouts  4.86 us
    pallas_call x1, Pallas kernels, build_bands(): pl.pallas_call(row_bands_kernel, out_shape=(pltpu.VMEM((MODES * CH * BLK,...  2.27 us
  transfers between devices with their start and end apart: 8, of which 7 were waited for; matrix products, arithmetic and copies ran while one was open for 0% of the time, Pallas kernels for 16%

profile of v2, /device:TPU:0, one launch (start us, length us, event | category | flops | bytes accessed | tf_op | source)
XLA Modules:
  0.0 66.0 jit_solution(6724472053256607582)
XLA Ops:
  0.6 0.7 %copy-done = f32[4,1024]{1,0:T(4,128)S(1)} copy-done((f32[4,1024]{1,0:T(4,128)S(1)}, f32[4,1024]{1,0:T(4,128)}, u32[]{:S(2)}) %copy-start) | copy-done | bytes 16408
  1.4 0.7 copy-done.6
  2.0 0.7 copy-done.7
  2.7 0.7 copy-done.8
  4.6 0.7 %copy-done.3 = bf16[12,4,2,63]{3,2,1,0:T(2,128)(2,1)S(1)} copy-done((bf16[12,4,2,63]{3,2,1,0:T(2,128)(2,1)S(1)}, bf16[12,4,2,63]{3,2,1,0:T(2,128)(2,1)}, u32[]{:S(2)}) %copy-start.3) | copy-done | bytes 12120
  5.3 0.7 %copy-done.4 = bf16[12,4,2,63]{3,2,1,0:T(2,128)(2,1)S(1)} copy-done((bf16[12,4,2,63]{3,2,1,0:T(2,128)(2,1)S(1)}, bf16[12,4,2,63]{3,2,1,0:T(2,128)(2,1)}, u32[]{:S(2)}) %copy-start.4) | copy-done | bytes 12120
  6.0 2.3 %row_bands.1 = (bf16[6144,128]{1,0:T(8,128)(2,1)S(1)}, f32[384,128]{1,0:T(8,128)S(1)}) custom-call(bf16[12,4,2,63]{3,2,1,0:T(2,128)(2,1)S(1)} %copy-done.3, bf16[12,4,2,63]{3,2,1,0:T(2,128)(2,1)S(1)} %copy-done.4), custom_call_target="tpu_custom_call" | custom-call | tf_op jit(solution)/shard_map/row_bands/pallas_call | solution.py:139
  8.3 2.5 %row_adjoint.1.rt_ref = bf16[24,256,128]{2,1,0:T(8,128)(2,1)S(1)} custom-call(f32[384,128]{1,0:T(8,128)S(1)} %get-tuple-element.10.taps), custom_call_target="tpu_custom_call" | custom-call | tf_op jit(solution)/shard_map/row_adjoint/pallas_call | solution.py:152
  10.8 2.9 %column_adjoint.1.ca_ref = bf16[48,256,128]{2,1,0:T(8,128)(2,1)S(1)} custom-call(f32[384,128]{1,0:T(8,128)S(1)} %get-tuple-element.10.taps), custom_call_target="tpu_custom_call" | custom-call | tf_op jit(solution)/shard_map/column_adjoint/pallas_call | solution.py:152
  13.7 2.9 %column_bands.1.cf_ref = bf16[24,512,128]{2,1,0:T(8,128)(2,1)S(1)} custom-call(f32[384,128]{1,0:T(8,128)S(1)} %get-tuple-element.10.taps), custom_call_target="tpu_custom_call" | custom-call | tf_op jit(solution)/shard_map/column_bands/pallas_call | solution.py:152
  16.6 2.6 %collective-permute-start.1 = (bf16[2,5,8,128]{3,2,1,0:T(8,128)(2,1)S(1)}, bf16[2,5,8,128]{3,2,1,0:T(8,128)(2,1)S(1)}, u32[]{:S(2)}, u32[]{:S(2)}) collective-permute-start(bf16[2,5,8,128]{3,2,1,0:T(8,128)(2,1)S(1)} %pad_maximum_fusion.2), channel_id=1, source_target_pairs={{0,2},{1,3},{2,0},{3,1},{4,6},{5,7},{6,4},{7,5},{8,10},{9,11},{10,... | collective-permute-start | bytes 61448 | tf_op jit(solution)/shard_map/ppermute | solution.py:452
  19.2 1.8 %collective-permute-done.1 = bf16[2,5,8,128]{3,2,1,0:T(8,128)(2,1)S(1)} collective-permute-done((bf16[2,5,8,128]{3,2,1,0:T(8,128)(2,1)S(1)}, bf16[2,5,8,128]{3,2,1,0:T(8,128)(2,1)S(1)}, u32[]{:S(2)}, u32[]{:S(2)}) %collective-permute-start.1) | collective-permute-done | bytes 20512 | tf_op jit(solution)/shard_map/ppermute | solution.py:452
  21.0 2.1 %collective-permute-start.2 = (bf16[4,5,8,128]{3,2,1,0:T(8,128)(2,1)S(1)}, bf16[4,5,8,128]{3,2,1,0:T(8,128)(2,1)S(1)}, u32[]{:S(2)}, u32[]{:S(2)}) collective-permute-start(bf16[4,5,8,128]{3,2,1,0:T(8,128)(2,1)S(1)} %pad_maximum_fusion.1), channel_id=1, source_target_pairs={{0,4},{1,5},{2,6},{3,7},{4,0},{5,1},{6,2},{7,3},{8,12},{9,13},{10,... | collective-permute-start | bytes 122888 | tf_op jit(solution)/shard_map/ppermute | solution.py:452
  23.2 2.0 %collective-permute-done.2 = bf16[4,5,8,128]{3,2,1,0:T(8,128)(2,1)S(1)} collective-permute-done((bf16[4,5,8,128]{3,2,1,0:T(8,128)(2,1)S(1)}, bf16[4,5,8,128]{3,2,1,0:T(8,128)(2,1)S(1)}, u32[]{:S(2)}, u32[]{:S(2)}) %collective-permute-start.2) | collective-permute-done | bytes 40992 | tf_op jit(solution)/shard_map/ppermute | solution.py:452
  25.1 3.1 %collective-permute-start.3 = (bf16[8,5,8,128]{3,2,1,0:T(8,128)(2,1)S(1)}, bf16[8,5,8,128]{3,2,1,0:T(8,128)(2,1)S(1)}, u32[]{:S(2)}, u32[]{:S(2)}) collective-permute-start(bf16[8,5,8,128]{3,2,1,0:T(8,128)(2,1)S(1)} %pad_maximum_fusion), channel_id=1, source_target_pairs={{0,8},{1,9},{2,10},{3,11},{4,12},{5,13},{6,14},{7,15},{8,0},{9,1},... | collective-permute-start | bytes 245768 | tf_op jit(solution)/shard_map/ppermute | solution.py:452
  28.3 2.4 %collective-permute-done.3 = bf16[8,5,8,128]{3,2,1,0:T(8,128)(2,1)S(1)} collective-permute-done((bf16[8,5,8,128]{3,2,1,0:T(8,128)(2,1)S(1)}, bf16[8,5,8,128]{3,2,1,0:T(8,128)(2,1)S(1)}, u32[]{:S(2)}, u32[]{:S(2)}) %collective-permute-start.3) | collective-permute-done | bytes 81952 | tf_op jit(solution)/shard_map/ppermute | solution.py:452
  30.7 19.8 %imaging.1 = (f32[64,256]{1,0:T(8,128)}, f32[16,4,8,128]{3,2,1,0:T(8,128)S(1)}) custom-call(f32[12]{0:T(128)S(1)} %copy-done.10, bf16[16,5,8,128]{3,2,1,0:T(8,128)(2,1)S(1)} %constant_dynamic-update-slice_fusion.gathered_ref, bf16[64,256]{1,0:T(8,128)(2,1)S(1)} %copy-done.2, bf16[6144,128]{1,0:T(8,128)(2,1)S(1)} %get-tuple-element.9.r_ref, ...), custom_call_target="tpu_custom_call" | custom-call | tf_op jit(solution)/shard_map/imaging/pallas_call | solution.py:375
  50.6 1.3 %collective-permute-done.4 = f32[8,4,8,128]{3,2,1,0:T(8,128)S(1)} collective-permute-done((f32[8,4,8,128]{3,2,1,0:T(8,128)S(1)}, f32[8,4,8,128]{3,2,1,0:T(8,128)S(1)}, u32[]{:S(2)}, u32[]{:S(2)}) %collective-permute-start.4) | collective-permute-done | bytes 131104 | tf_op jit(solution)/shard_map/ppermute | solution.py:452
  52.0 1.9 %collective-permute-start.5 = (f32[4,4,8,128]{3,2,1,0:T(8,128)S(1)}, f32[4,4,8,128]{3,2,1,0:T(8,128)S(1)}, u32[]{:S(2)}, u32[]{:S(2)}) collective-permute-start(f32[4,4,8,128]{3,2,1,0:T(8,128)S(1)} %slice.29), channel_id=1, source_target_pairs={{0,2},{1,3},{2,0},{3,1},{4,6},{5,7},{6,4},{7,5},{8,10},{9,11},{10,... | collective-permute-start | bytes 196616 | tf_op jit(solution)/shard_map/ppermute | solution.py:452
  53.9 2.4 %collective-permute-done.5 = f32[4,4,8,128]{3,2,1,0:T(8,128)S(1)} collective-permute-done((f32[4,4,8,128]{3,2,1,0:T(8,128)S(1)}, f32[4,4,8,128]{3,2,1,0:T(8,128)S(1)}, u32[]{:S(2)}, u32[]{:S(2)}) %collective-permute-start.5) | collective-permute-done | bytes 65568 | tf_op jit(solution)/shard_map/ppermute | solution.py:452
  56.4 2.0 %collective-permute-start.6 = (f32[2,4,8,128]{3,2,1,0:T(8,128)S(1)}, f32[2,4,8,128]{3,2,1,0:T(8,128)S(1)}, u32[]{:S(2)}, u32[]{:S(2)}) collective-permute-start(f32[2,4,8,128]{3,2,1,0:T(8,128)S(1)} %slice.31), channel_id=1, source_target_pairs={{0,4},{1,5},{2,6},{3,7},{4,0},{5,1},{6,2},{7,3},{8,12},{9,13},{10,... | collective-permute-start | bytes 98312 | tf_op jit(solution)/shard_map/ppermute | solution.py:452
  58.4 2.0 %collective-permute-done.6 = f32[2,4,8,128]{3,2,1,0:T(8,128)S(1)} collective-permute-done((f32[2,4,8,128]{3,2,1,0:T(8,128)S(1)}, f32[2,4,8,128]{3,2,1,0:T(8,128)S(1)}, u32[]{:S(2)}, u32[]{:S(2)}) %collective-permute-start.6) | collective-permute-done | bytes 32800 | tf_op jit(solution)/shard_map/ppermute | solution.py:452
  60.4 3.3 %collective-permute-start.7 = (f32[1,4,8,128]{3,2,1,0:T(8,128)S(1)}, f32[1,4,8,128]{3,2,1,0:T(8,128)S(1)}, u32[]{:S(2)}, u32[]{:S(2)}) collective-permute-start(f32[1,4,8,128]{3,2,1,0:T(8,128)S(1)} %slice.32), channel_id=1, source_target_pairs={{0,8},{1,9},{2,10},{3,11},{4,12},{5,13},{6,14},{7,15},{8,0},{9,1},... | collective-permute-start | bytes 49160 | tf_op jit(solution)/shard_map/ppermute | solution.py:452
  63.7 1.7 %collective-permute-done.7.sent_ref = f32[1,4,8,128]{3,2,1,0:T(8,128)S(1)} collective-permute-done((f32[1,4,8,128]{3,2,1,0:T(8,128)S(1)}, f32[1,4,8,128]{3,2,1,0:T(8,128)S(1)}, u32[]{:S(2)}, u32[]{:S(2)}) %collective-permute-start.7) | collective-permute-done | bytes 16416 | tf_op jit(solution)/shard_map/ppermute | solution.py:452
  (36 shorter events, 2.1 us)
Async XLA Ops:
  0.6 0.7 %copy-start = (f32[4,1024]{1,0:T(4,128)S(1)}, f32[4,1024]{1,0:T(4,128)}, u32[]{:S(2)}) copy-start(f32[4,1024]{1,0:T(4,128)} %masters_ref.3) | copy-start | bytes 49156
  1.4 0.7 copy-start.6
  2.0 0.7 copy-start.7
  2.7 0.7 copy-start.8
  3.3 0.7 copy-start.9
  4.0 12.6 %collective-permute-start = (bf16[1,5,8,128]{3,2,1,0:T(8,128)(2,1)S(1)}, bf16[1,5,8,128]{3,2,1,0:T(8,128)(2,1)S(1)}, u32[]{:S(2)}, u32[]{:S(2)}) collective-permute-start(bf16[1,5,8,128]{3,2,1,0:T(8,128)(2,1)S(1)} %pack.1), channel_id=1, source_target_pairs={{0,1},{1,0},{2,3},{3,2},{4,5},{5,4},{6,7},{7,6},{8,9},{9,8},{10,11... | collective-permute-start | bytes 30728 | tf_op jit(solution)/shard_map/ppermute | solution.py:452
  4.6 0.7 %copy-start.3 = (bf16[12,4,2,63]{3,2,1,0:T(2,128)(2,1)S(1)}, bf16[12,4,2,63]{3,2,1,0:T(2,128)(2,1)}, u32[]{:S(2)}) copy-start(bf16[12,4,2,63]{3,2,1,0:T(2,128)(2,1)} %row_ref.1) | copy-start | bytes 36292
  5.3 0.7 %copy-start.4 = (bf16[12,4,2,63]{3,2,1,0:T(2,128)(2,1)S(1)}, bf16[12,4,2,63]{3,2,1,0:T(2,128)(2,1)}, u32[]{:S(2)}) copy-start(bf16[12,4,2,63]{3,2,1,0:T(2,128)(2,1)} %col_ref.1) | copy-start | bytes 36292
  10.8 19.9 %copy-start.2 = (bf16[64,256]{1,0:T(8,128)(2,1)S(1)}, bf16[64,256]{1,0:T(8,128)(2,1)}, u32[]{:S(2)}) copy-start(bf16[64,256]{1,0:T(8,128)(2,1)} %target_ref.1) | copy-start | bytes 98308
  10.8 19.9 %copy-start.10 = (f32[12]{0:T(128)S(1)}, f32[12]{0:T(128)}, u32[]{:S(2)}) copy-start(f32[12]{0:T(128)} %weight_ref.1) | copy-start | bytes 148
  16.6 4.4 %collective-permute-start.1 = (bf16[2,5,8,128]{3,2,1,0:T(8,128)(2,1)S(1)}, bf16[2,5,8,128]{3,2,1,0:T(8,128)(2,1)S(1)}, u32[]{:S(2)}, u32[]{:S(2)}) collective-permute-start(bf16[2,5,8,128]{3,2,1,0:T(8,128)(2,1)S(1)} %pad_maximum_fusion.2), channel_id=1, source_target_pairs={{0,2},{1,3},{2,0},{3,1},{4,6},{5,7},{6,4},{7,5},{8,10},{9,11},{10,... | collective-permute-start | bytes 61448 | tf_op jit(solution)/shard_map/ppermute | solution.py:452
  21.0 4.1 %collective-permute-start.2 = (bf16[4,5,8,128]{3,2,1,0:T(8,128)(2,1)S(1)}, bf16[4,5,8,128]{3,2,1,0:T(8,128)(2,1)S(1)}, u32[]{:S(2)}, u32[]{:S(2)}) collective-permute-start(bf16[4,5,8,128]{3,2,1,0:T(8,128)(2,1)S(1)} %pad_maximum_fusion.1), channel_id=1, source_target_pairs={{0,4},{1,5},{2,6},{3,7},{4,0},{5,1},{6,2},{7,3},{8,12},{9,13},{10,... | collective-permute-start | bytes 122888 | tf_op jit(solution)/shard_map/ppermute | solution.py:452
  25.1 5.5 %collective-permute-start.3 = (bf16[8,5,8,128]{3,2,1,0:T(8,128)(2,1)S(1)}, bf16[8,5,8,128]{3,2,1,0:T(8,128)(2,1)S(1)}, u32[]{:S(2)}, u32[]{:S(2)}) collective-permute-start(bf16[8,5,8,128]{3,2,1,0:T(8,128)(2,1)S(1)} %pad_maximum_fusion), channel_id=1, source_target_pairs={{0,8},{1,9},{2,10},{3,11},{4,12},{5,13},{6,14},{7,15},{8,0},{9,1},... | collective-permute-start | bytes 245768 | tf_op jit(solution)/shard_map/ppermute | solution.py:452
  30.7 34.7 %copy-start.1 = (f32[4,1024]{1,0:T(4,128)S(1)}, f32[4,1024]{1,0:T(4,128)}, u32[]{:S(2)}) copy-start(f32[4,1024]{1,0:T(4,128)} %masters_ref.3) | copy-start | bytes 49156
  30.7 34.7 %copy-start.5 = (f32[4,1024]{1,0:T(4,128)S(1)}, f32[4,1024]{1,0:T(4,128)}, u32[]{:S(2)}) copy-start(f32[4,1024]{1,0:T(4,128)} %velocity_ref.1) | copy-start | bytes 49156
  50.6 1.4 %collective-permute-start.4 = (f32[8,4,8,128]{3,2,1,0:T(8,128)S(1)}, f32[8,4,8,128]{3,2,1,0:T(8,128)S(1)}, u32[]{:S(2)}, u32[]{:S(2)}) collective-permute-start(f32[8,4,8,128]{3,2,1,0:T(8,128)S(1)} %slice.22), channel_id=1, source_target_pairs={{0,1},{1,0},{2,3},{3,2},{4,5},{5,4},{6,7},{7,6},{8,9},{9,8},{10,11... | collective-permute-start | bytes 393224 | tf_op jit(solution)/shard_map/ppermute | solution.py:452
  52.0 4.3 %collective-permute-start.5 = (f32[4,4,8,128]{3,2,1,0:T(8,128)S(1)}, f32[4,4,8,128]{3,2,1,0:T(8,128)S(1)}, u32[]{:S(2)}, u32[]{:S(2)}) collective-permute-start(f32[4,4,8,128]{3,2,1,0:T(8,128)S(1)} %slice.29), channel_id=1, source_target_pairs={{0,2},{1,3},{2,0},{3,1},{4,6},{5,7},{6,4},{7,5},{8,10},{9,11},{10,... | collective-permute-start | bytes 196616 | tf_op jit(solution)/shard_map/ppermute | solution.py:452
  56.4 4.0 %collective-permute-start.6 = (f32[2,4,8,128]{3,2,1,0:T(8,128)S(1)}, f32[2,4,8,128]{3,2,1,0:T(8,128)S(1)}, u32[]{:S(2)}, u32[]{:S(2)}) collective-permute-start(f32[2,4,8,128]{3,2,1,0:T(8,128)S(1)} %slice.31), channel_id=1, source_target_pairs={{0,4},{1,5},{2,6},{3,7},{4,0},{5,1},{6,2},{7,3},{8,12},{9,13},{10,... | collective-permute-start | bytes 98312 | tf_op jit(solution)/shard_map/ppermute | solution.py:452
  60.4 5.0 %collective-permute-start.7 = (f32[1,4,8,128]{3,2,1,0:T(8,128)S(1)}, f32[1,4,8,128]{3,2,1,0:T(8,128)S(1)}, u32[]{:S(2)}, u32[]{:S(2)}) collective-permute-start(f32[1,4,8,128]{3,2,1,0:T(8,128)S(1)} %slice.32), channel_id=1, source_target_pairs={{0,8},{1,9},{2,10},{3,11},{4,12},{5,13},{6,14},{7,15},{8,0},{9,1},... | collective-permute-start | bytes 49160 | tf_op jit(solution)/shard_map/ppermute | solution.py:452

commit v3 on v2

--- a/solution.py
+++ b/solution.py
@@ -1,3 +1,4 @@
+import functools
 import jax
 import jax.numpy as jnp
 from jax import lax
@@ -27,6 +28,10 @@
 
 def in_vmem(x):
     return pltpu.with_memory_space_constraint(x, pltpu.VMEM)
+
+
+def in_hbm(x):
+    return pltpu.with_memory_space_constraint(x, pltpu.HBM)
 
 
 def lane_iota(shape):
@@ -74,10 +79,10 @@
             r_ref[pl.ds(at * BLK, BLK), :] = half_band(skew(taps[pl.ds(at, 1), :], 0))
         return carry
 
-    lax.fori_loop(0, 2 * MODES, step, 0)
-
-
-def row_adjoint_kernel(taps, rt_ref):
+    lax.fori_loop(0, 2 * MODES, step, 0, unroll=3)
+
+
+def row_adjoint_kernel(taps, _, rt_ref):
     count = MODES * CH
     low = low_lanes()
 
@@ -91,10 +96,10 @@
             rt_ref[n, par * EXT + BLK : (par + 1) * EXT, :] = half_band(jnp.where(low, a_far, b))
         return carry
 
-    lax.fori_loop(0, 2 * MODES, step, 0)
-
-
-def column_bands_kernel(taps, cf_ref):
+    lax.fori_loop(0, 2 * MODES, step, 0, unroll=3)
+
+
+def column_bands_kernel(taps, _, cf_ref):
     count = MODES * CH
     low = low_lanes()
 
@@ -111,10 +116,10 @@
             cf_ref[n, at + EXT + BLK : at + 2 * EXT, :] = half_band(jnp.where(low, -b_far, a))
         return carry
 
-    lax.fori_loop(0, 2 * MODES, step, 0)
-
-
-def column_adjoint_kernel(taps, ca_ref):
+    lax.fori_loop(0, 2 * MODES, step, 0, unroll=3)
+
+
+def column_adjoint_kernel(taps, _, ca_ref):
     count = MODES * CH
     low = low_lanes()
 
@@ -130,10 +135,10 @@
             ca_ref[n * 2 + t, EXT + BLK :, :] = half_band(jnp.where(low, b_far, a))
         return carry
 
-    lax.fori_loop(0, 2 * MODES, step, 0)
-
-
-def build_bands(row_taps, col_taps):
+    lax.fori_loop(0, 2 * MODES, step, 0, unroll=3)
+
+
+def build_bands(row_taps, col_taps, stages):
     vmem = pl.BlockSpec(memory_space=pltpu.VMEM)
     small = pltpu.CompilerParams(vmem_limit_bytes=4 << 20)
     r, taps = pl.pallas_call(
@@ -146,27 +151,31 @@
         out_specs=[vmem] * 2,
         compiler_params=small,
         name="row_bands",
-    )(row_taps, col_taps)
+    )(in_hbm(row_taps), in_hbm(col_taps))
     taps = in_vmem(taps)
     built = [
         pl.pallas_call(
             kernel,
             out_shape=pltpu.VMEM(shape, jnp.bfloat16),
-            in_specs=[vmem],
+            in_specs=[vmem, pl.BlockSpec(memory_space=pl.ANY)],
             out_specs=vmem,
             compiler_params=small,
             name=name,
-        )(taps)
-        for kernel, shape, name in (
-            (row_adjoint_kernel, (2 * MODES, 2 * EXT, LANES), "row_adjoint"),
-            (column_bands_kernel, (2 * MODES, CH * EXT // 2, LANES), "column_bands"),
-            (column_adjoint_kernel, (4 * MODES, 2 * EXT, LANES), "column_adjoint"),
+        )(taps, stage)
+        for stage, (kernel, shape, name) in zip(
+            stages,
+            (
+                (column_bands_kernel, (2 * MODES, CH * EXT // 2, LANES), "column_bands"),
+                (row_adjoint_kernel, (2 * MODES, 2 * EXT, LANES), "row_adjoint"),
+                (column_adjoint_kernel, (4 * MODES, 2 * EXT, LANES), "column_adjoint"),
+            ),
         )
     ]
-    return [r, *built]
+    return [r, built[1], built[0], built[2]]
 
 
 def main_kernel(
+    devices,
     weight_ref,
     gathered_ref,
     target_ref,
@@ -190,7 +199,7 @@
     ids,
     sem,
 ):
-    devices, slabs = gathered_ref.shape[:2]
+    slabs = gathered_ref.shape[0] // devices
     count = slabs - 1
     places = LANES
     rows = BLK
@@ -199,7 +208,7 @@
     for n, (other, missing) in enumerate(
         ((me, 0), (jnp.maximum(me - 1, 0), 0), (jnp.minimum(me + 1, devices - 1), BLK - MS))
     ):
-        slab = gathered_ref[other ^ me, count].astype(jnp.float32).astype(jnp.int32)
+        slab = gathered_ref[(other ^ me) * slabs + count].astype(jnp.float32).astype(jnp.int32)
         owner, local = slab[0:1] ^ me, slab[1:2]
         turned = sum(((owner >> b) & 1) << (bits - 1 - b) for b in range(bits))
         table[n, 0:1, :] = owner * slabs + local
@@ -217,8 +226,7 @@
 
     def place(q, carry):
         for n, canvas in canvases:
-            at = ids[n, 0, q]
-            master = gathered_ref[at // slabs, at % slabs].astype(jnp.float32)
+            master = gathered_ref[ids[n, 0, q]].astype(jnp.float32)
             top = ids[n, 2, q] + 7
             col = ids[n, 3, q] + HALF
             side = col >> 7
@@ -373,7 +381,7 @@
     vmem = pl.BlockSpec(memory_space=pltpu.VMEM)
     accumulator = pltpu.VMEM((devices * count, 8, LANES), jnp.float32)
     return pl.pallas_call(
-        main_kernel,
+        functools.partial(main_kernel, devices),
         out_shape=(
             jax.ShapeDtypeStruct(target.shape, jnp.float32),
             pltpu.VMEM((devices, count, 8, LANES), jnp.float32),
@@ -397,7 +405,7 @@
         ],
         compiler_params=pltpu.CompilerParams(vmem_limit_bytes=24 << 20),
         name="imaging",
-    )(weights, in_vmem(gathered), target, *[in_vmem(b) for b in bands])
+    )(weights, in_vmem(gathered.reshape(devices * slabs, 8, LANES)), target, *[in_vmem(b) for b in bands])
 
 
 def pack_kernel(masters_ref, owner_ref, local_ref, row_ref, col_ref, out_ref, spread):
@@ -421,7 +429,7 @@
         scratch_shapes=[pltpu.VMEM((8 * count + 8, LANES), jnp.float32)],
         compiler_params=pltpu.CompilerParams(vmem_limit_bytes=4 << 20),
         name="pack",
-    )(masters, *[p.reshape(1, LANES) for p in places])
+    )(in_hbm(masters), *[in_hbm(p.reshape(1, LANES)) for p in places])
 
 
 def update_kernel(kept_ref, sent_ref, velocity_ref, masters_ref, velocity_out, masters_out, sums):
@@ -467,9 +475,11 @@
     devices = lax.axis_size("tx")
     bits = devices.bit_length() - 1
     held = pack(masters, place_owner, place_local, place_row, place_col)
+    stages = []
     for b in range(bits):
         held = jnp.concatenate([held, swap(held, 1 << b, devices)], axis=0)
-    bands = build_bands(row_taps, col_taps)
+        stages.append(held)
+    bands = build_bands(row_taps, col_taps, stages[-4:-1])
     resid, grads = main_step(mode_weights, held, target, bands)
     for b in range(bits):
         half = grads.shape[0] // 2

time: 66.4 us -> 51.2 us (0.77)
  Pallas kernels: 31 us -> 25.7 us
  waiting for transfers between devices: 13.6 us -> 8.72 us
  local copies, waits for them, and re-layouts: 4.9 us -> 0.1 us
    ppermute x8, waiting for transfers between devices: 13.6 us -> 8.72 us  [swap(): return lax.ppermute(value, 'tx', [(i, i ^ bit) for i in range(devices)])]
    unnamed x26 -> x12, local copies, waits for them, and re-layouts: 4.86 us -> 0.06 us
    pallas_call x3, Pallas kernels: 8.27 us -> 4.91 us  [build_bands(): pl.pallas_call(kernel, out_shape=pltpu.VMEM(shape, jnp.bfloat16), in_spec...]
    pallas_call x1, Pallas kernels: 19.8 us -> 17.6 us  [main_step(): pl.pallas_call(functools.partial(main_kernel, devices), out_shape=(jax.Sh...]
    pallas_call x1, Pallas kernels: 0.01 us -> 0.77 us  [pack(): pl.pallas_call(pack_kernel, out_shape=pltpu.VMEM((1, count + 1, 8, LANES)...]
  transfers between devices with their start and end apart: 8 -> 8, of which waited for: 7 -> 6; matrix products, arithmetic and copies ran while one was open for 0% -> 0% of each run, Pallas kernels for 16% -> 13%
where the time goes in v3:
time: 51.2 us; the launch traced here: 51 us
  Pallas kernels  25.7 us (50%)
  starting transfers between devices  15.6 us (30%)
  waiting for transfers between devices  8.72 us (17%)
  between operations  0.81 us (2%)
    pallas_call x1, Pallas kernels, main_step(): pl.pallas_call(functools.partial(main_kernel, devices), out_shape=(jax.Sh...  17.6 us
    ppermute x8, starting transfers between devices, swap(): return lax.ppermute(value, 'tx', [(i, i ^ bit) for i in range(devices)])  15.6 us
    ppermute x8, waiting for transfers between devices, swap(): return lax.ppermute(value, 'tx', [(i, i ^ bit) for i in range(devices)])  8.72 us
    pallas_call x3, Pallas kernels, build_bands(): pl.pallas_call(kernel, out_shape=pltpu.VMEM(shape, jnp.bfloat16), in_spec...  4.91 us
    pallas_call x1, Pallas kernels, build_bands(): pl.pallas_call(row_bands_kernel, out_shape=(pltpu.VMEM((MODES * CH * BLK,...  1.89 us
  transfers between devices with their start and end apart: 8, of which 6 were waited for; matrix products, arithmetic and copies ran while one was open for 0% of the time, Pallas kernels for 13%

profile of v3, /device:TPU:0, one launch (start us, length us, event | category | flops | bytes accessed | tf_op | source)
XLA Modules:
  0.0 51.0 jit_solution(8453528749577806561)
XLA Ops:
  0.6 0.8 %pack.1 = bf16[1,5,8,128]{3,2,1,0:T(8,128)(2,1)S(1)} custom-call(f32[4,1024]{1,0:T(4,128)} %masters_ref.3, s32[1,128]{1,0:T(1,128)} %bitcast.6, s32[1,128]{1,0:T(1,128)} %bitcast.7, s32[1,128]{1,0:T(1,128)} %bitcast.8, s32[1,128]{1,0:T(1,128)} %bitcast.9), custom_call_target="tpu_custom_call" | custom-call | tf_op jit(solution)/shard_map/pack/pallas_call | solution.py:424
  1.4 0.6 %collective-permute-start = (bf16[1,5,8,128]{3,2,1,0:T(8,128)(2,1)S(1)}, bf16[1,5,8,128]{3,2,1,0:T(8,128)(2,1)S(1)}, u32[]{:S(2)}, u32[]{:S(2)}) collective-permute-start(bf16[1,5,8,128]{3,2,1,0:T(8,128)(2,1)S(1)} %pack.1), channel_id=1, source_target_pairs={{0,1},{1,0},{2,3},{3,2},{4,5},{5,4},{6,7},{7,6},{8,9},{9,8},{10,11... | collective-permute-start | bytes 30728 | tf_op jit(solution)/shard_map/ppermute | solution.py:460
  2.0 1.9 %row_bands.1 = (bf16[6144,128]{1,0:T(8,128)(2,1)S(1)}, f32[384,128]{1,0:T(8,128)S(1)}) custom-call(bf16[12,4,2,63]{3,2,1,0:T(2,128)(2,1)} %row_ref.1, bf16[12,4,2,63]{3,2,1,0:T(2,128)(2,1)} %col_ref.1), custom_call_target="tpu_custom_call" | custom-call | tf_op jit(solution)/shard_map/row_bands/pallas_call | solution.py:144
  3.9 2.6 %collective-permute-start.1 = (bf16[2,5,8,128]{3,2,1,0:T(8,128)(2,1)S(1)}, bf16[2,5,8,128]{3,2,1,0:T(8,128)(2,1)S(1)}, u32[]{:S(2)}, u32[]{:S(2)}) collective-permute-start(bf16[2,5,8,128]{3,2,1,0:T(8,128)(2,1)S(1)} %pad_maximum_fusion.2._), channel_id=1, source_target_pairs={{0,2},{1,3},{2,0},{3,1},{4,6},{5,7},{6,4},{7,5},{8,10},{9,11},{10,... | collective-permute-start | bytes 61448 | tf_op jit(solution)/shard_map/ppermute | solution.py:460
  6.5 1.8 %column_bands.1.cf_ref = bf16[24,512,128]{2,1,0:T(8,128)(2,1)S(1)} custom-call(f32[384,128]{1,0:T(8,128)S(1)} %get-tuple-element.10.taps, bf16[2,5,8,128]{3,2,1,0:T(8,128)(2,1)S(1)} %pad_maximum_fusion.2._), custom_call_target="tpu_custom_call" | custom-call | tf_op jit(solution)/shard_map/column_bands/pallas_call | solution.py:157
  8.3 0.0 copy-start.1
  8.3 0.0 copy-start.3
  8.3 2.1 %collective-permute-start.2 = (bf16[4,5,8,128]{3,2,1,0:T(8,128)(2,1)S(1)}, bf16[4,5,8,128]{3,2,1,0:T(8,128)(2,1)S(1)}, u32[]{:S(2)}, u32[]{:S(2)}) collective-permute-start(bf16[4,5,8,128]{3,2,1,0:T(8,128)(2,1)S(1)} %pad_maximum_fusion.1._), channel_id=1, source_target_pairs={{0,4},{1,5},{2,6},{3,7},{4,0},{5,1},{6,2},{7,3},{8,12},{9,13},{10,... | collective-permute-start | bytes 122888 | tf_op jit(solution)/shard_map/ppermute | solution.py:460
  10.4 1.4 %row_adjoint.1.rt_ref = bf16[24,256,128]{2,1,0:T(8,128)(2,1)S(1)} custom-call(f32[384,128]{1,0:T(8,128)S(1)} %get-tuple-element.10.taps, bf16[4,5,8,128]{3,2,1,0:T(8,128)(2,1)S(1)} %pad_maximum_fusion.1._), custom_call_target="tpu_custom_call" | custom-call | tf_op jit(solution)/shard_map/row_adjoint/pallas_call | solution.py:157
  11.8 0.6 %collective-permute-done.2 = bf16[4,5,8,128]{3,2,1,0:T(8,128)(2,1)S(1)} collective-permute-done((bf16[4,5,8,128]{3,2,1,0:T(8,128)(2,1)S(1)}, bf16[4,5,8,128]{3,2,1,0:T(8,128)(2,1)S(1)}, u32[]{:S(2)}, u32[]{:S(2)}) %collective-permute-start.2) | collective-permute-done | bytes 40992 | tf_op jit(solution)/shard_map/ppermute | solution.py:460
  12.4 3.1 %collective-permute-start.3 = (bf16[8,5,8,128]{3,2,1,0:T(8,128)(2,1)S(1)}, bf16[8,5,8,128]{3,2,1,0:T(8,128)(2,1)S(1)}, u32[]{:S(2)}, u32[]{:S(2)}) collective-permute-start(bf16[8,5,8,128]{3,2,1,0:T(8,128)(2,1)S(1)} %pad_maximum_fusion._), channel_id=1, source_target_pairs={{0,8},{1,9},{2,10},{3,11},{4,12},{5,13},{6,14},{7,15},{8,0},{9,1},... | collective-permute-start | bytes 245768 | tf_op jit(solution)/shard_map/ppermute | solution.py:460
  15.5 1.8 %column_adjoint.1.ca_ref = bf16[48,256,128]{2,1,0:T(8,128)(2,1)S(1)} custom-call(f32[384,128]{1,0:T(8,128)S(1)} %get-tuple-element.10.taps, bf16[8,5,8,128]{3,2,1,0:T(8,128)(2,1)S(1)} %pad_maximum_fusion._), custom_call_target="tpu_custom_call" | custom-call | tf_op jit(solution)/shard_map/column_adjoint/pallas_call | solution.py:157
  17.3 0.6 %collective-permute-done.3 = bf16[8,5,8,128]{3,2,1,0:T(8,128)(2,1)S(1)} collective-permute-done((bf16[8,5,8,128]{3,2,1,0:T(8,128)(2,1)S(1)}, bf16[8,5,8,128]{3,2,1,0:T(8,128)(2,1)S(1)}, u32[]{:S(2)}, u32[]{:S(2)}) %collective-permute-start.3) | collective-permute-done | bytes 81952 | tf_op jit(solution)/shard_map/ppermute | solution.py:460
  17.9 0.0 copy-start
  18.0 17.6 %imaging.1 = (f32[64,256]{1,0:T(8,128)}, f32[16,4,8,128]{3,2,1,0:T(8,128)S(1)}) custom-call(f32[12]{0:T(128)S(1)} %copy-done.3, bf16[80,8,128]{2,1,0:T(8,128)(2,1)S(1)} %bitcast.5, bf16[64,256]{1,0:T(8,128)(2,1)S(1)} %copy-done.1, bf16[6144,128]{1,0:T(8,128)(2,1)S(1)} %get-tuple-element.9.r_ref, bf16[24,256,128]{2,1,0:T(8,128)(2,1)S(1)} %row_adjoint.1.rt_ref, ...), custom_call_target="tpu_custom_call" | custom-call | tf_op jit(solution)/shard_map/imaging/pallas_call | solution.py:383
  35.5 0.1 collective-permute-start.4
  35.6 1.3 %collective-permute-done.4 = f32[8,4,8,128]{3,2,1,0:T(8,128)S(1)} collective-permute-done((f32[8,4,8,128]{3,2,1,0:T(8,128)S(1)}, f32[8,4,8,128]{3,2,1,0:T(8,128)S(1)}, u32[]{:S(2)}, u32[]{:S(2)}) %collective-permute-start.4) | collective-permute-done | bytes 131104 | tf_op jit(solution)/shard_map/ppermute | solution.py:460
  37.0 1.9 %collective-permute-start.5 = (f32[4,4,8,128]{3,2,1,0:T(8,128)S(1)}, f32[4,4,8,128]{3,2,1,0:T(8,128)S(1)}, u32[]{:S(2)}, u32[]{:S(2)}) collective-permute-start(f32[4,4,8,128]{3,2,1,0:T(8,128)S(1)} %slice.29), channel_id=1, source_target_pairs={{0,2},{1,3},{2,0},{3,1},{4,6},{5,7},{6,4},{7,5},{8,10},{9,11},{10,... | collective-permute-start | bytes 196616 | tf_op jit(solution)/shard_map/ppermute | solution.py:460
  38.9 2.4 %collective-permute-done.5 = f32[4,4,8,128]{3,2,1,0:T(8,128)S(1)} collective-permute-done((f32[4,4,8,128]{3,2,1,0:T(8,128)S(1)}, f32[4,4,8,128]{3,2,1,0:T(8,128)S(1)}, u32[]{:S(2)}, u32[]{:S(2)}) %collective-permute-start.5) | collective-permute-done | bytes 65568 | tf_op jit(solution)/shard_map/ppermute | solution.py:460
  41.3 2.0 %collective-permute-start.6 = (f32[2,4,8,128]{3,2,1,0:T(8,128)S(1)}, f32[2,4,8,128]{3,2,1,0:T(8,128)S(1)}, u32[]{:S(2)}, u32[]{:S(2)}) collective-permute-start(f32[2,4,8,128]{3,2,1,0:T(8,128)S(1)} %slice.31), channel_id=1, source_target_pairs={{0,4},{1,5},{2,6},{3,7},{4,0},{5,1},{6,2},{7,3},{8,12},{9,13},{10,... | collective-permute-start | bytes 98312 | tf_op jit(solution)/shard_map/ppermute | solution.py:460
  43.3 2.0 %collective-permute-done.6 = f32[2,4,8,128]{3,2,1,0:T(8,128)S(1)} collective-permute-done((f32[2,4,8,128]{3,2,1,0:T(8,128)S(1)}, f32[2,4,8,128]{3,2,1,0:T(8,128)S(1)}, u32[]{:S(2)}, u32[]{:S(2)}) %collective-permute-start.6) | collective-permute-done | bytes 32800 | tf_op jit(solution)/shard_map/ppermute | solution.py:460
  45.3 3.3 %collective-permute-start.7 = (f32[1,4,8,128]{3,2,1,0:T(8,128)S(1)}, f32[1,4,8,128]{3,2,1,0:T(8,128)S(1)}, u32[]{:S(2)}, u32[]{:S(2)}) collective-permute-start(f32[1,4,8,128]{3,2,1,0:T(8,128)S(1)} %slice.32), channel_id=1, source_target_pairs={{0,8},{1,9},{2,10},{3,11},{4,12},{5,13},{6,14},{7,15},{8,0},{9,1},... | collective-permute-start | bytes 49160 | tf_op jit(solution)/shard_map/ppermute | solution.py:460
  48.6 1.7 %collective-permute-done.7.sent_ref = f32[1,4,8,128]{3,2,1,0:T(8,128)S(1)} collective-permute-done((f32[1,4,8,128]{3,2,1,0:T(8,128)S(1)}, f32[1,4,8,128]{3,2,1,0:T(8,128)S(1)}, u32[]{:S(2)}, u32[]{:S(2)}) %collective-permute-start.7) | collective-permute-done | bytes 16416 | tf_op jit(solution)/shard_map/ppermute | solution.py:460
  50.4 0.6 %update.1 = (f32[4,1024]{1,0:T(4,128)}, f32[4,1024]{1,0:T(4,128)}) custom-call(f32[2,4,8,128]{3,2,1,0:T(8,128)S(1)} %slice_add_fusion.2.kept_ref, f32[1,4,8,128]{3,2,1,0:T(8,128)S(1)} %collective-permute-done.7.sent_ref, f32[4,1024]{1,0:T(4,128)S(1)} %copy-done.2, f32[4,1024]{1,0:T(4,128)S(1)} %copy-done), custom_call_target="tpu_custom_call" | custom-call | tf_op jit(solution)/shard_map/update/pallas_call | solution.py:448
  (22 shorter events, 0.1 us)
Async XLA Ops:
  1.4 2.5 %collective-permute-start = (bf16[1,5,8,128]{3,2,1,0:T(8,128)(2,1)S(1)}, bf16[1,5,8,128]{3,2,1,0:T(8,128)(2,1)S(1)}, u32[]{:S(2)}, u32[]{:S(2)}) collective-permute-start(bf16[1,5,8,128]{3,2,1,0:T(8,128)(2,1)S(1)} %pack.1), channel_id=1, source_target_pairs={{0,1},{1,0},{2,3},{3,2},{4,5},{5,4},{6,7},{7,6},{8,9},{9,8},{10,11... | collective-permute-start | bytes 30728 | tf_op jit(solution)/shard_map/ppermute | solution.py:460
  3.9 4.4 %collective-permute-start.1 = (bf16[2,5,8,128]{3,2,1,0:T(8,128)(2,1)S(1)}, bf16[2,5,8,128]{3,2,1,0:T(8,128)(2,1)S(1)}, u32[]{:S(2)}, u32[]{:S(2)}) collective-permute-start(bf16[2,5,8,128]{3,2,1,0:T(8,128)(2,1)S(1)} %pad_maximum_fusion.2._), channel_id=1, source_target_pairs={{0,2},{1,3},{2,0},{3,1},{4,6},{5,7},{6,4},{7,5},{8,10},{9,11},{10,... | collective-permute-start | bytes 61448 | tf_op jit(solution)/shard_map/ppermute | solution.py:460
  8.3 9.7 %copy-start.1 = (bf16[64,256]{1,0:T(8,128)(2,1)S(1)}, bf16[64,256]{1,0:T(8,128)(2,1)}, u32[]{:S(2)}) copy-start(bf16[64,256]{1,0:T(8,128)(2,1)} %target_ref.1) | copy-start | bytes 98308
  8.3 9.7 %copy-start.3 = (f32[12]{0:T(128)S(1)}, f32[12]{0:T(128)}, u32[]{:S(2)}) copy-start(f32[12]{0:T(128)} %weight_ref.1) | copy-start | bytes 148
  8.3 4.1 %collective-permute-start.2 = (bf16[4,5,8,128]{3,2,1,0:T(8,128)(2,1)S(1)}, bf16[4,5,8,128]{3,2,1,0:T(8,128)(2,1)S(1)}, u32[]{:S(2)}, u32[]{:S(2)}) collective-permute-start(bf16[4,5,8,128]{3,2,1,0:T(8,128)(2,1)S(1)} %pad_maximum_fusion.1._), channel_id=1, source_target_pairs={{0,4},{1,5},{2,6},{3,7},{4,0},{5,1},{6,2},{7,3},{8,12},{9,13},{10,... | collective-permute-start | bytes 122888 | tf_op jit(solution)/shard_map/ppermute | solution.py:460
  12.4 5.5 %collective-permute-start.3 = (bf16[8,5,8,128]{3,2,1,0:T(8,128)(2,1)S(1)}, bf16[8,5,8,128]{3,2,1,0:T(8,128)(2,1)S(1)}, u32[]{:S(2)}, u32[]{:S(2)}) collective-permute-start(bf16[8,5,8,128]{3,2,1,0:T(8,128)(2,1)S(1)} %pad_maximum_fusion._), channel_id=1, source_target_pairs={{0,8},{1,9},{2,10},{3,11},{4,12},{5,13},{6,14},{7,15},{8,0},{9,1},... | collective-permute-start | bytes 245768 | tf_op jit(solution)/shard_map/ppermute | solution.py:460
  17.9 32.4 %copy-start = (f32[4,1024]{1,0:T(4,128)S(1)}, f32[4,1024]{1,0:T(4,128)}, u32[]{:S(2)}) copy-start(f32[4,1024]{1,0:T(4,128)} %masters_ref.3) | copy-start | bytes 49156
  17.9 32.4 %copy-start.2 = (f32[4,1024]{1,0:T(4,128)S(1)}, f32[4,1024]{1,0:T(4,128)}, u32[]{:S(2)}) copy-start(f32[4,1024]{1,0:T(4,128)} %velocity_ref.1) | copy-start | bytes 49156
  35.5 1.4 %collective-permute-start.4 = (f32[8,4,8,128]{3,2,1,0:T(8,128)S(1)}, f32[8,4,8,128]{3,2,1,0:T(8,128)S(1)}, u32[]{:S(2)}, u32[]{:S(2)}) collective-permute-start(f32[8,4,8,128]{3,2,1,0:T(8,128)S(1)} %slice.22), channel_id=1, source_target_pairs={{0,1},{1,0},{2,3},{3,2},{4,5},{5,4},{6,7},{7,6},{8,9},{9,8},{10,11... | collective-permute-start | bytes 393224 | tf_op jit(solution)/shard_map/ppermute | solution.py:460
  37.0 4.3 %collective-permute-start.5 = (f32[4,4,8,128]{3,2,1,0:T(8,128)S(1)}, f32[4,4,8,128]{3,2,1,0:T(8,128)S(1)}, u32[]{:S(2)}, u32[]{:S(2)}) collective-permute-start(f32[4,4,8,128]{3,2,1,0:T(8,128)S(1)} %slice.29), channel_id=1, source_target_pairs={{0,2},{1,3},{2,0},{3,1},{4,6},{5,7},{6,4},{7,5},{8,10},{9,11},{10,... | collective-permute-start | bytes 196616 | tf_op jit(solution)/shard_map/ppermute | solution.py:460
  41.3 4.0 %collective-permute-start.6 = (f32[2,4,8,128]{3,2,1,0:T(8,128)S(1)}, f32[2,4,8,128]{3,2,1,0:T(8,128)S(1)}, u32[]{:S(2)}, u32[]{:S(2)}) collective-permute-start(f32[2,4,8,128]{3,2,1,0:T(8,128)S(1)} %slice.31), channel_id=1, source_target_pairs={{0,4},{1,5},{2,6},{3,7},{4,0},{5,1},{6,2},{7,3},{8,12},{9,13},{10,... | collective-permute-start | bytes 98312 | tf_op jit(solution)/shard_map/ppermute | solution.py:460
  45.3 5.0 %collective-permute-start.7 = (f32[1,4,8,128]{3,2,1,0:T(8,128)S(1)}, f32[1,4,8,128]{3,2,1,0:T(8,128)S(1)}, u32[]{:S(2)}, u32[]{:S(2)}) collective-permute-start(f32[1,4,8,128]{3,2,1,0:T(8,128)S(1)} %slice.32), channel_id=1, source_target_pairs={{0,8},{1,9},{2,10},{3,11},{4,12},{5,13},{6,14},{7,15},{8,0},{9,1},... | collective-permute-start | bytes 49160 | tf_op jit(solution)/shard_map/ppermute | solution.py:460

commit v4 on v3

--- a/solution.py
+++ b/solution.py
@@ -15,10 +15,12 @@
 CH = 2 * TERMS
 LANES = 128
 BLK = 64
+STEP = 32
 NBLK = W // BLK
 EXT = 128
 PAD = 40
 CROWS = 72
+GROWS = 2 * PAD + EXT
 
 steepness = 0.5
 threshold = 8.0
@@ -174,6 +176,10 @@
     return [r, built[1], built[0], built[2]]
 
 
+def reversed_bits(value, bits):
+    return sum(((value >> b) & 1) << (bits - 1 - b) for b in range(bits))
+
+
 def main_kernel(
     devices,
     weight_ref,
@@ -185,78 +191,108 @@
     ca_ref,
     resid_ref,
     grads_ref,
-    canvas_own,
-    canvas_above,
-    canvas_below,
-    window,
-    fields,
-    gys,
-    grad,
-    acc_own,
-    acc_above,
-    acc_below,
-    table,
-    ids,
-    sem,
+    *scratch,
 ):
+    canvases = (scratch[0:4], scratch[4:8], scratch[8:12])
+    grads = scratch[12:16]
+    sums = scratch[16:19]
+    window, lhs, fields, slope, gw, gys, table, ids, sem = scratch[19:]
     slabs = gathered_ref.shape[0] // devices
     count = slabs - 1
     places = LANES
     rows = BLK
     me = lax.axis_index("tx")
     bits = devices.bit_length() - 1
+    bases = (PAD + HALF, PAD + HALF - rows, PAD + HALF + rows)
     for n, (other, missing) in enumerate(
         ((me, 0), (jnp.maximum(me - 1, 0), 0), (jnp.minimum(me + 1, devices - 1), BLK - MS))
     ):
         slab = gathered_ref[(other ^ me) * slabs + count].astype(jnp.float32).astype(jnp.int32)
-        owner, local = slab[0:1] ^ me, slab[1:2]
-        turned = sum(((owner >> b) & 1) << (bits - 1 - b) for b in range(bits))
-        table[n, 0:1, :] = owner * slabs + local
-        table[n, 1:2, :] = turned * count + local
-        row = slab[2:3]
-        table[n, 2:3, :] = row if n == 0 else jnp.where(other == me, missing, row)
-        table[n, 3:4, :] = slab[3:4]
+        owner, local, row, col = slab[0:1] ^ me, slab[1:2], slab[2:3], slab[3:4]
+        if n:
+            row = jnp.where(other == me, missing, row)
+        lines = jnp.concatenate(
+            [
+                owner * slabs + local,
+                reversed_bits(owner, bits) * count + local,
+                ((col + HALF) >> 7) * CROWS + row + 7,
+                (col + HALF) & 127,
+                (col >> 7) * GROWS + row + bases[n],
+                col & 127,
+                (LANES - (col & 127)) & 127,
+                row,
+            ],
+            axis=0,
+        )
+        for j in range(places // STEP):
+            table[j, 8 * n : 8 * n + 8, :] = (
+                pltpu.roll(lines, LANES - STEP * j, 1) if j else lines
+            )[:, :STEP]
     to_scalar = pltpu.make_async_copy(table, ids, sem)
     to_scalar.start()
-    canvases = ((0, canvas_own), (1, canvas_above), (2, canvas_below))
-    for _, canvas in canvases:
-        canvas[...] = jnp.zeros_like(canvas)
+    for group in canvases:
+        for canvas in group:
+            canvas[...] = jnp.zeros_like(canvas)
+    for acc in sums:
+        acc[...] = jnp.zeros_like(acc)
     lanes8 = lane_iota((8, LANES))
     to_scalar.wait()
 
-    def place(q, carry):
-        for n, canvas in canvases:
-            master = gathered_ref[ids[n, 0, q]].astype(jnp.float32)
-            top = ids[n, 2, q] + 7
-            col = ids[n, 3, q] + HALF
-            side = col >> 7
-            shift = col & 127
-            for k in range(4):
-                moved = pltpu.roll(master, (shift + LANES - 32 * k) & 127, 1)
-                here = (lanes8 >= shift) & (lanes8 < shift + MS)
-                after = lanes8 < shift + MS - LANES
-                at = pl.ds(top + k, 8, stride=4)
-                canvas[side, at, :] += jnp.where(here, moved, 0.0)
-                canvas[side + 1, at, :] += jnp.where(after, moved, 0.0)
-        return carry
-
-    lax.fori_loop(0, places, place, 0, unroll=8)
-
-    sides = []
-    for h in range(3):
-        a, o, b = canvas_above[h], canvas_own[h], canvas_below[h]
-        sides.append(
+    def place(j, u):
+        for n, group in enumerate(canvases):
+            at, shift = ids[j, 8 * n + 2, u], ids[j, 8 * n + 3, u]
+            moved = pltpu.roll(gathered_ref[ids[j, 8 * n, u]].astype(jnp.float32), shift, 1)
+            ahead = lanes8 - shift
+            here = ahead >= 0
+            nth = (ahead & 127) >> 5
+            near, far = jnp.where(here, moved, 0.0), jnp.where(here, 0.0, moved)
+            for k, canvas in enumerate(group):
+                spot = pl.ds(at + k, 8, stride=4)
+                spot_far = pl.ds(at + k + CROWS, 8, stride=4)
+                mine = nth == k
+                old, old_far = canvas[spot, :], canvas[spot_far, :]
+                canvas[spot, :] = old + jnp.where(mine, near, 0.0)
+                canvas[spot_far, :] = old_far + jnp.where(mine, far, 0.0)
+
+    @pl.loop(0, places // STEP)
+    def _(j):
+        for u in range(STEP):
+            place(j, u)
+
+
+    lanes_ext = lane_iota((EXT, LANES))
+    parts = [
+        [
             jnp.concatenate(
-                [a[40:64], a[64:72] + o[0:8], o[8:64], o[64:72] + b[0:8], b[8:40]], axis=0
+                [
+                    above[h * CROWS + 40 : h * CROWS + 64],
+                    above[h * CROWS + 64 : (h + 1) * CROWS] + own[h * CROWS : h * CROWS + 8],
+                    own[h * CROWS + 8 : h * CROWS + 64],
+                    own[h * CROWS + 64 : (h + 1) * CROWS] + below[h * CROWS : h * CROWS + 8],
+                    below[h * CROWS + 8 : h * CROWS + 40],
+                ],
+                axis=0,
             )
-        )
-    low = lane_iota((EXT, LANES)) < BLK
-    turned = [pltpu.roll(s, BLK, 1) for s in sides]
+            for h in range(3)
+        ]
+        for own, above, below in zip(*canvases)
+    ]
+    sides = [parts[0][h] for h in range(3)]
+    for k in range(1, 4):
+        back = [pltpu.roll(part, LANES - MS * k, 1) for part in parts[k]]
+        for h in range(3):
+            after = back[h + 1] if h < 2 else 0.0
+            sides[h] = sides[h] + jnp.where(lanes_ext < LANES - MS * k, back[h], after)
+    low = lanes_ext < BLK
+    turned = [pltpu.roll(side, BLK, 1) for side in sides]
     window[:, 0:128] = sides[0].astype(jnp.bfloat16)
     window[:, 128:256] = jnp.where(low, turned[0], turned[1]).astype(jnp.bfloat16)
     window[:, 256:384] = sides[1].astype(jnp.bfloat16)
     window[:, 384:512] = jnp.where(low, turned[1], turned[2]).astype(jnp.bfloat16)
 
+    lanes16 = lane_iota((16, LANES))
+    before = lanes16 < HALF
+    until = lanes16 < HALF + BLK
     intensity = jnp.zeros((NBLK * rows, LANES), jnp.float32)
     for k in range(MODES):
         field_y = jnp.dot(
@@ -264,122 +300,115 @@
             window[...],
             preferred_element_type=jnp.float32,
         ).astype(jnp.bfloat16)
-        lhs = jnp.concatenate(
-            [
-                jnp.concatenate(
-                    [
-                        field_y[c * rows : (c + 1) * rows, b * LANES : (b + 1) * LANES]
-                        for c in range(CH)
-                    ],
-                    axis=1,
-                )
-                for b in range(NBLK)
-            ],
-            axis=0,
-        )
+        for c in range(CH):
+            for b in range(NBLK):
+                lhs[k % 2, b * rows : (b + 1) * rows, c * LANES : (c + 1) * LANES] = field_y[
+                    c * rows : (c + 1) * rows, b * LANES : (b + 1) * LANES
+                ]
         e = jnp.dot(
-            lhs,
+            lhs[k % 2],
             jnp.concatenate([cf_ref[2 * k], cf_ref[2 * k + 1]], axis=0),
             preferred_element_type=jnp.float32,
         )
         fields[k] = e
         intensity = intensity + weight_ref[k] * (e * e)
-    intensity = intensity + pltpu.roll(intensity, BLK, 1)
     low_rows = lane_iota((rows, LANES)) < BLK
-    goal = []
-    for h in range(2):
-        t = target_ref[:, h * LANES : (h + 1) * LANES].astype(jnp.float32)
+    resids = []
+    for b in range(NBLK):
+        inten = intensity[b * rows : (b + 1) * rows]
+        inten = inten + pltpu.roll(inten, BLK, 1)
+        t = target_ref[:, (b // 2) * LANES : (b // 2 + 1) * LANES].astype(jnp.float32)
         other = pltpu.roll(t, BLK, 1)
-        goal += [jnp.where(low_rows, t, other), jnp.where(low_rows, other, t)]
-    resist = jax.nn.sigmoid(steepness * (intensity - threshold))
-    resid = resist - jnp.concatenate(goal, axis=0)
-    for h in range(2):
-        first = resid[2 * h * rows : (2 * h + 1) * rows]
-        second = resid[(2 * h + 1) * rows : (2 * h + 2) * rows]
-        resid_ref[:, h * LANES : (h + 1) * LANES] = jnp.where(low_rows, first, second)
-    grad_intensity = resid * steepness * resist * (1.0 - resist)
-
-    lanes = lane_iota((rows, LANES))
-    middle = (lanes >= HALF) & (lanes < HALF + BLK)
-    left = lanes < HALF
-    nothing = jnp.zeros((rows, LANES), jnp.float32)
+        goal = jnp.where(low_rows, t, other) if b % 2 == 0 else jnp.where(low_rows, other, t)
+        resist = jax.nn.sigmoid(steepness * (inten - threshold))
+        resid = resist - goal
+        slope[b * rows : (b + 1) * rows, :] = 2.0 * (resid * steepness * resist * (1.0 - resist))
+        if b % 2 == 0:
+            resid_ref[:, (b // 2) * LANES : (b // 2 + 1) * LANES] = resid
+        else:
+            resid_ref[:, (b // 2) * LANES + BLK : (b // 2 + 1) * LANES] = resid[:, BLK:]
+
+    nothing = jnp.zeros((16, LANES), jnp.float32)
     for k in range(MODES):
-        g = 2.0 * weight_ref[k] * grad_intensity * fields[k]
-        r31 = pltpu.roll(g, HALF, 1)
-        r95 = pltpu.roll(g, HALF + BLK, 1)
-
-        def part(v, b):
-            return v[b * rows : (b + 1) * rows] if 0 <= b < NBLK else nothing
-
-        parts = []
-        for b in range(NBLK):
-            re = jnp.where(
-                middle, part(r31, b), jnp.where(left, part(r95, b - 1), part(r95, b + 1))
-            )
-            im = jnp.where(
-                middle, part(r95, b), jnp.where(left, part(r31, b - 1), part(r31, b + 1))
-            )
-            parts.append(jnp.concatenate([re, im], axis=1))
-        gw = jnp.concatenate(parts, axis=0).astype(jnp.bfloat16)
+        weight = weight_ref[k]
+        for i in range(0, rows, 16):
+            r31, r95 = [nothing], [nothing]
+            for b in range(NBLK):
+                at = slice(b * rows + i, b * rows + i + 16)
+                g = weight * slope[at, :] * fields[k, at, :]
+                r31.append(pltpu.roll(g, HALF, 1))
+                r95.append(pltpu.roll(g, HALF + BLK, 1))
+            r31.append(nothing)
+            r95.append(nothing)
+            for b in range(NBLK):
+                at = slice(b * rows + i, b * rows + i + 16)
+                re = jnp.where(before, r95[b], jnp.where(until, r31[b + 1], r95[b + 2]))
+                im = jnp.where(before, r31[b], jnp.where(until, r95[b + 1], r31[b + 2]))
+                gw[k % 2, at, :LANES] = re.astype(jnp.bfloat16)
+                gw[k % 2, at, LANES:] = im.astype(jnp.bfloat16)
         for t in range(TERMS):
             gy = jnp.dot(
-                gw, ca_ref[k * TERMS + t], preferred_element_type=jnp.float32
+                gw[k % 2], ca_ref[k * TERMS + t], preferred_element_type=jnp.float32
             ).astype(jnp.bfloat16)
             at = (k * TERMS + t) * rows
             for b in range(NBLK):
                 gys[at : at + rows, b * LANES : (b + 1) * LANES] = gy[b * rows : (b + 1) * rows]
 
     total = jnp.zeros((2 * EXT, NBLK * LANES), jnp.float32)
-    for n in range(2 * MODES):
+    for k in range(MODES):
         total = total + jnp.dot(
-            rt_ref[n], gys[n * LANES : (n + 1) * LANES, :], preferred_element_type=jnp.float32
+            jnp.concatenate([rt_ref[2 * k], rt_ref[2 * k + 1]], axis=1),
+            gys[2 * k * LANES : 2 * (k + 1) * LANES, :],
+            preferred_element_type=jnp.float32,
         )
-    zeros = jnp.zeros((PAD, LANES), jnp.float32)
+    whole = []
     for h in range(2):
         v0 = total[:EXT, 2 * h * LANES : (2 * h + 1) * LANES]
         v1 = total[:EXT, (2 * h + 1) * LANES : (2 * h + 2) * LANES]
         u0 = total[EXT:, 2 * h * LANES : (2 * h + 1) * LANES]
         u1 = total[EXT:, (2 * h + 1) * LANES : (2 * h + 2) * LANES]
-        grad[h, PAD : PAD + EXT, :] = jnp.where(
-            low, v0 + pltpu.roll(u0, BLK, 1), pltpu.roll(v1, BLK, 1) + u1
+        whole.append(
+            jnp.where(low, v0 + pltpu.roll(u0, BLK, 1), pltpu.roll(v1, BLK, 1) + u1)
         )
-        grad[h, :PAD, :] = zeros
-        grad[h, PAD + EXT :, :] = zeros
-
-    sums = (
-        (0, acc_own, PAD + HALF),
-        (1, acc_above, PAD + HALF - rows),
-        (2, acc_below, PAD + HALF + rows),
-    )
-    for _, acc, _ in sums:
-        acc[...] = jnp.zeros_like(acc)
-
-    def gather(q, carry):
-        for n, acc, base in sums:
-            m = ids[n, 1, q]
-            top = ids[n, 2, q] + base
-            col = ids[n, 3, q]
-            side = col >> 7
-            after = jnp.minimum(side + 1, 1)
-            shift = col & 127
-            patch = jnp.zeros((8, LANES), jnp.float32)
-            for k in range(4):
-                at = pl.ds(top + k, 8, stride=4)
-                both = jnp.where(lanes8 >= shift, grad[side, at, :], grad[after, at, :])
-                moved = pltpu.roll(both, (LANES + 32 * k - shift) & 127, 1)
-                patch = jnp.where((lanes8 >= 32 * k) & (lanes8 < 32 * k + MS), moved, patch)
-            acc[m] += patch
-        return carry
-
-    lax.fori_loop(0, places, gather, 0, unroll=8)
-    grads_ref[...] = (acc_own[...] + acc_above[...] + acc_below[...]).reshape(grads_ref.shape)
+    zeros = jnp.zeros((PAD, LANES), jnp.float32)
+    for k, grad in enumerate(grads):
+        ahead = [pltpu.roll(side, MS * k, 1) if k else side for side in whole]
+        for h in range(3):
+            here = ahead[h] if h < 2 else 0.0
+            behind = ahead[h - 1] if h else 0.0
+            base = h * GROWS
+            grad[base : base + PAD, :] = zeros
+            grad[base + PAD : base + PAD + EXT, :] = jnp.where(lanes_ext >= MS * k, here, behind)
+            grad[base + PAD + EXT : base + GROWS, :] = zeros
+
+    def gather(j, u):
+        for n, acc in enumerate(sums):
+            m, at, shift, back = [ids[j, 8 * n + line, u] for line in (1, 4, 5, 6)]
+            ahead = lanes8 - shift
+            here = ahead >= 0
+            nth = ahead & 127
+            patch = None
+            for k, grad in enumerate(grads):
+                both = jnp.where(
+                    here,
+                    grad[pl.ds(at + k, 8, stride=4), :],
+                    grad[pl.ds(at + k + GROWS, 8, stride=4), :],
+                )
+                patch = jnp.where(nth >= MS * k, both, patch) if k else both
+            acc[m] += pltpu.roll(patch, back, 1)
+
+    @pl.loop(0, places // STEP)
+    def _(j):
+        for u in range(STEP):
+            gather(j, u)
+
+    grads_ref[...] = (sums[0][...] + sums[1][...] + sums[2][...]).reshape(grads_ref.shape)
 
 
 def main_step(weights, gathered, target, bands):
     devices, slabs = gathered.shape[:2]
     count = slabs - 1
     vmem = pl.BlockSpec(memory_space=pltpu.VMEM)
-    accumulator = pltpu.VMEM((devices * count, 8, LANES), jnp.float32)
     return pl.pallas_call(
         functools.partial(main_kernel, devices),
         out_shape=(
@@ -389,18 +418,17 @@
         in_specs=[pl.BlockSpec(memory_space=pltpu.SMEM)] + [vmem] * 6,
         out_specs=[vmem] * 2,
         scratch_shapes=[
-            pltpu.VMEM((3, CROWS, LANES), jnp.float32),
-            pltpu.VMEM((3, CROWS, LANES), jnp.float32),
-            pltpu.VMEM((3, CROWS, LANES), jnp.float32),
+            *[pltpu.VMEM((3 * CROWS, LANES), jnp.float32)] * 12,
+            *[pltpu.VMEM((3 * GROWS, LANES), jnp.float32)] * 4,
+            *[pltpu.VMEM((devices * count, 8, LANES), jnp.float32)] * 3,
             pltpu.VMEM((EXT, NBLK * LANES), jnp.bfloat16),
+            pltpu.VMEM((2, NBLK * BLK, CH * LANES), jnp.bfloat16),
             pltpu.VMEM((MODES, NBLK * BLK, LANES), jnp.float32),
+            pltpu.VMEM((NBLK * BLK, LANES), jnp.float32),
+            pltpu.VMEM((2, NBLK * BLK, 2 * LANES), jnp.bfloat16),
             pltpu.VMEM((MODES * TERMS * BLK, NBLK * LANES), jnp.bfloat16),
-            pltpu.VMEM((2, 2 * PAD + EXT, LANES), jnp.float32),
-            accumulator,
-            accumulator,
-            accumulator,
-            pltpu.VMEM((3, 8, LANES), jnp.int32),
-            pltpu.SMEM((3, 8, LANES), jnp.int32),
+            pltpu.VMEM((LANES // STEP, 24, STEP), jnp.int32),
+            pltpu.SMEM((LANES // STEP, 24, STEP), jnp.int32),
             pltpu.SemaphoreType.DMA,
         ],
         compiler_params=pltpu.CompilerParams(vmem_limit_bytes=24 << 20),

time: 51.2 us -> 47.9 us (0.936)
  Pallas kernels: 25.7 us -> 22.4 us
    pallas_call x1, Pallas kernels: 17.6 us -> 14.2 us  [main_step(): pl.pallas_call(functools.partial(main_kernel, devices), out_shape=(jax.Sh...]
  transfers between devices with their start and end apart: 8 -> 8, of which waited for: 6 -> 6; matrix products, arithmetic and copies ran while one was open for 0% -> 0% of each run, Pallas kernels for 13% -> 14%
where the time goes in v4:
time: 47.9 us; the launch traced here: 47.7 us
  Pallas kernels  22.4 us (47%)
  starting transfers between devices  15.5 us (32%)
  waiting for transfers between devices  8.73 us (18%)
  between operations  0.81 us (2%)
    ppermute x8, starting transfers between devices, swap(): return lax.ppermute(value, 'tx', [(i, i ^ bit) for i in range(devices)])  15.5 us
    pallas_call x1, Pallas kernels, main_step(): pl.pallas_call(functools.partial(main_kernel, devices), out_shape=(jax.Sh...  14.2 us
    ppermute x8, waiting for transfers between devices, swap(): return lax.ppermute(value, 'tx', [(i, i ^ bit) for i in range(devices)])  8.73 us
    pallas_call x3, Pallas kernels, build_bands(): pl.pallas_call(kernel, out_shape=pltpu.VMEM(shape, jnp.bfloat16), in_spec...  4.91 us
    pallas_call x1, Pallas kernels, build_bands(): pl.pallas_call(row_bands_kernel, out_shape=(pltpu.VMEM((MODES * CH * BLK,...  1.89 us
  transfers between devices with their start and end apart: 8, of which 6 were waited for; matrix products, arithmetic and copies ran while one was open for 0% of the time, Pallas kernels for 14%

profile of v4, /device:TPU:0, one launch (start us, length us, event | category | flops | bytes accessed | tf_op | source)
XLA Modules:
  0.0 47.7 jit_solution(11230084566981737998)
XLA Ops:
  0.6 0.8 %pack.1 = bf16[1,5,8,128]{3,2,1,0:T(8,128)(2,1)S(1)} custom-call(f32[4,1024]{1,0:T(4,128)} %masters_ref.3, s32[1,128]{1,0:T(1,128)} %bitcast.6, s32[1,128]{1,0:T(1,128)} %bitcast.7, s32[1,128]{1,0:T(1,128)} %bitcast.8, s32[1,128]{1,0:T(1,128)} %bitcast.9), custom_call_target="tpu_custom_call" | custom-call | tf_op jit(solution)/shard_map/pack/pallas_call | solution.py:452
  1.4 0.6 %collective-permute-start = (bf16[1,5,8,128]{3,2,1,0:T(8,128)(2,1)S(1)}, bf16[1,5,8,128]{3,2,1,0:T(8,128)(2,1)S(1)}, u32[]{:S(2)}, u32[]{:S(2)}) collective-permute-start(bf16[1,5,8,128]{3,2,1,0:T(8,128)(2,1)S(1)} %pack.1), channel_id=1, source_target_pairs={{0,1},{1,0},{2,3},{3,2},{4,5},{5,4},{6,7},{7,6},{8,9},{9,8},{10,11... | collective-permute-start | bytes 30728 | tf_op jit(solution)/shard_map/ppermute | solution.py:488
  2.0 1.9 %row_bands.1 = (bf16[6144,128]{1,0:T(8,128)(2,1)S(1)}, f32[384,128]{1,0:T(8,128)S(1)}) custom-call(bf16[12,4,2,63]{3,2,1,0:T(2,128)(2,1)} %row_ref.1, bf16[12,4,2,63]{3,2,1,0:T(2,128)(2,1)} %col_ref.1), custom_call_target="tpu_custom_call" | custom-call | tf_op jit(solution)/shard_map/row_bands/pallas_call | solution.py:146
  3.9 2.6 %collective-permute-start.1 = (bf16[2,5,8,128]{3,2,1,0:T(8,128)(2,1)S(1)}, bf16[2,5,8,128]{3,2,1,0:T(8,128)(2,1)S(1)}, u32[]{:S(2)}, u32[]{:S(2)}) collective-permute-start(bf16[2,5,8,128]{3,2,1,0:T(8,128)(2,1)S(1)} %pad_maximum_fusion.2._), channel_id=1, source_target_pairs={{0,2},{1,3},{2,0},{3,1},{4,6},{5,7},{6,4},{7,5},{8,10},{9,11},{10,... | collective-permute-start | bytes 61448 | tf_op jit(solution)/shard_map/ppermute | solution.py:488
  6.5 1.8 %column_bands.1.cf_ref = bf16[24,512,128]{2,1,0:T(8,128)(2,1)S(1)} custom-call(f32[384,128]{1,0:T(8,128)S(1)} %get-tuple-element.10.taps, bf16[2,5,8,128]{3,2,1,0:T(8,128)(2,1)S(1)} %pad_maximum_fusion.2._), custom_call_target="tpu_custom_call" | custom-call | tf_op jit(solution)/shard_map/column_bands/pallas_call | solution.py:159
  8.3 0.0 copy-start.1
  8.3 0.0 copy-start.3
  8.3 2.1 %collective-permute-start.2 = (bf16[4,5,8,128]{3,2,1,0:T(8,128)(2,1)S(1)}, bf16[4,5,8,128]{3,2,1,0:T(8,128)(2,1)S(1)}, u32[]{:S(2)}, u32[]{:S(2)}) collective-permute-start(bf16[4,5,8,128]{3,2,1,0:T(8,128)(2,1)S(1)} %pad_maximum_fusion.1._), channel_id=1, source_target_pairs={{0,4},{1,5},{2,6},{3,7},{4,0},{5,1},{6,2},{7,3},{8,12},{9,13},{10,... | collective-permute-start | bytes 122888 | tf_op jit(solution)/shard_map/ppermute | solution.py:488
  10.4 1.4 %row_adjoint.1.rt_ref = bf16[24,256,128]{2,1,0:T(8,128)(2,1)S(1)} custom-call(f32[384,128]{1,0:T(8,128)S(1)} %get-tuple-element.10.taps, bf16[4,5,8,128]{3,2,1,0:T(8,128)(2,1)S(1)} %pad_maximum_fusion.1._), custom_call_target="tpu_custom_call" | custom-call | tf_op jit(solution)/shard_map/row_adjoint/pallas_call | solution.py:159
  11.8 0.6 %collective-permute-done.2 = bf16[4,5,8,128]{3,2,1,0:T(8,128)(2,1)S(1)} collective-permute-done((bf16[4,5,8,128]{3,2,1,0:T(8,128)(2,1)S(1)}, bf16[4,5,8,128]{3,2,1,0:T(8,128)(2,1)S(1)}, u32[]{:S(2)}, u32[]{:S(2)}) %collective-permute-start.2) | collective-permute-done | bytes 40992 | tf_op jit(solution)/shard_map/ppermute | solution.py:488
  12.4 3.1 %collective-permute-start.3 = (bf16[8,5,8,128]{3,2,1,0:T(8,128)(2,1)S(1)}, bf16[8,5,8,128]{3,2,1,0:T(8,128)(2,1)S(1)}, u32[]{:S(2)}, u32[]{:S(2)}) collective-permute-start(bf16[8,5,8,128]{3,2,1,0:T(8,128)(2,1)S(1)} %pad_maximum_fusion._), channel_id=1, source_target_pairs={{0,8},{1,9},{2,10},{3,11},{4,12},{5,13},{6,14},{7,15},{8,0},{9,1},... | collective-permute-start | bytes 245768 | tf_op jit(solution)/shard_map/ppermute | solution.py:488
  15.5 1.8 %column_adjoint.1.ca_ref = bf16[48,256,128]{2,1,0:T(8,128)(2,1)S(1)} custom-call(f32[384,128]{1,0:T(8,128)S(1)} %get-tuple-element.10.taps, bf16[8,5,8,128]{3,2,1,0:T(8,128)(2,1)S(1)} %pad_maximum_fusion._), custom_call_target="tpu_custom_call" | custom-call | tf_op jit(solution)/shard_map/column_adjoint/pallas_call | solution.py:159
  17.3 0.6 %collective-permute-done.3 = bf16[8,5,8,128]{3,2,1,0:T(8,128)(2,1)S(1)} collective-permute-done((bf16[8,5,8,128]{3,2,1,0:T(8,128)(2,1)S(1)}, bf16[8,5,8,128]{3,2,1,0:T(8,128)(2,1)S(1)}, u32[]{:S(2)}, u32[]{:S(2)}) %collective-permute-start.3) | collective-permute-done | bytes 81952 | tf_op jit(solution)/shard_map/ppermute | solution.py:488
  17.9 0.0 copy-start
  18.0 14.2 %imaging.1 = (f32[64,256]{1,0:T(8,128)}, f32[16,4,8,128]{3,2,1,0:T(8,128)S(1)}) custom-call(f32[12]{0:T(128)S(1)} %copy-done.3, bf16[80,8,128]{2,1,0:T(8,128)(2,1)S(1)} %bitcast.5, bf16[64,256]{1,0:T(8,128)(2,1)S(1)} %copy-done.1, bf16[6144,128]{1,0:T(8,128)(2,1)S(1)} %get-tuple-element.9.r_ref, bf16[24,256,128]{2,1,0:T(8,128)(2,1)S(1)} %row_adjoint.1.rt_ref, ...), custom_call_target="tpu_custom_call" | custom-call | tf_op jit(solution)/shard_map/imaging/pallas_call | solution.py:412
  32.2 0.1 collective-permute-start.4
  32.3 1.3 %collective-permute-done.4 = f32[8,4,8,128]{3,2,1,0:T(8,128)S(1)} collective-permute-done((f32[8,4,8,128]{3,2,1,0:T(8,128)S(1)}, f32[8,4,8,128]{3,2,1,0:T(8,128)S(1)}, u32[]{:S(2)}, u32[]{:S(2)}) %collective-permute-start.4) | collective-permute-done | bytes 131104 | tf_op jit(solution)/shard_map/ppermute | solution.py:488
  33.7 1.9 %collective-permute-start.5 = (f32[4,4,8,128]{3,2,1,0:T(8,128)S(1)}, f32[4,4,8,128]{3,2,1,0:T(8,128)S(1)}, u32[]{:S(2)}, u32[]{:S(2)}) collective-permute-start(f32[4,4,8,128]{3,2,1,0:T(8,128)S(1)} %slice.29), channel_id=1, source_target_pairs={{0,2},{1,3},{2,0},{3,1},{4,6},{5,7},{6,4},{7,5},{8,10},{9,11},{10,... | collective-permute-start | bytes 196616 | tf_op jit(solution)/shard_map/ppermute | solution.py:488
  35.6 2.4 %collective-permute-done.5 = f32[4,4,8,128]{3,2,1,0:T(8,128)S(1)} collective-permute-done((f32[4,4,8,128]{3,2,1,0:T(8,128)S(1)}, f32[4,4,8,128]{3,2,1,0:T(8,128)S(1)}, u32[]{:S(2)}, u32[]{:S(2)}) %collective-permute-start.5) | collective-permute-done | bytes 65568 | tf_op jit(solution)/shard_map/ppermute | solution.py:488
  38.0 2.0 %collective-permute-start.6 = (f32[2,4,8,128]{3,2,1,0:T(8,128)S(1)}, f32[2,4,8,128]{3,2,1,0:T(8,128)S(1)}, u32[]{:S(2)}, u32[]{:S(2)}) collective-permute-start(f32[2,4,8,128]{3,2,1,0:T(8,128)S(1)} %slice.31), channel_id=1, source_target_pairs={{0,4},{1,5},{2,6},{3,7},{4,0},{5,1},{6,2},{7,3},{8,12},{9,13},{10,... | collective-permute-start | bytes 98312 | tf_op jit(solution)/shard_map/ppermute | solution.py:488
  40.0 2.0 %collective-permute-done.6 = f32[2,4,8,128]{3,2,1,0:T(8,128)S(1)} collective-permute-done((f32[2,4,8,128]{3,2,1,0:T(8,128)S(1)}, f32[2,4,8,128]{3,2,1,0:T(8,128)S(1)}, u32[]{:S(2)}, u32[]{:S(2)}) %collective-permute-start.6) | collective-permute-done | bytes 32800 | tf_op jit(solution)/shard_map/ppermute | solution.py:488
  42.0 3.3 %collective-permute-start.7 = (f32[1,4,8,128]{3,2,1,0:T(8,128)S(1)}, f32[1,4,8,128]{3,2,1,0:T(8,128)S(1)}, u32[]{:S(2)}, u32[]{:S(2)}) collective-permute-start(f32[1,4,8,128]{3,2,1,0:T(8,128)S(1)} %slice.32), channel_id=1, source_target_pairs={{0,8},{1,9},{2,10},{3,11},{4,12},{5,13},{6,14},{7,15},{8,0},{9,1},... | collective-permute-start | bytes 49160 | tf_op jit(solution)/shard_map/ppermute | solution.py:488
  45.3 1.7 %collective-permute-done.7.sent_ref = f32[1,4,8,128]{3,2,1,0:T(8,128)S(1)} collective-permute-done((f32[1,4,8,128]{3,2,1,0:T(8,128)S(1)}, f32[1,4,8,128]{3,2,1,0:T(8,128)S(1)}, u32[]{:S(2)}, u32[]{:S(2)}) %collective-permute-start.7) | collective-permute-done | bytes 16416 | tf_op jit(solution)/shard_map/ppermute | solution.py:488
  47.0 0.6 %update.1 = (f32[4,1024]{1,0:T(4,128)}, f32[4,1024]{1,0:T(4,128)}) custom-call(f32[2,4,8,128]{3,2,1,0:T(8,128)S(1)} %slice_add_fusion.2.kept_ref, f32[1,4,8,128]{3,2,1,0:T(8,128)S(1)} %collective-permute-done.7.sent_ref, f32[4,1024]{1,0:T(4,128)S(1)} %copy-done.2, f32[4,1024]{1,0:T(4,128)S(1)} %copy-done), custom_call_target="tpu_custom_call" | custom-call | tf_op jit(solution)/shard_map/update/pallas_call | solution.py:476
  (22 shorter events, 0.1 us)
Async XLA Ops:
  1.4 2.5 %collective-permute-start = (bf16[1,5,8,128]{3,2,1,0:T(8,128)(2,1)S(1)}, bf16[1,5,8,128]{3,2,1,0:T(8,128)(2,1)S(1)}, u32[]{:S(2)}, u32[]{:S(2)}) collective-permute-start(bf16[1,5,8,128]{3,2,1,0:T(8,128)(2,1)S(1)} %pack.1), channel_id=1, source_target_pairs={{0,1},{1,0},{2,3},{3,2},{4,5},{5,4},{6,7},{7,6},{8,9},{9,8},{10,11... | collective-permute-start | bytes 30728 | tf_op jit(solution)/shard_map/ppermute | solution.py:488
  3.9 4.4 %collective-permute-start.1 = (bf16[2,5,8,128]{3,2,1,0:T(8,128)(2,1)S(1)}, bf16[2,5,8,128]{3,2,1,0:T(8,128)(2,1)S(1)}, u32[]{:S(2)}, u32[]{:S(2)}) collective-permute-start(bf16[2,5,8,128]{3,2,1,0:T(8,128)(2,1)S(1)} %pad_maximum_fusion.2._), channel_id=1, source_target_pairs={{0,2},{1,3},{2,0},{3,1},{4,6},{5,7},{6,4},{7,5},{8,10},{9,11},{10,... | collective-permute-start | bytes 61448 | tf_op jit(solution)/shard_map/ppermute | solution.py:488
  8.3 9.7 %copy-start.1 = (bf16[64,256]{1,0:T(8,128)(2,1)S(1)}, bf16[64,256]{1,0:T(8,128)(2,1)}, u32[]{:S(2)}) copy-start(bf16[64,256]{1,0:T(8,128)(2,1)} %target_ref.1) | copy-start | bytes 98308
  8.3 9.7 %copy-start.3 = (f32[12]{0:T(128)S(1)}, f32[12]{0:T(128)}, u32[]{:S(2)}) copy-start(f32[12]{0:T(128)} %weight_ref.1) | copy-start | bytes 148
  8.3 4.1 %collective-permute-start.2 = (bf16[4,5,8,128]{3,2,1,0:T(8,128)(2,1)S(1)}, bf16[4,5,8,128]{3,2,1,0:T(8,128)(2,1)S(1)}, u32[]{:S(2)}, u32[]{:S(2)}) collective-permute-start(bf16[4,5,8,128]{3,2,1,0:T(8,128)(2,1)S(1)} %pad_maximum_fusion.1._), channel_id=1, source_target_pairs={{0,4},{1,5},{2,6},{3,7},{4,0},{5,1},{6,2},{7,3},{8,12},{9,13},{10,... | collective-permute-start | bytes 122888 | tf_op jit(solution)/shard_map/ppermute | solution.py:488
  12.4 5.5 %collective-permute-start.3 = (bf16[8,5,8,128]{3,2,1,0:T(8,128)(2,1)S(1)}, bf16[8,5,8,128]{3,2,1,0:T(8,128)(2,1)S(1)}, u32[]{:S(2)}, u32[]{:S(2)}) collective-permute-start(bf16[8,5,8,128]{3,2,1,0:T(8,128)(2,1)S(1)} %pad_maximum_fusion._), channel_id=1, source_target_pairs={{0,8},{1,9},{2,10},{3,11},{4,12},{5,13},{6,14},{7,15},{8,0},{9,1},... | collective-permute-start | bytes 245768 | tf_op jit(solution)/shard_map/ppermute | solution.py:488
  17.9 29.1 %copy-start = (f32[4,1024]{1,0:T(4,128)S(1)}, f32[4,1024]{1,0:T(4,128)}, u32[]{:S(2)}) copy-start(f32[4,1024]{1,0:T(4,128)} %masters_ref.3) | copy-start | bytes 49156
  17.9 29.1 %copy-start.2 = (f32[4,1024]{1,0:T(4,128)S(1)}, f32[4,1024]{1,0:T(4,128)}, u32[]{:S(2)}) copy-start(f32[4,1024]{1,0:T(4,128)} %velocity_ref.1) | copy-start | bytes 49156
  32.2 1.4 %collective-permute-start.4 = (f32[8,4,8,128]{3,2,1,0:T(8,128)S(1)}, f32[8,4,8,128]{3,2,1,0:T(8,128)S(1)}, u32[]{:S(2)}, u32[]{:S(2)}) collective-permute-start(f32[8,4,8,128]{3,2,1,0:T(8,128)S(1)} %slice.22), channel_id=1, source_target_pairs={{0,1},{1,0},{2,3},{3,2},{4,5},{5,4},{6,7},{7,6},{8,9},{9,8},{10,11... | collective-permute-start | bytes 393224 | tf_op jit(solution)/shard_map/ppermute | solution.py:488
  33.7 4.3 %collective-permute-start.5 = (f32[4,4,8,128]{3,2,1,0:T(8,128)S(1)}, f32[4,4,8,128]{3,2,1,0:T(8,128)S(1)}, u32[]{:S(2)}, u32[]{:S(2)}) collective-permute-start(f32[4,4,8,128]{3,2,1,0:T(8,128)S(1)} %slice.29), channel_id=1, source_target_pairs={{0,2},{1,3},{2,0},{3,1},{4,6},{5,7},{6,4},{7,5},{8,10},{9,11},{10,... | collective-permute-start | bytes 196616 | tf_op jit(solution)/shard_map/ppermute | solution.py:488
  38.0 4.0 %collective-permute-start.6 = (f32[2,4,8,128]{3,2,1,0:T(8,128)S(1)}, f32[2,4,8,128]{3,2,1,0:T(8,128)S(1)}, u32[]{:S(2)}, u32[]{:S(2)}) collective-permute-start(f32[2,4,8,128]{3,2,1,0:T(8,128)S(1)} %slice.31), channel_id=1, source_target_pairs={{0,4},{1,5},{2,6},{3,7},{4,0},{5,1},{6,2},{7,3},{8,12},{9,13},{10,... | collective-permute-start | bytes 98312 | tf_op jit(solution)/shard_map/ppermute | solution.py:488
  42.0 5.0 %collective-permute-start.7 = (f32[1,4,8,128]{3,2,1,0:T(8,128)S(1)}, f32[1,4,8,128]{3,2,1,0:T(8,128)S(1)}, u32[]{:S(2)}, u32[]{:S(2)}) collective-permute-start(f32[1,4,8,128]{3,2,1,0:T(8,128)S(1)} %slice.32), channel_id=1, source_target_pairs={{0,8},{1,9},{2,10},{3,11},{4,12},{5,13},{6,14},{7,15},{8,0},{9,1},... | collective-permute-start | bytes 49160 | tf_op jit(solution)/shard_map/ppermute | solution.py:488

commit v5 on v4

--- a/solution.py
+++ b/solution.py
@@ -15,9 +15,16 @@
 CH = 2 * TERMS
 LANES = 128
 BLK = 64
+EXT = 128
 STEP = 32
+GROUP = 4
+BANDS = (
+    (MODES * CH * BLK, LANES),
+    (2 * MODES, 2 * EXT, LANES),
+    (2 * MODES, CH * EXT // 2, LANES),
+    (4 * MODES, 2 * EXT, LANES),
+)
 NBLK = W // BLK
-EXT = 128
 PAD = 40
 CROWS = 72
 GROWS = 2 * PAD + EXT
@@ -58,7 +65,7 @@
     return lane_iota((BLK, LANES)) < BLK
 
 
-def row_bands_kernel(row_ref, col_ref, r_ref, taps):
+def fill_taps(row_ref, col_ref, taps):
     count = MODES * CH
     taps[...] = jnp.zeros_like(taps)
     for k in range(MODES):
@@ -75,61 +82,42 @@
     )
     taps[count : 2 * count, :] = pltpu.roll(taps[count : 2 * count, :], LANES - (TAPS - 1), 1)
 
+
+def bands_kernel(row_ref, col_ref, r_ref, rt_ref, cf_ref, ca_ref, taps):
+    count = MODES * CH
+
+    @pl.when(pl.program_id(0) == 0)
+    def _():
+        fill_taps(row_ref, col_ref, taps)
+
+    low = low_lanes()
+
     def step(n, carry):
+        first = (pl.program_id(0) * GROUP + n) * 4
         for f in range(4):
-            at = n * 4 + f
-            r_ref[pl.ds(at * BLK, BLK), :] = half_band(skew(taps[pl.ds(at, 1), :], 0))
-        return carry
-
-    lax.fori_loop(0, 2 * MODES, step, 0, unroll=3)
-
-
-def row_adjoint_kernel(taps, _, rt_ref):
-    count = MODES * CH
-    low = low_lanes()
-
-    def step(n, carry):
-        first = 2 * count + 4 * n
+            r_ref[pl.ds((4 * n + f) * BLK, BLK), :] = half_band(
+                skew(taps[pl.ds(first + f, 1), :], 0)
+            )
         for par in range(2):
             a, a_far, b, b_far = pair(
-                taps[pl.ds(first + par, 1), :], taps[pl.ds(first + 2 + par, 1), :]
+                taps[pl.ds(2 * count + first + par, 1), :],
+                taps[pl.ds(2 * count + first + 2 + par, 1), :],
             )
             rt_ref[n, par * EXT : par * EXT + BLK, :] = half_band(jnp.where(low, a, b_far))
             rt_ref[n, par * EXT + BLK : (par + 1) * EXT, :] = half_band(jnp.where(low, a_far, b))
-        return carry
-
-    lax.fori_loop(0, 2 * MODES, step, 0, unroll=3)
-
-
-def column_bands_kernel(taps, _, cf_ref):
-    count = MODES * CH
-    low = low_lanes()
-
-    def step(n, carry):
-        first = 3 * count + 4 * n
         for t in range(2):
             at = t * 2 * EXT
             a, a_far, b, b_far = pair(
-                taps[pl.ds(first + 2 * t, 1), :], taps[pl.ds(first + 2 * t + 1, 1), :]
+                taps[pl.ds(3 * count + first + 2 * t, 1), :],
+                taps[pl.ds(3 * count + first + 2 * t + 1, 1), :],
             )
             cf_ref[n, at : at + BLK, :] = half_band(jnp.where(low, a, b_far))
             cf_ref[n, at + BLK : at + EXT, :] = half_band(jnp.where(low, a_far, b))
             cf_ref[n, at + EXT : at + EXT + BLK, :] = half_band(jnp.where(low, -b, a_far))
             cf_ref[n, at + EXT + BLK : at + 2 * EXT, :] = half_band(jnp.where(low, -b_far, a))
-        return carry
-
-    lax.fori_loop(0, 2 * MODES, step, 0, unroll=3)
-
-
-def column_adjoint_kernel(taps, _, ca_ref):
-    count = MODES * CH
-    low = low_lanes()
-
-    def step(n, carry):
-        first = count + 4 * n
-        for t in range(2):
             a, a_far, b, b_far = pair(
-                taps[pl.ds(first + 2 * t, 1), :], taps[pl.ds(first + 2 * t + 1, 1), :]
+                taps[pl.ds(count + first + 2 * t, 1), :],
+                taps[pl.ds(count + first + 2 * t + 1, 1), :],
             )
             ca_ref[n * 2 + t, :BLK, :] = half_band(jnp.where(low, a, -b_far))
             ca_ref[n * 2 + t, BLK:EXT, :] = half_band(jnp.where(low, a_far, -b))
@@ -137,43 +125,26 @@
             ca_ref[n * 2 + t, EXT + BLK :, :] = half_band(jnp.where(low, b_far, a))
         return carry
 
-    lax.fori_loop(0, 2 * MODES, step, 0, unroll=3)
-
-
-def build_bands(row_taps, col_taps, stages):
+    lax.fori_loop(0, GROUP, step, 0)
+
+
+def build_bands(row_taps, col_taps):
     vmem = pl.BlockSpec(memory_space=pltpu.VMEM)
-    small = pltpu.CompilerParams(vmem_limit_bytes=4 << 20)
-    r, taps = pl.pallas_call(
-        row_bands_kernel,
-        out_shape=(
-            pltpu.VMEM((MODES * CH * BLK, LANES), jnp.bfloat16),
-            pltpu.VMEM((4 * MODES * CH, LANES), jnp.float32),
-        ),
+    return pl.pallas_call(
+        bands_kernel,
+        grid=(2 * MODES // GROUP,),
+        out_shape=[pltpu.HBM(shape, jnp.bfloat16) for shape in BANDS],
         in_specs=[vmem] * 2,
-        out_specs=[vmem] * 2,
-        compiler_params=small,
-        name="row_bands",
+        out_specs=[
+            pl.BlockSpec((4 * GROUP * BLK, LANES), lambda n: (n, 0)),
+            pl.BlockSpec((GROUP, 2 * EXT, LANES), lambda n: (n, 0, 0)),
+            pl.BlockSpec((GROUP, CH * EXT // 2, LANES), lambda n: (n, 0, 0)),
+            pl.BlockSpec((2 * GROUP, 2 * EXT, LANES), lambda n: (n, 0, 0)),
+        ],
+        scratch_shapes=[pltpu.VMEM((4 * MODES * CH, LANES), jnp.float32)],
+        compiler_params=pltpu.CompilerParams(vmem_limit_bytes=8 << 20),
+        name="bands",
     )(in_hbm(row_taps), in_hbm(col_taps))
-    taps = in_vmem(taps)
-    built = [
-        pl.pallas_call(
-            kernel,
-            out_shape=pltpu.VMEM(shape, jnp.bfloat16),
-            in_specs=[vmem, pl.BlockSpec(memory_space=pl.ANY)],
-            out_specs=vmem,
-            compiler_params=small,
-            name=name,
-        )(taps, stage)
-        for stage, (kernel, shape, name) in zip(
-            stages,
-            (
-                (column_bands_kernel, (2 * MODES, CH * EXT // 2, LANES), "column_bands"),
-                (row_adjoint_kernel, (2 * MODES, 2 * EXT, LANES), "row_adjoint"),
-                (column_adjoint_kernel, (4 * MODES, 2 * EXT, LANES), "column_adjoint"),
-            ),
-        )
-    ]
-    return [r, built[1], built[0], built[2]]
 
 
 def reversed_bits(value, bits):
@@ -185,10 +156,10 @@
     weight_ref,
     gathered_ref,
     target_ref,
-    r_ref,
-    rt_ref,
-    cf_ref,
-    ca_ref,
+    r_hbm,
+    rt_hbm,
+    cf_hbm,
+    ca_hbm,
     resid_ref,
     grads_ref,
     *scratch,
@@ -196,7 +167,14 @@
     canvases = (scratch[0:4], scratch[4:8], scratch[8:12])
     grads = scratch[12:16]
     sums = scratch[16:19]
-    window, lhs, fields, slope, gw, gys, table, ids, sem = scratch[19:]
+    window, lhs, fields, slope, gw, gys, table, ids, sem = scratch[19:28]
+    r_ref, rt_ref, cf_ref, ca_ref, band_sems = scratch[28:]
+    loads = [
+        pltpu.make_async_copy(source, target, band_sems.at[n])
+        for n, (source, target) in enumerate(
+            ((r_hbm, r_ref), (cf_hbm, cf_ref), (ca_hbm, ca_ref), (rt_hbm, rt_ref))
+        )
+    ]
     slabs = gathered_ref.shape[0] // devices
     count = slabs - 1
     places = LANES
@@ -207,14 +185,14 @@
     for n, (other, missing) in enumerate(
         ((me, 0), (jnp.maximum(me - 1, 0), 0), (jnp.minimum(me + 1, devices - 1), BLK - MS))
     ):
-        slab = gathered_ref[(other ^ me) * slabs + count].astype(jnp.float32).astype(jnp.int32)
-        owner, local, row, col = slab[0:1] ^ me, slab[1:2], slab[2:3], slab[3:4]
+        slab = gathered_ref[other * slabs + count].astype(jnp.float32).astype(jnp.int32)
+        owner, local, row, col = slab[0:1], slab[1:2], slab[2:3], slab[3:4]
         if n:
             row = jnp.where(other == me, missing, row)
         lines = jnp.concatenate(
             [
                 owner * slabs + local,
-                reversed_bits(owner, bits) * count + local,
+                reversed_bits(owner ^ me, bits) * count + local,
                 ((col + HALF) >> 7) * CROWS + row + 7,
                 (col + HALF) & 127,
                 (col >> 7) * GROWS + row + bases[n],
@@ -230,6 +208,8 @@
             )[:, :STEP]
     to_scalar = pltpu.make_async_copy(table, ids, sem)
     to_scalar.start()
+    for load in loads:
+        load.start()
     for group in canvases:
         for canvas in group:
             canvas[...] = jnp.zeros_like(canvas)
@@ -293,6 +273,8 @@
     lanes16 = lane_iota((16, LANES))
     before = lanes16 < HALF
     until = lanes16 < HALF + BLK
+    loads[0].wait()
+    loads[1].wait()
     intensity = jnp.zeros((NBLK * rows, LANES), jnp.float32)
     for k in range(MODES):
         field_y = jnp.dot(
@@ -328,6 +310,7 @@
         else:
             resid_ref[:, (b // 2) * LANES + BLK : (b // 2 + 1) * LANES] = resid[:, BLK:]
 
+    loads[2].wait()
     nothing = jnp.zeros((16, LANES), jnp.float32)
     for k in range(MODES):
         weight = weight_ref[k]
@@ -354,6 +337,7 @@
             for b in range(NBLK):
                 gys[at : at + rows, b * LANES : (b + 1) * LANES] = gy[b * rows : (b + 1) * rows]
 
+    loads[3].wait()
     total = jnp.zeros((2 * EXT, NBLK * LANES), jnp.float32)
     for k in range(MODES):
         total = total + jnp.dot(
@@ -415,7 +399,9 @@
             jax.ShapeDtypeStruct(target.shape, jnp.float32),
             pltpu.VMEM((devices, count, 8, LANES), jnp.float32),
         ),
-        in_specs=[pl.BlockSpec(memory_space=pltpu.SMEM)] + [vmem] * 6,
+        in_specs=[pl.BlockSpec(memory_space=pltpu.SMEM)]
+        + [vmem] * 2
+        + [pl.BlockSpec(memory_space=pl.ANY)] * 4,
         out_specs=[vmem] * 2,
         scratch_shapes=[
             *[pltpu.VMEM((3 * CROWS, LANES), jnp.float32)] * 12,
@@ -430,10 +416,12 @@
             pltpu.VMEM((LANES // STEP, 24, STEP), jnp.int32),
             pltpu.SMEM((LANES // STEP, 24, STEP), jnp.int32),
             pltpu.SemaphoreType.DMA,
+            *[pltpu.VMEM(shape, jnp.bfloat16) for shape in BANDS],
+            pltpu.SemaphoreType.DMA((4,)),
         ],
-        compiler_params=pltpu.CompilerParams(vmem_limit_bytes=24 << 20),
+        compiler_params=pltpu.CompilerParams(vmem_limit_bytes=36 << 20),
         name="imaging",
-    )(weights, in_vmem(gathered.reshape(devices * slabs, 8, LANES)), target, *[in_vmem(b) for b in bands])
+    )(weights, in_vmem(gathered.reshape(devices * slabs, 8, LANES)), target, *[in_hbm(b) for b in bands])
 
 
 def pack_kernel(masters_ref, owner_ref, local_ref, row_ref, col_ref, out_ref, spread):
@@ -443,15 +431,17 @@
     spread[8 * count :, :] = jnp.zeros((8, LANES), jnp.float32)
     for n, ref in enumerate((owner_ref, local_ref, row_ref, col_ref)):
         spread[8 * count + n : 8 * count + n + 1, :] = ref[...].astype(jnp.float32)
-    out_ref[...] = spread[...].reshape(out_ref.shape).astype(jnp.bfloat16)
-
-
-def pack(masters, *places):
+    packed = spread[...].reshape(out_ref.shape[1:]).astype(jnp.bfloat16)
+    for d in range(out_ref.shape[0]):
+        out_ref[d] = packed
+
+
+def pack(devices, masters, *places):
     count = masters.shape[0]
     vmem = pl.BlockSpec(memory_space=pltpu.VMEM)
     return pl.pallas_call(
         pack_kernel,
-        out_shape=pltpu.VMEM((1, count + 1, 8, LANES), jnp.bfloat16),
+        out_shape=pltpu.VMEM((devices, count + 1, 8, LANES), jnp.bfloat16),
         in_specs=[vmem] * 5,
         out_specs=vmem,
         scratch_shapes=[pltpu.VMEM((8 * count + 8, LANES), jnp.float32)],
@@ -502,12 +492,9 @@
 ):
     devices = lax.axis_size("tx")
     bits = devices.bit_length() - 1
-    held = pack(masters, place_owner, place_local, place_row, place_col)
-    stages = []
-    for b in range(bits):
-        held = jnp.concatenate([held, swap(held, 1 << b, devices)], axis=0)
-        stages.append(held)
-    bands = build_bands(row_taps, col_taps, stages[-4:-1])
+    packed = pack(devices, masters, place_owner, place_local, place_row, place_col)
+    held = lax.all_to_all(packed, "tx", split_axis=0, concat_axis=0, tiled=True)
+    bands = build_bands(row_taps, col_taps)
     resid, grads = main_step(mode_weights, held, target, bands)
     for b in range(bits):
         half = grads.shape[0] // 2

time: 47.9 us -> 49.3 us (1.029)
  Pallas kernels: 22.4 us -> 24.6 us
  starting transfers between devices: 15.5 us -> 13.6 us
  local copies, waits for them, and re-layouts: 0.1 us -> 1.45 us
    ppermute x8 -> x4, starting transfers between devices: 15.5 us -> 6.16 us  [swap(): return lax.ppermute(value, 'tx', [(i, i ^ bit) for i in range(devices)])]
    all_to_all x0 -> x1, starting transfers between devices: none -> 7.41 us  [on_device(): held = lax.all_to_all(packed, 'tx', split_axis=0, concat_axis=0, tiled=True)]
    pallas_call x5 -> x2, Pallas kernels: 7.57 us -> 9.57 us  [the longest x1 8.13 us: build_bands(): pl.pallas_call(bands_kernel, grid=(2 * MODES // GROUP,), out_shape=[pltpu...]
    unnamed x12 -> x8, local copies, waits for them, and re-layouts: 0.06 us -> 1.42 us
    ppermute x8 -> x4, waiting for transfers between devices: 8.73 us -> 8.26 us  [swap(): return lax.ppermute(value, 'tx', [(i, i ^ bit) for i in range(devices)])]
  transfers between devices with their start and end apart: 8 -> 5, of which waited for: 6 -> 5; matrix products, arithmetic and copies ran while one was open for 0% -> 0% of each run, Pallas kernels for 14% -> 17%
where the time goes in v5:
time: 49.3 us; the launch traced here: 48.9 us
  Pallas kernels  24.6 us (50%)
  starting transfers between devices  13.6 us (28%)
  waiting for transfers between devices  8.56 us (17%)
  local copies, waits for them, and re-layouts  1.45 us (3%)
  between operations  0.69 us (1%)
    pallas_call x1, Pallas kernels, main_step(): pl.pallas_call(functools.partial(main_kernel, devices), out_shape=(jax.Sh...  14.4 us
    ppermute x4, waiting for transfers between devices, swap(): return lax.ppermute(value, 'tx', [(i, i ^ bit) for i in range(devices)])  8.26 us
    pallas_call x1, Pallas kernels, build_bands(): pl.pallas_call(bands_kernel, grid=(2 * MODES // GROUP,), out_shape=[pltpu...  8.13 us
    all_to_all x1, starting transfers between devices, on_device(): held = lax.all_to_all(packed, 'tx', split_axis=0, concat_axis=0, tiled=True)  7.41 us
    ppermute x4, starting transfers between devices, swap(): return lax.ppermute(value, 'tx', [(i, i ^ bit) for i in range(devices)])  6.16 us
    pallas_call x1, Pallas kernels, pack(): pl.pallas_call(pack_kernel, out_shape=pltpu.VMEM((devices, count + 1, 8,...  1.43 us
    unnamed x8, local copies, waits for them, and re-layouts  1.42 us
  transfers between devices with their start and end apart: 5, of which 5 were waited for; matrix products, arithmetic and copies ran while one was open for 0% of the time, Pallas kernels for 17%

profile of v5, /device:TPU:0, one launch (start us, length us, event | category | flops | bytes accessed | tf_op | source)
XLA Modules:
  0.0 48.9 jit_solution(15936130563751156114)
XLA Ops:
  0.6 1.4 %pack.1 = bf16[16,5,8,128]{3,2,1,0:T(8,128)(2,1)} custom-call(f32[4,1024]{1,0:T(4,128)} %masters_ref.3, s32[1,128]{1,0:T(1,128)} %bitcast.6, s32[1,128]{1,0:T(1,128)} %bitcast.7, s32[1,128]{1,0:T(1,128)} %bitcast.8, s32[1,128]{1,0:T(1,128)} %bitcast.9), custom_call_target="tpu_custom_call" | custom-call | tf_op jit(solution)/shard_map/pack/pallas_call | solution.py:442
  2.1 7.4 %all-to-all-start = ((bf16[16,5,8,128]{3,2,1,0:T(8,128)(2,1)}), bf16[16,5,8,128]{3,2,1,0:T(8,128)(2,1)S(1)}, u32[]{:S(2)}, u32[]{:S(2)}) async-start(bf16[16,5,8,128]{3,2,1,0:T(8,128)(2,1)} %pack.1), calls=%async_computation | async-start | bytes 327680 | tf_op jit(solution)/shard_map/all_to_all | solution.py:496
  9.5 8.1 %bands.1 = (bf16[6144,128]{1,0:T(8,128)(2,1)}, bf16[24,256,128]{2,1,0:T(8,128)(2,1)}, bf16[24,512,128]{2,1,0:T(8,128)(2,1)}, bf16[48,256,128]{2,1,0:T(8,128)(2,1)}) custom-call(bf16[12,4,2,63]{3,2,1,0:T(2,128)(2,1)} %row_ref.1, bf16[12,4,2,63]{3,2,1,0:T(2,128)(2,1)} %col_ref.1), custom_call_target="tpu_custom_call" | custom-call | tf_op jit(solution)/shard_map/bands/pallas_call | solution.py:133
  17.6 0.3 all-to-all-done
  17.9 0.0 copy-start.1
  17.9 0.8 %copy-done.1 = bf16[64,256]{1,0:T(8,128)(2,1)S(1)} copy-done((bf16[64,256]{1,0:T(8,128)(2,1)S(1)}, bf16[64,256]{1,0:T(8,128)(2,1)}, u32[]{:S(2)}) %copy-start.1) | copy-done | bytes 32792
  18.7 0.0 copy-start.3
  18.7 0.7 %copy-done.3 = f32[12]{0:T(128)S(1)} copy-done((f32[12]{0:T(128)S(1)}, f32[12]{0:T(128)}, u32[]{:S(2)}) %copy-start.3) | copy-done | bytes 72
  19.3 0.0 copy-start
  19.3 0.0 copy-start.2
  19.3 14.4 %imaging.1 = (f32[64,256]{1,0:T(8,128)}, f32[16,4,8,128]{3,2,1,0:T(8,128)S(1)}) custom-call(f32[12]{0:T(128)S(1)} %copy-done.3, bf16[80,8,128]{2,1,0:T(8,128)(2,1)S(1)} %bitcast.5, bf16[64,256]{1,0:T(8,128)(2,1)S(1)} %copy-done.1, bf16[6144,128]{1,0:T(8,128)(2,1)} %get-tuple-element.11.r_hbm, bf16[24,256,128]{2,1,0:T(8,128)(2,1)} %get-tuple-element.12.rt_hbm, ...), custom_call_target="tpu_custom_call" | custom-call | tf_op jit(solution)/shard_map/imaging/pallas_call | solution.py:396
  33.8 0.2 collective-permute-start
  33.9 1.2 %collective-permute-done = f32[8,4,8,128]{3,2,1,0:T(8,128)S(1)} collective-permute-done((f32[8,4,8,128]{3,2,1,0:T(8,128)S(1)}, f32[8,4,8,128]{3,2,1,0:T(8,128)S(1)}, u32[]{:S(2)}, u32[]{:S(2)}) %collective-permute-start) | collective-permute-done | bytes 131104 | tf_op jit(solution)/shard_map/ppermute | solution.py:478
  35.2 1.7 %collective-permute-start.1 = (f32[4,4,8,128]{3,2,1,0:T(8,128)S(1)}, f32[4,4,8,128]{3,2,1,0:T(8,128)S(1)}, u32[]{:S(2)}, u32[]{:S(2)}) collective-permute-start(f32[4,4,8,128]{3,2,1,0:T(8,128)S(1)} %slice.29), channel_id=1, source_target_pairs={{0,2},{1,3},{2,0},{3,1},{4,6},{5,7},{6,4},{7,5},{8,10},{9,11},{10,... | collective-permute-start | bytes 196616 | tf_op jit(solution)/shard_map/ppermute | solution.py:478
  36.9 2.6 %collective-permute-done.1 = f32[4,4,8,128]{3,2,1,0:T(8,128)S(1)} collective-permute-done((f32[4,4,8,128]{3,2,1,0:T(8,128)S(1)}, f32[4,4,8,128]{3,2,1,0:T(8,128)S(1)}, u32[]{:S(2)}, u32[]{:S(2)}) %collective-permute-start.1) | collective-permute-done | bytes 65568 | tf_op jit(solution)/shard_map/ppermute | solution.py:478
  39.6 1.7 %collective-permute-start.2 = (f32[2,4,8,128]{3,2,1,0:T(8,128)S(1)}, f32[2,4,8,128]{3,2,1,0:T(8,128)S(1)}, u32[]{:S(2)}, u32[]{:S(2)}) collective-permute-start(f32[2,4,8,128]{3,2,1,0:T(8,128)S(1)} %slice.31), channel_id=1, source_target_pairs={{0,4},{1,5},{2,6},{3,7},{4,0},{5,1},{6,2},{7,3},{8,12},{9,13},{10,... | collective-permute-start | bytes 98312 | tf_op jit(solution)/shard_map/ppermute | solution.py:478
  41.3 2.3 %collective-permute-done.2 = f32[2,4,8,128]{3,2,1,0:T(8,128)S(1)} collective-permute-done((f32[2,4,8,128]{3,2,1,0:T(8,128)S(1)}, f32[2,4,8,128]{3,2,1,0:T(8,128)S(1)}, u32[]{:S(2)}, u32[]{:S(2)}) %collective-permute-start.2) | collective-permute-done | bytes 32800 | tf_op jit(solution)/shard_map/ppermute | solution.py:478
  43.6 2.6 %collective-permute-start.3 = (f32[1,4,8,128]{3,2,1,0:T(8,128)S(1)}, f32[1,4,8,128]{3,2,1,0:T(8,128)S(1)}, u32[]{:S(2)}, u32[]{:S(2)}) collective-permute-start(f32[1,4,8,128]{3,2,1,0:T(8,128)S(1)} %slice.32), channel_id=1, source_target_pairs={{0,8},{1,9},{2,10},{3,11},{4,12},{5,13},{6,14},{7,15},{8,0},{9,1},... | collective-permute-start | bytes 49160 | tf_op jit(solution)/shard_map/ppermute | solution.py:478
  46.2 2.1 %collective-permute-done.3.sent_ref = f32[1,4,8,128]{3,2,1,0:T(8,128)S(1)} collective-permute-done((f32[1,4,8,128]{3,2,1,0:T(8,128)S(1)}, f32[1,4,8,128]{3,2,1,0:T(8,128)S(1)}, u32[]{:S(2)}, u32[]{:S(2)}) %collective-permute-start.3) | collective-permute-done | bytes 16416 | tf_op jit(solution)/shard_map/ppermute | solution.py:478
  48.3 0.0 copy-done
  48.3 0.0 copy-done.2
  48.3 0.6 %update.1 = (f32[4,1024]{1,0:T(4,128)}, f32[4,1024]{1,0:T(4,128)}) custom-call(f32[2,4,8,128]{3,2,1,0:T(8,128)S(1)} %slice_add_fusion.2.kept_ref, f32[1,4,8,128]{3,2,1,0:T(8,128)S(1)} %collective-permute-done.3.sent_ref, f32[4,1024]{1,0:T(4,128)S(1)} %copy-done.2, f32[4,1024]{1,0:T(4,128)S(1)} %copy-done), custom_call_target="tpu_custom_call" | custom-call | tf_op jit(solution)/shard_map/update/pallas_call | solution.py:466
  (7 shorter events, 0.1 us)
Async XLA Ops:
  2.1 15.9 %all-to-all-start = ((bf16[16,5,8,128]{3,2,1,0:T(8,128)(2,1)}), bf16[16,5,8,128]{3,2,1,0:T(8,128)(2,1)S(1)}, u32[]{:S(2)}, u32[]{:S(2)}) async-start(bf16[16,5,8,128]{3,2,1,0:T(8,128)(2,1)} %pack.1), calls=%async_computation | async-start | bytes 327680 | tf_op jit(solution)/shard_map/all_to_all | solution.py:496
  17.9 0.8 %copy-start.1 = (bf16[64,256]{1,0:T(8,128)(2,1)S(1)}, bf16[64,256]{1,0:T(8,128)(2,1)}, u32[]{:S(2)}) copy-start(bf16[64,256]{1,0:T(8,128)(2,1)} %target_ref.1) | copy-start | bytes 98308
  18.7 0.7 %copy-start.3 = (f32[12]{0:T(128)S(1)}, f32[12]{0:T(128)}, u32[]{:S(2)}) copy-start(f32[12]{0:T(128)} %weight_ref.1) | copy-start | bytes 148
  19.3 28.9 %copy-start = (f32[4,1024]{1,0:T(4,128)S(1)}, f32[4,1024]{1,0:T(4,128)}, u32[]{:S(2)}) copy-start(f32[4,1024]{1,0:T(4,128)} %masters_ref.3) | copy-start | bytes 49156
  19.3 28.9 %copy-start.2 = (f32[4,1024]{1,0:T(4,128)S(1)}, f32[4,1024]{1,0:T(4,128)}, u32[]{:S(2)}) copy-start(f32[4,1024]{1,0:T(4,128)} %velocity_ref.1) | copy-start | bytes 49156
  33.8 1.4 %collective-permute-start = (f32[8,4,8,128]{3,2,1,0:T(8,128)S(1)}, f32[8,4,8,128]{3,2,1,0:T(8,128)S(1)}, u32[]{:S(2)}, u32[]{:S(2)}) collective-permute-start(f32[8,4,8,128]{3,2,1,0:T(8,128)S(1)} %slice.22), channel_id=1, source_target_pairs={{0,1},{1,0},{2,3},{3,2},{4,5},{5,4},{6,7},{7,6},{8,9},{9,8},{10,11... | collective-permute-start | bytes 393224 | tf_op jit(solution)/shard_map/ppermute | solution.py:478
  35.2 4.3 %collective-permute-start.1 = (f32[4,4,8,128]{3,2,1,0:T(8,128)S(1)}, f32[4,4,8,128]{3,2,1,0:T(8,128)S(1)}, u32[]{:S(2)}, u32[]{:S(2)}) collective-permute-start(f32[4,4,8,128]{3,2,1,0:T(8,128)S(1)} %slice.29), channel_id=1, source_target_pairs={{0,2},{1,3},{2,0},{3,1},{4,6},{5,7},{6,4},{7,5},{8,10},{9,11},{10,... | collective-permute-start | bytes 196616 | tf_op jit(solution)/shard_map/ppermute | solution.py:478
  39.6 4.0 %collective-permute-start.2 = (f32[2,4,8,128]{3,2,1,0:T(8,128)S(1)}, f32[2,4,8,128]{3,2,1,0:T(8,128)S(1)}, u32[]{:S(2)}, u32[]{:S(2)}) collective-permute-start(f32[2,4,8,128]{3,2,1,0:T(8,128)S(1)} %slice.31), channel_id=1, source_target_pairs={{0,4},{1,5},{2,6},{3,7},{4,0},{5,1},{6,2},{7,3},{8,12},{9,13},{10,... | collective-permute-start | bytes 98312 | tf_op jit(solution)/shard_map/ppermute | solution.py:478
  43.6 4.7 %collective-permute-start.3 = (f32[1,4,8,128]{3,2,1,0:T(8,128)S(1)}, f32[1,4,8,128]{3,2,1,0:T(8,128)S(1)}, u32[]{:S(2)}, u32[]{:S(2)}) collective-permute-start(f32[1,4,8,128]{3,2,1,0:T(8,128)S(1)} %slice.32), channel_id=1, source_target_pairs={{0,8},{1,9},{2,10},{3,11},{4,12},{5,13},{6,14},{7,15},{8,0},{9,1},... | collective-permute-start | bytes 49160 | tf_op jit(solution)/shard_map/ppermute | solution.py:478

commit v6 on v5

--- a/solution.py
+++ b/solution.py
@@ -18,12 +18,6 @@
 EXT = 128
 STEP = 32
 GROUP = 4
-BANDS = (
-    (MODES * CH * BLK, LANES),
-    (2 * MODES, 2 * EXT, LANES),
-    (2 * MODES, CH * EXT // 2, LANES),
-    (4 * MODES, 2 * EXT, LANES),
-)
 NBLK = W // BLK
 PAD = 40
 CROWS = 72
@@ -83,7 +77,7 @@
     taps[count : 2 * count, :] = pltpu.roll(taps[count : 2 * count, :], LANES - (TAPS - 1), 1)
 
 
-def bands_kernel(row_ref, col_ref, r_ref, rt_ref, cf_ref, ca_ref, taps):
+def bands_kernel(row_ref, col_ref, taps, cf_ref, ca_ref):
     count = MODES * CH
 
     @pl.when(pl.program_id(0) == 0)
@@ -94,17 +88,6 @@
 
     def step(n, carry):
         first = (pl.program_id(0) * GROUP + n) * 4
-        for f in range(4):
-            r_ref[pl.ds((4 * n + f) * BLK, BLK), :] = half_band(
-                skew(taps[pl.ds(first + f, 1), :], 0)
-            )
-        for par in range(2):
-            a, a_far, b, b_far = pair(
-                taps[pl.ds(2 * count + first + par, 1), :],
-                taps[pl.ds(2 * count + first + 2 + par, 1), :],
-            )
-            rt_ref[n, par * EXT : par * EXT + BLK, :] = half_band(jnp.where(low, a, b_far))
-            rt_ref[n, par * EXT + BLK : (par + 1) * EXT, :] = half_band(jnp.where(low, a_far, b))
         for t in range(2):
             at = t * 2 * EXT
             a, a_far, b, b_far = pair(
@@ -125,7 +108,7 @@
             ca_ref[n * 2 + t, EXT + BLK :, :] = half_band(jnp.where(low, b_far, a))
         return carry
 
-    lax.fori_loop(0, GROUP, step, 0)
+    lax.fori_loop(0, GROUP, step, 0, unroll=2)
 
 
 def build_bands(row_taps, col_taps):
@@ -133,15 +116,17 @@
     return pl.pallas_call(
         bands_kernel,
         grid=(2 * MODES // GROUP,),
-        out_shape=[pltpu.HBM(shape, jnp.bfloat16) for shape in BANDS],
+        out_shape=(
+            pltpu.HBM((4 * MODES * CH, LANES), jnp.float32),
+            pltpu.HBM((2 * MODES, CH * EXT // 2, LANES), jnp.bfloat16),
+            pltpu.HBM((4 * MODES, 2 * EXT, LANES), jnp.bfloat16),
+        ),
         in_specs=[vmem] * 2,
         out_specs=[
-            pl.BlockSpec((4 * GROUP * BLK, LANES), lambda n: (n, 0)),
-            pl.BlockSpec((GROUP, 2 * EXT, LANES), lambda n: (n, 0, 0)),
+            pl.BlockSpec((4 * MODES * CH, LANES), lambda n: (0, 0)),
             pl.BlockSpec((GROUP, CH * EXT // 2, LANES), lambda n: (n, 0, 0)),
             pl.BlockSpec((2 * GROUP, 2 * EXT, LANES), lambda n: (n, 0, 0)),
         ],
-        scratch_shapes=[pltpu.VMEM((4 * MODES * CH, LANES), jnp.float32)],
         compiler_params=pltpu.CompilerParams(vmem_limit_bytes=8 << 20),
         name="bands",
     )(in_hbm(row_taps), in_hbm(col_taps))
@@ -153,11 +138,10 @@
 
 def main_kernel(
     devices,
-    weight_ref,
     gathered_ref,
-    target_ref,
-    r_hbm,
-    rt_hbm,
+    weight_hbm,
+    target_hbm,
+    taps_hbm,
     cf_hbm,
     ca_hbm,
     resid_ref,
@@ -168,11 +152,17 @@
     grads = scratch[12:16]
     sums = scratch[16:19]
     window, lhs, fields, slope, gw, gys, table, ids, sem = scratch[19:28]
-    r_ref, rt_ref, cf_ref, ca_ref, band_sems = scratch[28:]
+    weight_ref, target_ref, taps, cf_ref, ca_ref, r_ref, rt_ref, load_sems = scratch[28:]
     loads = [
-        pltpu.make_async_copy(source, target, band_sems.at[n])
+        pltpu.make_async_copy(source, target, load_sems.at[n])
         for n, (source, target) in enumerate(
-            ((r_hbm, r_ref), (cf_hbm, cf_ref), (ca_hbm, ca_ref), (rt_hbm, rt_ref))
+            (
+                (taps_hbm, taps),
+                (weight_hbm, weight_ref),
+                (cf_hbm, cf_ref),
+                (target_hbm, target_ref),
+                (ca_hbm, ca_ref),
+            )
         )
     ]
     slabs = gathered_ref.shape[0] // devices
@@ -273,10 +263,31 @@
     lanes16 = lane_iota((16, LANES))
     before = lanes16 < HALF
     until = lanes16 < HALF + BLK
-    loads[0].wait()
-    loads[1].wait()
+    low64 = low_lanes()
+
+    def row_bands(k):
+        for c in range(CH):
+            at = k * CH + c
+            r_ref[at * BLK : (at + 1) * BLK, :] = half_band(skew(taps[at : at + 1, :], 0))
+
+    def row_adjoint_bands(k):
+        for n in (2 * k, 2 * k + 1):
+            tap = 2 * MODES * CH + 4 * n
+            for par in range(2):
+                one, two = tap + par, tap + 2 + par
+                a, a_far, b, b_far = pair(taps[one : one + 1, :], taps[two : two + 1, :])
+                at = par * EXT
+                rt_ref[n, at : at + BLK, :] = half_band(jnp.where(low64, a, b_far))
+                rt_ref[n, at + BLK : at + EXT, :] = half_band(jnp.where(low64, a_far, b))
+
+    for load in loads[:3]:
+        load.wait()
+    row_bands(0)
     intensity = jnp.zeros((NBLK * rows, LANES), jnp.float32)
     for k in range(MODES):
+        if k + 1 < MODES:
+            row_bands(k + 1)
+        row_adjoint_bands(k)
         field_y = jnp.dot(
             r_ref[k * CH * rows : (k + 1) * CH * rows, :],
             window[...],
@@ -294,8 +305,8 @@
         )
         fields[k] = e
         intensity = intensity + weight_ref[k] * (e * e)
+    loads[3].wait()
     low_rows = lane_iota((rows, LANES)) < BLK
-    resids = []
     for b in range(NBLK):
         inten = intensity[b * rows : (b + 1) * rows]
         inten = inten + pltpu.roll(inten, BLK, 1)
@@ -310,7 +321,7 @@
         else:
             resid_ref[:, (b // 2) * LANES + BLK : (b // 2 + 1) * LANES] = resid[:, BLK:]
 
-    loads[2].wait()
+    loads[4].wait()
     nothing = jnp.zeros((16, LANES), jnp.float32)
     for k in range(MODES):
         weight = weight_ref[k]
@@ -337,7 +348,6 @@
             for b in range(NBLK):
                 gys[at : at + rows, b * LANES : (b + 1) * LANES] = gy[b * rows : (b + 1) * rows]
 
-    loads[3].wait()
     total = jnp.zeros((2 * EXT, NBLK * LANES), jnp.float32)
     for k in range(MODES):
         total = total + jnp.dot(
@@ -399,9 +409,7 @@
             jax.ShapeDtypeStruct(target.shape, jnp.float32),
             pltpu.VMEM((devices, count, 8, LANES), jnp.float32),
         ),
-        in_specs=[pl.BlockSpec(memory_space=pltpu.SMEM)]
-        + [vmem] * 2
-        + [pl.BlockSpec(memory_space=pl.ANY)] * 4,
+        in_specs=[vmem] + [pl.BlockSpec(memory_space=pl.ANY)] * 5,
         out_specs=[vmem] * 2,
         scratch_shapes=[
             *[pltpu.VMEM((3 * CROWS, LANES), jnp.float32)] * 12,
@@ -416,12 +424,21 @@
             pltpu.VMEM((LANES // STEP, 24, STEP), jnp.int32),
             pltpu.SMEM((LANES // STEP, 24, STEP), jnp.int32),
             pltpu.SemaphoreType.DMA,
-            *[pltpu.VMEM(shape, jnp.bfloat16) for shape in BANDS],
-            pltpu.SemaphoreType.DMA((4,)),
+            pltpu.SMEM(weights.shape, jnp.float32),
+            pltpu.VMEM(target.shape, jnp.bfloat16),
+            pltpu.VMEM(bands[0].shape, jnp.float32),
+            pltpu.VMEM(bands[1].shape, jnp.bfloat16),
+            pltpu.VMEM(bands[2].shape, jnp.bfloat16),
+            pltpu.VMEM((MODES * CH * BLK, LANES), jnp.bfloat16),
+            pltpu.VMEM((2 * MODES, 2 * EXT, LANES), jnp.bfloat16),
+            pltpu.SemaphoreType.DMA((5,)),
         ],
         compiler_params=pltpu.CompilerParams(vmem_limit_bytes=36 << 20),
         name="imaging",
-    )(weights, in_vmem(gathered.reshape(devices * slabs, 8, LANES)), target, *[in_hbm(b) for b in bands])
+    )(
+        in_vmem(gathered.reshape(devices * slabs, 8, LANES)),
+        *[in_hbm(x) for x in (weights, target, *bands)],
+    )
 
 
 def pack_kernel(masters_ref, owner_ref, local_ref, row_ref, col_ref, out_ref, spread):

time: 49.3 us -> 47.3 us (0.959)
  waiting for transfers between devices: 8.56 us -> 15.6 us
  starting transfers between devices: 13.6 us -> 8.38 us
  Pallas kernels: 24.6 us -> 22.2 us
  local copies, waits for them, and re-layouts: 1.45 us -> 0.03 us
    ppermute x4, starting transfers between devices: 6.16 us -> 0.96 us  [swap(): return lax.ppermute(value, 'tx', [(i, i ^ bit) for i in range(devices)])]
    ppermute x4, waiting for transfers between devices: 8.26 us -> 13.4 us  [swap(): return lax.ppermute(value, 'tx', [(i, i ^ bit) for i in range(devices)])]
    pallas_call x1, Pallas kernels: 8.13 us -> 6.27 us  [build_bands(): pl.pallas_call(bands_kernel, grid=(2 * MODES // GROUP,), out_shape=(pltpu...]
    all_to_all x1, waiting for transfers between devices: 0.29 us -> 2.16 us  [on_device(): held = lax.all_to_all(packed, 'tx', split_axis=0, concat_axis=0, tiled=True)]
    unnamed x8 -> x4, local copies, waits for them, and re-layouts: 1.42 us -> 0.01 us
    pallas_call x1, Pallas kernels: 14.4 us -> 13.9 us  [main_step(): pl.pallas_call(functools.partial(main_kernel, devices), out_shape=(jax.Sh...]
  transfers between devices with their start and end apart: 5 -> 5, of which waited for: 5 -> 5; matrix products, arithmetic and copies ran while one was open for 0% -> 0% of each run, Pallas kernels for 17% -> 13%
where the time goes in v6:
time: 47.3 us; the launch traced here: 47 us
  Pallas kernels  22.2 us (47%)
  waiting for transfers between devices  15.6 us (33%)
  starting transfers between devices  8.38 us (18%)
  between operations  0.71 us (2%)
    pallas_call x1, Pallas kernels, main_step(): pl.pallas_call(functools.partial(main_kernel, devices), out_shape=(jax.Sh...  13.9 us
    ppermute x4, waiting for transfers between devices, swap(): return lax.ppermute(value, 'tx', [(i, i ^ bit) for i in range(devices)])  13.4 us
    all_to_all x1, starting transfers between devices, on_device(): held = lax.all_to_all(packed, 'tx', split_axis=0, concat_axis=0, tiled=True)  7.41 us
    pallas_call x1, Pallas kernels, build_bands(): pl.pallas_call(bands_kernel, grid=(2 * MODES // GROUP,), out_shape=(pltpu...  6.27 us
    all_to_all x1, waiting for transfers between devices, on_device(): held = lax.all_to_all(packed, 'tx', split_axis=0, concat_axis=0, tiled=True)  2.16 us
    pallas_call x1, Pallas kernels, pack(): pl.pallas_call(pack_kernel, out_shape=pltpu.VMEM((devices, count + 1, 8,...  1.45 us
    ppermute x4, starting transfers between devices, swap(): return lax.ppermute(value, 'tx', [(i, i ^ bit) for i in range(devices)])  0.96 us
  transfers between devices with their start and end apart: 5, of which 5 were waited for; matrix products, arithmetic and copies ran while one was open for 0% of the time, Pallas kernels for 13%

profile of v6, /device:TPU:0, one launch (start us, length us, event | category | flops | bytes accessed | tf_op | source)
XLA Modules:
  0.0 47.0 jit_solution(9950481360627890249)
XLA Ops:
  0.6 1.4 %pack.1 = bf16[16,5,8,128]{3,2,1,0:T(8,128)(2,1)} custom-call(f32[4,1024]{1,0:T(4,128)} %masters_ref.3, s32[1,128]{1,0:T(1,128)} %bitcast.6, s32[1,128]{1,0:T(1,128)} %bitcast.7, s32[1,128]{1,0:T(1,128)} %bitcast.8, s32[1,128]{1,0:T(1,128)} %bitcast.9), custom_call_target="tpu_custom_call" | custom-call | tf_op jit(solution)/shard_map/pack/pallas_call | solution.py:459
  2.1 7.4 %all-to-all-start = ((bf16[16,5,8,128]{3,2,1,0:T(8,128)(2,1)}), bf16[16,5,8,128]{3,2,1,0:T(8,128)(2,1)S(1)}, u32[]{:S(2)}, u32[]{:S(2)}) async-start(bf16[16,5,8,128]{3,2,1,0:T(8,128)(2,1)} %pack.1), calls=%async_computation | async-start | bytes 327680 | tf_op jit(solution)/shard_map/all_to_all | solution.py:513
  9.5 6.3 %bands.1 = (f32[384,128]{1,0:T(8,128)}, bf16[24,512,128]{2,1,0:T(8,128)(2,1)}, bf16[48,256,128]{2,1,0:T(8,128)(2,1)}) custom-call(bf16[12,4,2,63]{3,2,1,0:T(2,128)(2,1)} %row_ref.1, bf16[12,4,2,63]{3,2,1,0:T(2,128)(2,1)} %col_ref.1), custom_call_target="tpu_custom_call" | custom-call | tf_op jit(solution)/shard_map/bands/pallas_call | solution.py:116
  15.8 2.2 %all-to-all-done = bf16[16,5,8,128]{3,2,1,0:T(8,128)(2,1)S(1)} async-done(((bf16[16,5,8,128]{3,2,1,0:T(8,128)(2,1)}), bf16[16,5,8,128]{3,2,1,0:T(8,128)(2,1)S(1)}, u32[]{:S(2)}, u32[]{:S(2)}) %all-to-all-start) | async-done | bytes 163872 | tf_op jit(solution)/shard_map/all_to_all | solution.py:513
  17.9 0.0 copy-start
  17.9 0.0 copy-start.1
  17.9 13.9 %imaging.1 = (f32[64,256]{1,0:T(8,128)}, f32[16,4,8,128]{3,2,1,0:T(8,128)S(1)}) custom-call(bf16[80,8,128]{2,1,0:T(8,128)(2,1)S(1)} %bitcast.5, f32[12]{0:T(128)} %weight_hbm.1, bf16[64,256]{1,0:T(8,128)(2,1)} %target_hbm.1, f32[384,128]{1,0:T(8,128)} %get-tuple-element.10.taps_hbm, bf16[24,512,128]{2,1,0:T(8,128)(2,1)} %get-tuple-element.11.cf_hbm, ...), custom_call_target="tpu_custom_call" | custom-call | tf_op jit(solution)/shard_map/imaging/pallas_call | solution.py:406
  31.9 0.1 collective-permute-start
  31.9 1.3 %collective-permute-done = f32[8,4,8,128]{3,2,1,0:T(8,128)S(1)} collective-permute-done((f32[8,4,8,128]{3,2,1,0:T(8,128)S(1)}, f32[8,4,8,128]{3,2,1,0:T(8,128)S(1)}, u32[]{:S(2)}, u32[]{:S(2)}) %collective-permute-start) | collective-permute-done | bytes 131104 | tf_op jit(solution)/shard_map/ppermute | solution.py:495
  33.3 0.1 collective-permute-start.1
  33.4 4.3 %collective-permute-done.1 = f32[4,4,8,128]{3,2,1,0:T(8,128)S(1)} collective-permute-done((f32[4,4,8,128]{3,2,1,0:T(8,128)S(1)}, f32[4,4,8,128]{3,2,1,0:T(8,128)S(1)}, u32[]{:S(2)}, u32[]{:S(2)}) %collective-permute-start.1) | collective-permute-done | bytes 65568 | tf_op jit(solution)/shard_map/ppermute | solution.py:495
  37.7 0.1 collective-permute-start.2
  37.7 3.9 %collective-permute-done.2 = f32[2,4,8,128]{3,2,1,0:T(8,128)S(1)} collective-permute-done((f32[2,4,8,128]{3,2,1,0:T(8,128)S(1)}, f32[2,4,8,128]{3,2,1,0:T(8,128)S(1)}, u32[]{:S(2)}, u32[]{:S(2)}) %collective-permute-start.2) | collective-permute-done | bytes 32800 | tf_op jit(solution)/shard_map/ppermute | solution.py:495
  41.7 0.8 %collective-permute-start.3 = (f32[1,4,8,128]{3,2,1,0:T(8,128)S(1)}, f32[1,4,8,128]{3,2,1,0:T(8,128)S(1)}, u32[]{:S(2)}, u32[]{:S(2)}) collective-permute-start(f32[1,4,8,128]{3,2,1,0:T(8,128)S(1)} %slice.32), channel_id=1, source_target_pairs={{0,8},{1,9},{2,10},{3,11},{4,12},{5,13},{6,14},{7,15},{8,0},{9,1},... | collective-permute-start | bytes 49160 | tf_op jit(solution)/shard_map/ppermute | solution.py:495
  42.4 4.0 %collective-permute-done.3.sent_ref = f32[1,4,8,128]{3,2,1,0:T(8,128)S(1)} collective-permute-done((f32[1,4,8,128]{3,2,1,0:T(8,128)S(1)}, f32[1,4,8,128]{3,2,1,0:T(8,128)S(1)}, u32[]{:S(2)}, u32[]{:S(2)}) %collective-permute-start.3) | collective-permute-done | bytes 16416 | tf_op jit(solution)/shard_map/ppermute | solution.py:495
  46.4 0.0 copy-done
  46.4 0.0 copy-done.1
  46.4 0.6 %update.1 = (f32[4,1024]{1,0:T(4,128)}, f32[4,1024]{1,0:T(4,128)}) custom-call(f32[2,4,8,128]{3,2,1,0:T(8,128)S(1)} %slice_add_fusion.2.kept_ref, f32[1,4,8,128]{3,2,1,0:T(8,128)S(1)} %collective-permute-done.3.sent_ref, f32[4,1024]{1,0:T(4,128)S(1)} %copy-done.1, f32[4,1024]{1,0:T(4,128)S(1)} %copy-done), custom_call_target="tpu_custom_call" | custom-call | tf_op jit(solution)/shard_map/update/pallas_call | solution.py:483
  (7 shorter events, 0.1 us)
Async XLA Ops:
  2.1 15.9 %all-to-all-start = ((bf16[16,5,8,128]{3,2,1,0:T(8,128)(2,1)}), bf16[16,5,8,128]{3,2,1,0:T(8,128)(2,1)S(1)}, u32[]{:S(2)}, u32[]{:S(2)}) async-start(bf16[16,5,8,128]{3,2,1,0:T(8,128)(2,1)} %pack.1), calls=%async_computation | async-start | bytes 327680 | tf_op jit(solution)/shard_map/all_to_all | solution.py:513
  17.9 28.4 %copy-start = (f32[4,1024]{1,0:T(4,128)S(1)}, f32[4,1024]{1,0:T(4,128)}, u32[]{:S(2)}) copy-start(f32[4,1024]{1,0:T(4,128)} %masters_ref.3) | copy-start | bytes 49156
  17.9 28.4 %copy-start.1 = (f32[4,1024]{1,0:T(4,128)S(1)}, f32[4,1024]{1,0:T(4,128)}, u32[]{:S(2)}) copy-start(f32[4,1024]{1,0:T(4,128)} %velocity_ref.1) | copy-start | bytes 49156
  31.9 1.4 %collective-permute-start = (f32[8,4,8,128]{3,2,1,0:T(8,128)S(1)}, f32[8,4,8,128]{3,2,1,0:T(8,128)S(1)}, u32[]{:S(2)}, u32[]{:S(2)}) collective-permute-start(f32[8,4,8,128]{3,2,1,0:T(8,128)S(1)} %slice.22), channel_id=1, source_target_pairs={{0,1},{1,0},{2,3},{3,2},{4,5},{5,4},{6,7},{7,6},{8,9},{9,8},{10,11... | collective-permute-start | bytes 393224 | tf_op jit(solution)/shard_map/ppermute | solution.py:495
  33.3 4.3 %collective-permute-start.1 = (f32[4,4,8,128]{3,2,1,0:T(8,128)S(1)}, f32[4,4,8,128]{3,2,1,0:T(8,128)S(1)}, u32[]{:S(2)}, u32[]{:S(2)}) collective-permute-start(f32[4,4,8,128]{3,2,1,0:T(8,128)S(1)} %slice.29), channel_id=1, source_target_pairs={{0,2},{1,3},{2,0},{3,1},{4,6},{5,7},{6,4},{7,5},{8,10},{9,11},{10,... | collective-permute-start | bytes 196616 | tf_op jit(solution)/shard_map/ppermute | solution.py:495
  37.7 4.0 %collective-permute-start.2 = (f32[2,4,8,128]{3,2,1,0:T(8,128)S(1)}, f32[2,4,8,128]{3,2,1,0:T(8,128)S(1)}, u32[]{:S(2)}, u32[]{:S(2)}) collective-permute-start(f32[2,4,8,128]{3,2,1,0:T(8,128)S(1)} %slice.31), channel_id=1, source_target_pairs={{0,4},{1,5},{2,6},{3,7},{4,0},{5,1},{6,2},{7,3},{8,12},{9,13},{10,... | collective-permute-start | bytes 98312 | tf_op jit(solution)/shard_map/ppermute | solution.py:495
  41.7 4.7 %collective-permute-start.3 = (f32[1,4,8,128]{3,2,1,0:T(8,128)S(1)}, f32[1,4,8,128]{3,2,1,0:T(8,128)S(1)}, u32[]{:S(2)}, u32[]{:S(2)}) collective-permute-start(f32[1,4,8,128]{3,2,1,0:T(8,128)S(1)} %slice.32), channel_id=1, source_target_pairs={{0,8},{1,9},{2,10},{3,11},{4,12},{5,13},{6,14},{7,15},{8,0},{9,1},... | collective-permute-start | bytes 49160 | tf_op jit(solution)/shard_map/ppermute | solution.py:495

commit v7 on v4

--- a/solution.py
+++ b/solution.py
@@ -15,9 +15,9 @@
 CH = 2 * TERMS
 LANES = 128
 BLK = 64
+EXT = 128
 STEP = 32
 NBLK = W // BLK
-EXT = 128
 PAD = 40
 CROWS = 72
 GROWS = 2 * PAD + EXT
@@ -58,7 +58,7 @@
     return lane_iota((BLK, LANES)) < BLK
 
 
-def row_bands_kernel(row_ref, col_ref, r_ref, taps):
+def taps_kernel(row_ref, col_ref, taps):
     count = MODES * CH
     taps[...] = jnp.zeros_like(taps)
     for k in range(MODES):
@@ -75,31 +75,6 @@
     )
     taps[count : 2 * count, :] = pltpu.roll(taps[count : 2 * count, :], LANES - (TAPS - 1), 1)
 
-    def step(n, carry):
-        for f in range(4):
-            at = n * 4 + f
-            r_ref[pl.ds(at * BLK, BLK), :] = half_band(skew(taps[pl.ds(at, 1), :], 0))
-        return carry
-
-    lax.fori_loop(0, 2 * MODES, step, 0, unroll=3)
-
-
-def row_adjoint_kernel(taps, _, rt_ref):
-    count = MODES * CH
-    low = low_lanes()
-
-    def step(n, carry):
-        first = 2 * count + 4 * n
-        for par in range(2):
-            a, a_far, b, b_far = pair(
-                taps[pl.ds(first + par, 1), :], taps[pl.ds(first + 2 + par, 1), :]
-            )
-            rt_ref[n, par * EXT : par * EXT + BLK, :] = half_band(jnp.where(low, a, b_far))
-            rt_ref[n, par * EXT + BLK : (par + 1) * EXT, :] = half_band(jnp.where(low, a_far, b))
-        return carry
-
-    lax.fori_loop(0, 2 * MODES, step, 0, unroll=3)
-
 
 def column_bands_kernel(taps, _, cf_ref):
     count = MODES * CH
@@ -143,18 +118,16 @@
 def build_bands(row_taps, col_taps, stages):
     vmem = pl.BlockSpec(memory_space=pltpu.VMEM)
     small = pltpu.CompilerParams(vmem_limit_bytes=4 << 20)
-    r, taps = pl.pallas_call(
-        row_bands_kernel,
-        out_shape=(
-            pltpu.VMEM((MODES * CH * BLK, LANES), jnp.bfloat16),
-            pltpu.VMEM((4 * MODES * CH, LANES), jnp.float32),
-        ),
-        in_specs=[vmem] * 2,
-        out_specs=[vmem] * 2,
-        compiler_params=small,
-        name="row_bands",
-    )(in_hbm(row_taps), in_hbm(col_taps))
-    taps = in_vmem(taps)
+    taps = in_vmem(
+        pl.pallas_call(
+            taps_kernel,
+            out_shape=pltpu.VMEM((4 * MODES * CH, LANES), jnp.float32),
+            in_specs=[vmem] * 2,
+            out_specs=vmem,
+            compiler_params=small,
+            name="taps",
+        )(in_hbm(row_taps), in_hbm(col_taps))
+    )
     built = [
         pl.pallas_call(
             kernel,
@@ -168,12 +141,11 @@
             stages,
             (
                 (column_bands_kernel, (2 * MODES, CH * EXT // 2, LANES), "column_bands"),
-                (row_adjoint_kernel, (2 * MODES, 2 * EXT, LANES), "row_adjoint"),
                 (column_adjoint_kernel, (4 * MODES, 2 * EXT, LANES), "column_adjoint"),
             ),
         )
     ]
-    return [r, built[1], built[0], built[2]]
+    return [taps, *built]
 
 
 def reversed_bits(value, bits):
@@ -182,13 +154,12 @@
 
 def main_kernel(
     devices,
-    weight_ref,
     gathered_ref,
-    target_ref,
-    r_ref,
-    rt_ref,
+    taps,
     cf_ref,
     ca_ref,
+    weight_hbm,
+    target_hbm,
     resid_ref,
     grads_ref,
     *scratch,
@@ -196,7 +167,17 @@
     canvases = (scratch[0:4], scratch[4:8], scratch[8:12])
     grads = scratch[12:16]
     sums = scratch[16:19]
-    window, lhs, fields, slope, gw, gys, table, ids, sem = scratch[19:]
+    window, lhs, fields, slope, gw, gys, table, ids, sem = scratch[19:28]
+    weight_ref, target_ref, r_ref, rt_ref, load_sems = scratch[28:]
+    loads = [
+        pltpu.make_async_copy(source, target, load_sems.at[n])
+        for n, (source, target) in enumerate(
+            (
+                (weight_hbm, weight_ref),
+                (target_hbm, target_ref),
+            )
+        )
+    ]
     slabs = gathered_ref.shape[0] // devices
     count = slabs - 1
     places = LANES
@@ -230,6 +211,8 @@
             )[:, :STEP]
     to_scalar = pltpu.make_async_copy(table, ids, sem)
     to_scalar.start()
+    for load in loads:
+        load.start()
     for group in canvases:
         for canvas in group:
             canvas[...] = jnp.zeros_like(canvas)
@@ -293,8 +276,30 @@
     lanes16 = lane_iota((16, LANES))
     before = lanes16 < HALF
     until = lanes16 < HALF + BLK
+    low64 = low_lanes()
+
+    def row_bands(k):
+        for c in range(CH):
+            at = k * CH + c
+            r_ref[at * BLK : (at + 1) * BLK, :] = half_band(skew(taps[at : at + 1, :], 0))
+
+    def row_adjoint_bands(k):
+        for n in (2 * k, 2 * k + 1):
+            tap = 2 * MODES * CH + 4 * n
+            for par in range(2):
+                one, two = tap + par, tap + 2 + par
+                a, a_far, b, b_far = pair(taps[one : one + 1, :], taps[two : two + 1, :])
+                at = par * EXT
+                rt_ref[n, at : at + BLK, :] = half_band(jnp.where(low64, a, b_far))
+                rt_ref[n, at + BLK : at + EXT, :] = half_band(jnp.where(low64, a_far, b))
+
+    loads[0].wait()
+    row_bands(0)
     intensity = jnp.zeros((NBLK * rows, LANES), jnp.float32)
     for k in range(MODES):
+        if k + 1 < MODES:
+            row_bands(k + 1)
+        row_adjoint_bands(k)
         field_y = jnp.dot(
             r_ref[k * CH * rows : (k + 1) * CH * rows, :],
             window[...],
@@ -312,8 +317,8 @@
         )
         fields[k] = e
         intensity = intensity + weight_ref[k] * (e * e)
+    loads[1].wait()
     low_rows = lane_iota((rows, LANES)) < BLK
-    resids = []
     for b in range(NBLK):
         inten = intensity[b * rows : (b + 1) * rows]
         inten = inten + pltpu.roll(inten, BLK, 1)
@@ -415,7 +420,7 @@
             jax.ShapeDtypeStruct(target.shape, jnp.float32),
             pltpu.VMEM((devices, count, 8, LANES), jnp.float32),
         ),
-        in_specs=[pl.BlockSpec(memory_space=pltpu.SMEM)] + [vmem] * 6,
+        in_specs=[vmem] * 4 + [pl.BlockSpec(memory_space=pl.ANY)] * 2,
         out_specs=[vmem] * 2,
         scratch_shapes=[
             *[pltpu.VMEM((3 * CROWS, LANES), jnp.float32)] * 12,
@@ -430,10 +435,20 @@
             pltpu.VMEM((LANES // STEP, 24, STEP), jnp.int32),
             pltpu.SMEM((LANES // STEP, 24, STEP), jnp.int32),
             pltpu.SemaphoreType.DMA,
+            pltpu.SMEM(weights.shape, jnp.float32),
+            pltpu.VMEM(target.shape, jnp.bfloat16),
+            pltpu.VMEM((MODES * CH * BLK, LANES), jnp.bfloat16),
+            pltpu.VMEM((2 * MODES, 2 * EXT, LANES), jnp.bfloat16),
+            pltpu.SemaphoreType.DMA((2,)),
         ],
-        compiler_params=pltpu.CompilerParams(vmem_limit_bytes=24 << 20),
+        compiler_params=pltpu.CompilerParams(vmem_limit_bytes=28 << 20),
         name="imaging",
-    )(weights, in_vmem(gathered.reshape(devices * slabs, 8, LANES)), target, *[in_vmem(b) for b in bands])
+    )(
+        in_vmem(gathered.reshape(devices * slabs, 8, LANES)),
+        *[in_vmem(x) for x in bands],
+        in_hbm(weights),
+        in_hbm(target),
+    )
 
 
 def pack_kernel(masters_ref, owner_ref, local_ref, row_ref, col_ref, out_ref, spread):
@@ -507,7 +522,7 @@
     for b in range(bits):
         held = jnp.concatenate([held, swap(held, 1 << b, devices)], axis=0)
         stages.append(held)
-    bands = build_bands(row_taps, col_taps, stages[-4:-1])
+    bands = build_bands(row_taps, col_taps, (stages[0], stages[-2]))
     resid, grads = main_step(mode_weights, held, target, bands)
     for b in range(bits):
         half = grads.shape[0] // 2

time: 47.9 us -> 46.7 us (0.975)
  Pallas kernels: 22.4 us -> 19.8 us
  waiting for transfers between devices: 8.73 us -> 10.1 us
    pallas_call x3 -> x2, Pallas kernels: 4.91 us -> 3.54 us  [build_bands(): pl.pallas_call(kernel, out_shape=pltpu.VMEM(shape, jnp.bfloat16), in_spec...]
    ppermute x8, waiting for transfers between devices: 8.73 us -> 10.1 us  [swap(): return lax.ppermute(value, 'tx', [(i, i ^ bit) for i in range(devices)])]
    pallas_call x1, Pallas kernels: 1.89 us -> 0.93 us  [build_bands(): pl.pallas_call(taps_kernel, out_shape=pltpu.VMEM((4 * MODES * CH, LANES),...]
  transfers between devices with their start and end apart: 8 -> 8, of which waited for: 6 -> 6; matrix products, arithmetic and copies ran while one was open for 0% -> 0% of each run, Pallas kernels for 14% -> 10%
where the time goes in v7:
time: 46.7 us; the launch traced here: 46.5 us
  Pallas kernels  19.8 us (42%)
  starting transfers between devices  15.7 us (34%)
  waiting for transfers between devices  10.1 us (22%)
  between operations  0.75 us (2%)
    ppermute x8, starting transfers between devices, swap(): return lax.ppermute(value, 'tx', [(i, i ^ bit) for i in range(devices)])  15.7 us
    pallas_call x1, Pallas kernels, main_step(): pl.pallas_call(functools.partial(main_kernel, devices), out_shape=(jax.Sh...  13.9 us
    ppermute x8, waiting for transfers between devices, swap(): return lax.ppermute(value, 'tx', [(i, i ^ bit) for i in range(devices)])  10.1 us
    pallas_call x2, Pallas kernels, build_bands(): pl.pallas_call(kernel, out_shape=pltpu.VMEM(shape, jnp.bfloat16), in_spec...  3.54 us
  transfers between devices with their start and end apart: 8, of which 6 were waited for; matrix products, arithmetic and copies ran while one was open for 0% of the time, Pallas kernels for 10%

profile of v7, /device:TPU:0, one launch (start us, length us, event | category | flops | bytes accessed | tf_op | source)
XLA Modules:
  0.0 46.5 jit_solution(14371722055293643642)
XLA Ops:
  0.6 0.8 %pack.1 = bf16[1,5,8,128]{3,2,1,0:T(8,128)(2,1)S(1)} custom-call(f32[4,1024]{1,0:T(4,128)} %masters_ref.3, s32[1,128]{1,0:T(1,128)} %bitcast.6, s32[1,128]{1,0:T(1,128)} %bitcast.7, s32[1,128]{1,0:T(1,128)} %bitcast.8, s32[1,128]{1,0:T(1,128)} %bitcast.9), custom_call_target="tpu_custom_call" | custom-call | tf_op jit(solution)/shard_map/pack/pallas_call | solution.py:467
  1.4 0.6 %collective-permute-start = (bf16[1,5,8,128]{3,2,1,0:T(8,128)(2,1)S(1)}, bf16[1,5,8,128]{3,2,1,0:T(8,128)(2,1)S(1)}, u32[]{:S(2)}, u32[]{:S(2)}) collective-permute-start(bf16[1,5,8,128]{3,2,1,0:T(8,128)(2,1)S(1)} %pack.1), channel_id=1, source_target_pairs={{0,1},{1,0},{2,3},{3,2},{4,5},{5,4},{6,7},{7,6},{8,9},{9,8},{10,11... | collective-permute-start | bytes 30728 | tf_op jit(solution)/shard_map/ppermute | solution.py:503
  2.0 0.9 %taps.1 = f32[384,128]{1,0:T(8,128)S(1)} custom-call(bf16[12,4,2,63]{3,2,1,0:T(2,128)(2,1)} %row_ref.1, bf16[12,4,2,63]{3,2,1,0:T(2,128)(2,1)} %col_ref.1), custom_call_target="tpu_custom_call" | custom-call | tf_op jit(solution)/shard_map/taps/pallas_call | solution.py:122
  2.9 0.0 collective-permute-done
  2.9 2.7 %collective-permute-start.1 = (bf16[2,5,8,128]{3,2,1,0:T(8,128)(2,1)S(1)}, bf16[2,5,8,128]{3,2,1,0:T(8,128)(2,1)S(1)}, u32[]{:S(2)}, u32[]{:S(2)}) collective-permute-start(bf16[2,5,8,128]{3,2,1,0:T(8,128)(2,1)S(1)} %pad_maximum_fusion.2._), channel_id=1, source_target_pairs={{0,2},{1,3},{2,0},{3,1},{4,6},{5,7},{6,4},{7,5},{8,10},{9,11},{10,... | collective-permute-start | bytes 61448 | tf_op jit(solution)/shard_map/ppermute | solution.py:503
  5.7 1.8 %column_bands.1.cf_ref = bf16[24,512,128]{2,1,0:T(8,128)(2,1)S(1)} custom-call(f32[384,128]{1,0:T(8,128)S(1)} %taps.1, bf16[2,5,8,128]{3,2,1,0:T(8,128)(2,1)S(1)} %pad_maximum_fusion.2._), custom_call_target="tpu_custom_call" | custom-call | tf_op jit(solution)/shard_map/column_bands/pallas_call | solution.py:132
  7.4 0.0 collective-permute-done.1
  7.5 2.1 %collective-permute-start.2 = (bf16[4,5,8,128]{3,2,1,0:T(8,128)(2,1)S(1)}, bf16[4,5,8,128]{3,2,1,0:T(8,128)(2,1)S(1)}, u32[]{:S(2)}, u32[]{:S(2)}) collective-permute-start(bf16[4,5,8,128]{3,2,1,0:T(8,128)(2,1)S(1)} %pad_maximum_fusion.1), channel_id=1, source_target_pairs={{0,4},{1,5},{2,6},{3,7},{4,0},{5,1},{6,2},{7,3},{8,12},{9,13},{10,... | collective-permute-start | bytes 122888 | tf_op jit(solution)/shard_map/ppermute | solution.py:503
  9.6 2.0 %collective-permute-done.2 = bf16[4,5,8,128]{3,2,1,0:T(8,128)(2,1)S(1)} collective-permute-done((bf16[4,5,8,128]{3,2,1,0:T(8,128)(2,1)S(1)}, bf16[4,5,8,128]{3,2,1,0:T(8,128)(2,1)S(1)}, u32[]{:S(2)}, u32[]{:S(2)}) %collective-permute-start.2) | collective-permute-done | bytes 40992 | tf_op jit(solution)/shard_map/ppermute | solution.py:503
  11.5 3.1 %collective-permute-start.3 = (bf16[8,5,8,128]{3,2,1,0:T(8,128)(2,1)S(1)}, bf16[8,5,8,128]{3,2,1,0:T(8,128)(2,1)S(1)}, u32[]{:S(2)}, u32[]{:S(2)}) collective-permute-start(bf16[8,5,8,128]{3,2,1,0:T(8,128)(2,1)S(1)} %pad_maximum_fusion._), channel_id=1, source_target_pairs={{0,8},{1,9},{2,10},{3,11},{4,12},{5,13},{6,14},{7,15},{8,0},{9,1},... | collective-permute-start | bytes 245768 | tf_op jit(solution)/shard_map/ppermute | solution.py:503
  14.6 1.8 %column_adjoint.1.ca_ref = bf16[48,256,128]{2,1,0:T(8,128)(2,1)S(1)} custom-call(f32[384,128]{1,0:T(8,128)S(1)} %taps.1, bf16[8,5,8,128]{3,2,1,0:T(8,128)(2,1)S(1)} %pad_maximum_fusion._), custom_call_target="tpu_custom_call" | custom-call | tf_op jit(solution)/shard_map/column_adjoint/pallas_call | solution.py:132
  16.4 0.6 %collective-permute-done.3 = bf16[8,5,8,128]{3,2,1,0:T(8,128)(2,1)S(1)} collective-permute-done((bf16[8,5,8,128]{3,2,1,0:T(8,128)(2,1)S(1)}, bf16[8,5,8,128]{3,2,1,0:T(8,128)(2,1)S(1)}, u32[]{:S(2)}, u32[]{:S(2)}) %collective-permute-start.3) | collective-permute-done | bytes 81952 | tf_op jit(solution)/shard_map/ppermute | solution.py:503
  17.1 0.0 copy-start
  17.1 0.0 copy-start.1
  17.1 13.9 %imaging.1 = (f32[64,256]{1,0:T(8,128)}, f32[16,4,8,128]{3,2,1,0:T(8,128)S(1)}) custom-call(bf16[80,8,128]{2,1,0:T(8,128)(2,1)S(1)} %bitcast.5, f32[384,128]{1,0:T(8,128)S(1)} %taps.1, bf16[24,512,128]{2,1,0:T(8,128)(2,1)S(1)} %column_bands.1.cf_ref, bf16[48,256,128]{2,1,0:T(8,128)(2,1)S(1)} %column_adjoint.1.ca_ref, f32[12]{0:T(128)} %weight_hbm.1, ...), custom_call_target="tpu_custom_call" | custom-call | tf_op jit(solution)/shard_map/imaging/pallas_call | solution.py:417
  31.0 0.1 collective-permute-start.4
  31.1 1.3 %collective-permute-done.4 = f32[8,4,8,128]{3,2,1,0:T(8,128)S(1)} collective-permute-done((f32[8,4,8,128]{3,2,1,0:T(8,128)S(1)}, f32[8,4,8,128]{3,2,1,0:T(8,128)S(1)}, u32[]{:S(2)}, u32[]{:S(2)}) %collective-permute-start.4) | collective-permute-done | bytes 131104 | tf_op jit(solution)/shard_map/ppermute | solution.py:503
  32.5 1.9 %collective-permute-start.5 = (f32[4,4,8,128]{3,2,1,0:T(8,128)S(1)}, f32[4,4,8,128]{3,2,1,0:T(8,128)S(1)}, u32[]{:S(2)}, u32[]{:S(2)}) collective-permute-start(f32[4,4,8,128]{3,2,1,0:T(8,128)S(1)} %slice.29), channel_id=1, source_target_pairs={{0,2},{1,3},{2,0},{3,1},{4,6},{5,7},{6,4},{7,5},{8,10},{9,11},{10,... | collective-permute-start | bytes 196616 | tf_op jit(solution)/shard_map/ppermute | solution.py:503
  34.4 2.4 %collective-permute-done.5 = f32[4,4,8,128]{3,2,1,0:T(8,128)S(1)} collective-permute-done((f32[4,4,8,128]{3,2,1,0:T(8,128)S(1)}, f32[4,4,8,128]{3,2,1,0:T(8,128)S(1)}, u32[]{:S(2)}, u32[]{:S(2)}) %collective-permute-start.5) | collective-permute-done | bytes 65568 | tf_op jit(solution)/shard_map/ppermute | solution.py:503
  36.9 2.0 %collective-permute-start.6 = (f32[2,4,8,128]{3,2,1,0:T(8,128)S(1)}, f32[2,4,8,128]{3,2,1,0:T(8,128)S(1)}, u32[]{:S(2)}, u32[]{:S(2)}) collective-permute-start(f32[2,4,8,128]{3,2,1,0:T(8,128)S(1)} %slice.31), channel_id=1, source_target_pairs={{0,4},{1,5},{2,6},{3,7},{4,0},{5,1},{6,2},{7,3},{8,12},{9,13},{10,... | collective-permute-start | bytes 98312 | tf_op jit(solution)/shard_map/ppermute | solution.py:503
  38.8 2.0 %collective-permute-done.6 = f32[2,4,8,128]{3,2,1,0:T(8,128)S(1)} collective-permute-done((f32[2,4,8,128]{3,2,1,0:T(8,128)S(1)}, f32[2,4,8,128]{3,2,1,0:T(8,128)S(1)}, u32[]{:S(2)}, u32[]{:S(2)}) %collective-permute-start.6) | collective-permute-done | bytes 32800 | tf_op jit(solution)/shard_map/ppermute | solution.py:503
  40.8 3.3 %collective-permute-start.7 = (f32[1,4,8,128]{3,2,1,0:T(8,128)S(1)}, f32[1,4,8,128]{3,2,1,0:T(8,128)S(1)}, u32[]{:S(2)}, u32[]{:S(2)}) collective-permute-start(f32[1,4,8,128]{3,2,1,0:T(8,128)S(1)} %slice.32), channel_id=1, source_target_pairs={{0,8},{1,9},{2,10},{3,11},{4,12},{5,13},{6,14},{7,15},{8,0},{9,1},... | collective-permute-start | bytes 49160 | tf_op jit(solution)/shard_map/ppermute | solution.py:503
  44.1 1.7 %collective-permute-done.7.sent_ref = f32[1,4,8,128]{3,2,1,0:T(8,128)S(1)} collective-permute-done((f32[1,4,8,128]{3,2,1,0:T(8,128)S(1)}, f32[1,4,8,128]{3,2,1,0:T(8,128)S(1)}, u32[]{:S(2)}, u32[]{:S(2)}) %collective-permute-start.7) | collective-permute-done | bytes 16416 | tf_op jit(solution)/shard_map/ppermute | solution.py:503
  45.9 0.6 %update.1 = (f32[4,1024]{1,0:T(4,128)}, f32[4,1024]{1,0:T(4,128)}) custom-call(f32[2,4,8,128]{3,2,1,0:T(8,128)S(1)} %slice_add_fusion.2.kept_ref, f32[1,4,8,128]{3,2,1,0:T(8,128)S(1)} %collective-permute-done.7.sent_ref, f32[4,1024]{1,0:T(4,128)S(1)} %copy-done.1, f32[4,1024]{1,0:T(4,128)S(1)} %copy-done), custom_call_target="tpu_custom_call" | custom-call | tf_op jit(solution)/shard_map/update/pallas_call | solution.py:491
  (17 shorter events, 0.1 us)
Async XLA Ops:
  1.4 1.5 %collective-permute-start = (bf16[1,5,8,128]{3,2,1,0:T(8,128)(2,1)S(1)}, bf16[1,5,8,128]{3,2,1,0:T(8,128)(2,1)S(1)}, u32[]{:S(2)}, u32[]{:S(2)}) collective-permute-start(bf16[1,5,8,128]{3,2,1,0:T(8,128)(2,1)S(1)} %pack.1), channel_id=1, source_target_pairs={{0,1},{1,0},{2,3},{3,2},{4,5},{5,4},{6,7},{7,6},{8,9},{9,8},{10,11... | collective-permute-start | bytes 30728 | tf_op jit(solution)/shard_map/ppermute | solution.py:503
  2.9 4.5 %collective-permute-start.1 = (bf16[2,5,8,128]{3,2,1,0:T(8,128)(2,1)S(1)}, bf16[2,5,8,128]{3,2,1,0:T(8,128)(2,1)S(1)}, u32[]{:S(2)}, u32[]{:S(2)}) collective-permute-start(bf16[2,5,8,128]{3,2,1,0:T(8,128)(2,1)S(1)} %pad_maximum_fusion.2._), channel_id=1, source_target_pairs={{0,2},{1,3},{2,0},{3,1},{4,6},{5,7},{6,4},{7,5},{8,10},{9,11},{10,... | collective-permute-start | bytes 61448 | tf_op jit(solution)/shard_map/ppermute | solution.py:503
  7.5 4.1 %collective-permute-start.2 = (bf16[4,5,8,128]{3,2,1,0:T(8,128)(2,1)S(1)}, bf16[4,5,8,128]{3,2,1,0:T(8,128)(2,1)S(1)}, u32[]{:S(2)}, u32[]{:S(2)}) collective-permute-start(bf16[4,5,8,128]{3,2,1,0:T(8,128)(2,1)S(1)} %pad_maximum_fusion.1), channel_id=1, source_target_pairs={{0,4},{1,5},{2,6},{3,7},{4,0},{5,1},{6,2},{7,3},{8,12},{9,13},{10,... | collective-permute-start | bytes 122888 | tf_op jit(solution)/shard_map/ppermute | solution.py:503
  11.5 5.5 %collective-permute-start.3 = (bf16[8,5,8,128]{3,2,1,0:T(8,128)(2,1)S(1)}, bf16[8,5,8,128]{3,2,1,0:T(8,128)(2,1)S(1)}, u32[]{:S(2)}, u32[]{:S(2)}) collective-permute-start(bf16[8,5,8,128]{3,2,1,0:T(8,128)(2,1)S(1)} %pad_maximum_fusion._), channel_id=1, source_target_pairs={{0,8},{1,9},{2,10},{3,11},{4,12},{5,13},{6,14},{7,15},{8,0},{9,1},... | collective-permute-start | bytes 245768 | tf_op jit(solution)/shard_map/ppermute | solution.py:503
  17.1 28.8 %copy-start = (f32[4,1024]{1,0:T(4,128)S(1)}, f32[4,1024]{1,0:T(4,128)}, u32[]{:S(2)}) copy-start(f32[4,1024]{1,0:T(4,128)} %masters_ref.3) | copy-start | bytes 49156
  17.1 28.8 %copy-start.1 = (f32[4,1024]{1,0:T(4,128)S(1)}, f32[4,1024]{1,0:T(4,128)}, u32[]{:S(2)}) copy-start(f32[4,1024]{1,0:T(4,128)} %velocity_ref.1) | copy-start | bytes 49156
  31.0 1.4 %collective-permute-start.4 = (f32[8,4,8,128]{3,2,1,0:T(8,128)S(1)}, f32[8,4,8,128]{3,2,1,0:T(8,128)S(1)}, u32[]{:S(2)}, u32[]{:S(2)}) collective-permute-start(f32[8,4,8,128]{3,2,1,0:T(8,128)S(1)} %slice.22), channel_id=1, source_target_pairs={{0,1},{1,0},{2,3},{3,2},{4,5},{5,4},{6,7},{7,6},{8,9},{9,8},{10,11... | collective-permute-start | bytes 393224 | tf_op jit(solution)/shard_map/ppermute | solution.py:503
  32.5 4.3 %collective-permute-start.5 = (f32[4,4,8,128]{3,2,1,0:T(8,128)S(1)}, f32[4,4,8,128]{3,2,1,0:T(8,128)S(1)}, u32[]{:S(2)}, u32[]{:S(2)}) collective-permute-start(f32[4,4,8,128]{3,2,1,0:T(8,128)S(1)} %slice.29), channel_id=1, source_target_pairs={{0,2},{1,3},{2,0},{3,1},{4,6},{5,7},{6,4},{7,5},{8,10},{9,11},{10,... | collective-permute-start | bytes 196616 | tf_op jit(solution)/shard_map/ppermute | solution.py:503
  36.9 4.0 %collective-permute-start.6 = (f32[2,4,8,128]{3,2,1,0:T(8,128)S(1)}, f32[2,4,8,128]{3,2,1,0:T(8,128)S(1)}, u32[]{:S(2)}, u32[]{:S(2)}) collective-permute-start(f32[2,4,8,128]{3,2,1,0:T(8,128)S(1)} %slice.31), channel_id=1, source_target_pairs={{0,4},{1,5},{2,6},{3,7},{4,0},{5,1},{6,2},{7,3},{8,12},{9,13},{10,... | collective-permute-start | bytes 98312 | tf_op jit(solution)/shard_map/ppermute | solution.py:503
  40.8 5.0 %collective-permute-start.7 = (f32[1,4,8,128]{3,2,1,0:T(8,128)S(1)}, f32[1,4,8,128]{3,2,1,0:T(8,128)S(1)}, u32[]{:S(2)}, u32[]{:S(2)}) collective-permute-start(f32[1,4,8,128]{3,2,1,0:T(8,128)S(1)} %slice.32), channel_id=1, source_target_pairs={{0,8},{1,9},{2,10},{3,11},{4,12},{5,13},{6,14},{7,15},{8,0},{9,1},... | collective-permute-start | bytes 49160 | tf_op jit(solution)/shard_map/ppermute | solution.py:503

commit v8 on v7

--- a/solution.py
+++ b/solution.py
@@ -18,9 +18,7 @@
 EXT = 128
 STEP = 32
 NBLK = W // BLK
-PAD = 40
-CROWS = 72
-GROWS = 2 * PAD + EXT
+CROWS = 320
 
 steepness = 0.5
 threshold = 8.0
@@ -164,11 +162,9 @@
     grads_ref,
     *scratch,
 ):
-    canvases = (scratch[0:4], scratch[4:8], scratch[8:12])
-    grads = scratch[12:16]
-    sums = scratch[16:19]
-    window, lhs, fields, slope, gw, gys, table, ids, sem = scratch[19:28]
-    weight_ref, target_ref, r_ref, rt_ref, load_sems = scratch[28:]
+    canvases, grads, sums = scratch[0:3], scratch[3:6], scratch[6:9]
+    window, lhs, fields, slope, gw, gys, table, ids, sem = scratch[9:18]
+    weight_ref, target_ref, r_ref, rt_ref, load_sems = scratch[18:]
     loads = [
         pltpu.make_async_copy(source, target, load_sems.at[n])
         for n, (source, target) in enumerate(
@@ -184,7 +180,7 @@
     rows = BLK
     me = lax.axis_index("tx")
     bits = devices.bit_length() - 1
-    bases = (PAD + HALF, PAD + HALF - rows, PAD + HALF + rows)
+    bases = (HALF, HALF - rows, HALF + rows)
     for n, (other, missing) in enumerate(
         ((me, 0), (jnp.maximum(me - 1, 0), 0), (jnp.minimum(me + 1, devices - 1), BLK - MS))
     ):
@@ -192,15 +188,16 @@
         owner, local, row, col = slab[0:1] ^ me, slab[1:2], slab[2:3], slab[3:4]
         if n:
             row = jnp.where(other == me, missing, row)
+        first_lane = (row + bases[n]) & 127
         lines = jnp.concatenate(
             [
                 owner * slabs + local,
                 reversed_bits(owner, bits) * count + local,
-                ((col + HALF) >> 7) * CROWS + row + 7,
-                (col + HALF) & 127,
-                (col >> 7) * GROWS + row + bases[n],
-                col & 127,
-                (LANES - (col & 127)) & 127,
+                col + HALF,
+                first_lane,
+                col,
+                (LANES - first_lane) & 127,
+                row,
                 row,
             ],
             axis=0,
@@ -213,29 +210,22 @@
     to_scalar.start()
     for load in loads:
         load.start()
-    for group in canvases:
-        for canvas in group:
-            canvas[...] = jnp.zeros_like(canvas)
+    for canvas in canvases:
+        canvas[...] = jnp.zeros_like(canvas)
     for acc in sums:
         acc[...] = jnp.zeros_like(acc)
     lanes8 = lane_iota((8, LANES))
     to_scalar.wait()
 
     def place(j, u):
-        for n, group in enumerate(canvases):
+        for n, canvas in enumerate(canvases):
             at, shift = ids[j, 8 * n + 2, u], ids[j, 8 * n + 3, u]
             moved = pltpu.roll(gathered_ref[ids[j, 8 * n, u]].astype(jnp.float32), shift, 1)
-            ahead = lanes8 - shift
-            here = ahead >= 0
-            nth = (ahead & 127) >> 5
-            near, far = jnp.where(here, moved, 0.0), jnp.where(here, 0.0, moved)
-            for k, canvas in enumerate(group):
-                spot = pl.ds(at + k, 8, stride=4)
-                spot_far = pl.ds(at + k + CROWS, 8, stride=4)
-                mine = nth == k
-                old, old_far = canvas[spot, :], canvas[spot_far, :]
-                canvas[spot, :] = old + jnp.where(mine, near, 0.0)
-                canvas[spot_far, :] = old_far + jnp.where(mine, far, 0.0)
+            nth = ((lanes8 - shift) & 127) >> 5
+            spots = [pl.ds(at + k * CROWS + k, 8, stride=4) for k in range(4)]
+            old = [canvas[spot, :] for spot in spots]
+            for k, spot in enumerate(spots):
+                canvas[spot, :] = old[k] + jnp.where(nth == k, moved, 0.0)
 
     @pl.loop(0, places // STEP)
     def _(j):
@@ -243,35 +233,37 @@
             place(j, u)
 
 
-    lanes_ext = lane_iota((EXT, LANES))
-    parts = [
+    def of_above(k, lanes):
+        return ((lanes - MS * k) & 127) < HALF
+
+    def of_below(k, lanes):
+        return ((lanes - MS * k) & 127) >= HALF + BLK
+
+    used = slice(24, 288)
+    wide = lane_iota((used.stop - used.start, LANES))
+    columns = 0.0
+    for k in range(4):
+        lines = slice(k * CROWS + used.start, k * CROWS + used.stop)
+        own, above, below = [canvas[lines, :] for canvas in canvases]
+        joined = (
+            own
+            + jnp.where(of_above(k, wide), above, 0.0)
+            + jnp.where(of_below(k, wide), below, 0.0)
+        )
+        columns = columns + (pltpu.roll(joined, LANES - MS * k, 1) if k else joined)
+    columns = jnp.concatenate(
         [
-            jnp.concatenate(
-                [
-                    above[h * CROWS + 40 : h * CROWS + 64],
-                    above[h * CROWS + 64 : (h + 1) * CROWS] + own[h * CROWS : h * CROWS + 8],
-                    own[h * CROWS + 8 : h * CROWS + 64],
-                    own[h * CROWS + 64 : (h + 1) * CROWS] + below[h * CROWS : h * CROWS + 8],
-                    below[h * CROWS + 8 : h * CROWS + 40],
-                ],
-                axis=0,
-            )
-            for h in range(3)
-        ]
-        for own, above, below in zip(*canvases)
-    ]
-    sides = [parts[0][h] for h in range(3)]
-    for k in range(1, 4):
-        back = [pltpu.roll(part, LANES - MS * k, 1) for part in parts[k]]
-        for h in range(3):
-            after = back[h + 1] if h < 2 else 0.0
-            sides[h] = sides[h] + jnp.where(lanes_ext < LANES - MS * k, back[h], after)
-    low = lanes_ext < BLK
-    turned = [pltpu.roll(side, BLK, 1) for side in sides]
-    window[:, 0:128] = sides[0].astype(jnp.bfloat16)
-    window[:, 128:256] = jnp.where(low, turned[0], turned[1]).astype(jnp.bfloat16)
-    window[:, 256:384] = sides[1].astype(jnp.bfloat16)
-    window[:, 384:512] = jnp.where(low, turned[1], turned[2]).astype(jnp.bfloat16)
+            jnp.zeros((used.start, LANES), jnp.float32),
+            columns,
+            jnp.zeros((CROWS - used.stop, LANES), jnp.float32),
+        ],
+        axis=0,
+    )
+    for b in range(NBLK):
+        window[:, b * LANES : (b + 1) * LANES] = jnp.transpose(
+            columns[b * BLK : b * BLK + LANES]
+        ).astype(jnp.bfloat16)
+    low = lane_iota((EXT, LANES)) < BLK
 
     lanes16 = lane_iota((16, LANES))
     before = lanes16 < HALF
@@ -375,31 +367,23 @@
         whole.append(
             jnp.where(low, v0 + pltpu.roll(u0, BLK, 1), pltpu.roll(v1, BLK, 1) + u1)
         )
-    zeros = jnp.zeros((PAD, LANES), jnp.float32)
-    for k, grad in enumerate(grads):
-        ahead = [pltpu.roll(side, MS * k, 1) if k else side for side in whole]
-        for h in range(3):
-            here = ahead[h] if h < 2 else 0.0
-            behind = ahead[h - 1] if h else 0.0
-            base = h * GROWS
-            grad[base : base + PAD, :] = zeros
-            grad[base + PAD : base + PAD + EXT, :] = jnp.where(lanes_ext >= MS * k, here, behind)
-            grad[base + PAD + EXT : base + GROWS, :] = zeros
+    columns = jnp.concatenate([jnp.transpose(side) for side in whole], axis=0)
+    wide = lane_iota((W, LANES))
+    for k in range(4):
+        turned = pltpu.roll(columns, MS * k, 1) if k else columns
+        lines = slice(k * W, (k + 1) * W)
+        grads[0][lines, :] = turned
+        grads[1][lines, :] = jnp.where(of_above(k, wide), turned, 0.0)
+        grads[2][lines, :] = jnp.where(of_below(k, wide), turned, 0.0)
 
     def gather(j, u):
         for n, acc in enumerate(sums):
-            m, at, shift, back = [ids[j, 8 * n + line, u] for line in (1, 4, 5, 6)]
-            ahead = lanes8 - shift
-            here = ahead >= 0
-            nth = ahead & 127
+            m, shift, at, back = [ids[j, 8 * n + line, u] for line in (1, 3, 4, 5)]
+            nth = (lanes8 - shift) & 127
             patch = None
-            for k, grad in enumerate(grads):
-                both = jnp.where(
-                    here,
-                    grad[pl.ds(at + k, 8, stride=4), :],
-                    grad[pl.ds(at + k + GROWS, 8, stride=4), :],
-                )
-                patch = jnp.where(nth >= MS * k, both, patch) if k else both
+            for k in range(4):
+                rows_k = grads[n][pl.ds(at + k * W + k, 8, stride=4), :]
+                patch = jnp.where(nth >= MS * k, rows_k, patch) if k else rows_k
             acc[m] += pltpu.roll(patch, back, 1)
 
     @pl.loop(0, places // STEP)
@@ -423,8 +407,8 @@
         in_specs=[vmem] * 4 + [pl.BlockSpec(memory_space=pl.ANY)] * 2,
         out_specs=[vmem] * 2,
         scratch_shapes=[
-            *[pltpu.VMEM((3 * CROWS, LANES), jnp.float32)] * 12,
-            *[pltpu.VMEM((3 * GROWS, LANES), jnp.float32)] * 4,
+            *[pltpu.VMEM((4 * CROWS, LANES), jnp.float32)] * 3,
+            *[pltpu.VMEM((4 * W, LANES), jnp.float32)] * 3,
             *[pltpu.VMEM((devices * count, 8, LANES), jnp.float32)] * 3,
             pltpu.VMEM((EXT, NBLK * LANES), jnp.bfloat16),
             pltpu.VMEM((2, NBLK * BLK, CH * LANES), jnp.bfloat16),
@@ -451,10 +435,36 @@
     )
 
 
-def pack_kernel(masters_ref, owner_ref, local_ref, row_ref, col_ref, out_ref, spread):
+def flip_pixels(slabs, cells):
+    lanes = lane_iota((8, LANES))
+
+    def chosen(parts):
+        out = parts[0]
+        for n, part in enumerate(parts):
+            if n:
+                out = jnp.where(lanes >= MS * n, part, out)
+        return out
+
+    def turned(x, blocks):
+        return pltpu.roll(x, (MS * blocks) % LANES, 1) if blocks else x
+
+    cells[MS:, :] = jnp.zeros((LANES - MS, LANES), jnp.float32)
+    for k in range(4):
+        cells[pl.ds(k, 8, stride=4), :] = chosen([turned(x, m - k) for m, x in enumerate(slabs)])
+    cells[...] = jnp.transpose(cells[...])
+    return [
+        chosen([turned(cells[pl.ds(MS * m + k, 8, stride=4), :], k) for k in range(4)])
+        for m in range(len(slabs))
+    ]
+
+
+def pack_kernel(masters_ref, owner_ref, local_ref, row_ref, col_ref, out_ref, spread, cells):
     count = masters_ref.shape[0]
     for s in range(8):
         spread[pl.ds(s, count, stride=8), :] = masters_ref[:, s * LANES : (s + 1) * LANES]
+    flipped = flip_pixels([spread[8 * m : 8 * m + 8, :] for m in range(count)], cells)
+    for m, slab in enumerate(flipped):
+        spread[8 * m : 8 * m + 8, :] = slab
     spread[8 * count :, :] = jnp.zeros((8, LANES), jnp.float32)
     for n, ref in enumerate((owner_ref, local_ref, row_ref, col_ref)):
         spread[8 * count + n : 8 * count + n + 1, :] = ref[...].astype(jnp.float32)
@@ -469,15 +479,22 @@
         out_shape=pltpu.VMEM((1, count + 1, 8, LANES), jnp.bfloat16),
         in_specs=[vmem] * 5,
         out_specs=vmem,
-        scratch_shapes=[pltpu.VMEM((8 * count + 8, LANES), jnp.float32)],
+        scratch_shapes=[
+            pltpu.VMEM((8 * count + 8, LANES), jnp.float32),
+            pltpu.VMEM((LANES, LANES), jnp.float32),
+        ],
         compiler_params=pltpu.CompilerParams(vmem_limit_bytes=4 << 20),
         name="pack",
     )(in_hbm(masters), *[in_hbm(p.reshape(1, LANES)) for p in places])
 
 
-def update_kernel(kept_ref, sent_ref, velocity_ref, masters_ref, velocity_out, masters_out, sums):
+def update_kernel(
+    kept_ref, sent_ref, velocity_ref, masters_ref, velocity_out, masters_out, sums, cells
+):
     count = velocity_ref.shape[0]
-    sums[...] = (kept_ref[0] + sent_ref[0]).reshape(count * 8, LANES)
+    flipped = flip_pixels([kept_ref[0, m] + sent_ref[0, m] for m in range(count)], cells)
+    for m, slab in enumerate(flipped):
+        sums[8 * m : 8 * m + 8, :] = slab
     for s in range(8):
         at = slice(s * LANES, (s + 1) * LANES)
         gradient = sums[pl.ds(s, count, stride=8), :]
@@ -493,7 +510,10 @@
         out_shape=(jax.ShapeDtypeStruct(velocity.shape, jnp.float32),) * 2,
         in_specs=[vmem] * 4,
         out_specs=[vmem] * 2,
-        scratch_shapes=[pltpu.VMEM((8 * velocity.shape[0], LANES), jnp.float32)],
+        scratch_shapes=[
+            pltpu.VMEM((8 * velocity.shape[0], LANES), jnp.float32),
+            pltpu.VMEM((LANES, LANES), jnp.float32),
+        ],
         compiler_params=pltpu.CompilerParams(vmem_limit_bytes=4 << 20),
         name="update",
     )(kept, sent, velocity, masters)

time: 46.7 us -> 46.2 us (0.989)
  Pallas kernels: 19.8 us -> 19.2 us
    pallas_call x1, Pallas kernels: 13.9 us -> 12.9 us  [main_step(): pl.pallas_call(functools.partial(main_kernel, devices), out_shape=(jax.Sh...]
where the time goes in v8:
time: 46.2 us; the launch traced here: 46 us
  Pallas kernels  19.2 us (42%)
  starting transfers between devices  15.7 us (34%)
  waiting for transfers between devices  10.1 us (22%)
  between operations  0.76 us (2%)
    ppermute x8, starting transfers between devices, swap(): return lax.ppermute(value, 'tx', [(i, i ^ bit) for i in range(devices)])  15.7 us
    pallas_call x1, Pallas kernels, main_step(): pl.pallas_call(functools.partial(main_kernel, devices), out_shape=(jax.Sh...  12.9 us
    ppermute x8, waiting for transfers between devices, swap(): return lax.ppermute(value, 'tx', [(i, i ^ bit) for i in range(devices)])  10.1 us
    pallas_call x2, Pallas kernels, build_bands(): pl.pallas_call(kernel, out_shape=pltpu.VMEM(shape, jnp.bfloat16), in_spec...  3.54 us
    pallas_call x1, Pallas kernels, pack(): pl.pallas_call(pack_kernel, out_shape=pltpu.VMEM((1, count + 1, 8, LANES)...  1.02 us
    pallas_call x1, Pallas kernels, build_bands(): pl.pallas_call(taps_kernel, out_shape=pltpu.VMEM((4 * MODES * CH, LANES),...  0.93 us
  transfers between devices with their start and end apart: 8, of which 6 were waited for; matrix products, arithmetic and copies ran while one was open for 0% of the time, Pallas kernels for 10%

profile of v8, /device:TPU:0, one launch (start us, length us, event | category | flops | bytes accessed | tf_op | source)
XLA Modules:
  0.0 46.0 jit_solution(8136084544131102783)
XLA Ops:
  0.6 1.0 %pack.1 = bf16[1,5,8,128]{3,2,1,0:T(8,128)(2,1)S(1)} custom-call(f32[4,1024]{1,0:T(4,128)} %masters_ref.3, s32[1,128]{1,0:T(1,128)} %bitcast.6, s32[1,128]{1,0:T(1,128)} %bitcast.7, s32[1,128]{1,0:T(1,128)} %bitcast.8, s32[1,128]{1,0:T(1,128)} %bitcast.9), custom_call_target="tpu_custom_call" | custom-call | tf_op jit(solution)/shard_map/pack/pallas_call | solution.py:477
  1.7 0.6 %collective-permute-start = (bf16[1,5,8,128]{3,2,1,0:T(8,128)(2,1)S(1)}, bf16[1,5,8,128]{3,2,1,0:T(8,128)(2,1)S(1)}, u32[]{:S(2)}, u32[]{:S(2)}) collective-permute-start(bf16[1,5,8,128]{3,2,1,0:T(8,128)(2,1)S(1)} %pack.1), channel_id=1, source_target_pairs={{0,1},{1,0},{2,3},{3,2},{4,5},{5,4},{6,7},{7,6},{8,9},{9,8},{10,11... | collective-permute-start | bytes 30728 | tf_op jit(solution)/shard_map/ppermute | solution.py:523
  2.2 0.9 %taps.1 = f32[384,128]{1,0:T(8,128)S(1)} custom-call(bf16[12,4,2,63]{3,2,1,0:T(2,128)(2,1)} %row_ref.1, bf16[12,4,2,63]{3,2,1,0:T(2,128)(2,1)} %col_ref.1), custom_call_target="tpu_custom_call" | custom-call | tf_op jit(solution)/shard_map/taps/pallas_call | solution.py:120
  3.1 0.0 collective-permute-done
  3.2 2.7 %collective-permute-start.1 = (bf16[2,5,8,128]{3,2,1,0:T(8,128)(2,1)S(1)}, bf16[2,5,8,128]{3,2,1,0:T(8,128)(2,1)S(1)}, u32[]{:S(2)}, u32[]{:S(2)}) collective-permute-start(bf16[2,5,8,128]{3,2,1,0:T(8,128)(2,1)S(1)} %pad_maximum_fusion.2._), channel_id=1, source_target_pairs={{0,2},{1,3},{2,0},{3,1},{4,6},{5,7},{6,4},{7,5},{8,10},{9,11},{10,... | collective-permute-start | bytes 61448 | tf_op jit(solution)/shard_map/ppermute | solution.py:523
  5.9 1.8 %column_bands.1.cf_ref = bf16[24,512,128]{2,1,0:T(8,128)(2,1)S(1)} custom-call(f32[384,128]{1,0:T(8,128)S(1)} %taps.1, bf16[2,5,8,128]{3,2,1,0:T(8,128)(2,1)S(1)} %pad_maximum_fusion.2._), custom_call_target="tpu_custom_call" | custom-call | tf_op jit(solution)/shard_map/column_bands/pallas_call | solution.py:130
  7.7 0.0 collective-permute-done.1
  7.7 2.1 %collective-permute-start.2 = (bf16[4,5,8,128]{3,2,1,0:T(8,128)(2,1)S(1)}, bf16[4,5,8,128]{3,2,1,0:T(8,128)(2,1)S(1)}, u32[]{:S(2)}, u32[]{:S(2)}) collective-permute-start(bf16[4,5,8,128]{3,2,1,0:T(8,128)(2,1)S(1)} %pad_maximum_fusion.1), channel_id=1, source_target_pairs={{0,4},{1,5},{2,6},{3,7},{4,0},{5,1},{6,2},{7,3},{8,12},{9,13},{10,... | collective-permute-start | bytes 122888 | tf_op jit(solution)/shard_map/ppermute | solution.py:523
  9.8 2.0 %collective-permute-done.2 = bf16[4,5,8,128]{3,2,1,0:T(8,128)(2,1)S(1)} collective-permute-done((bf16[4,5,8,128]{3,2,1,0:T(8,128)(2,1)S(1)}, bf16[4,5,8,128]{3,2,1,0:T(8,128)(2,1)S(1)}, u32[]{:S(2)}, u32[]{:S(2)}) %collective-permute-start.2) | collective-permute-done | bytes 40992 | tf_op jit(solution)/shard_map/ppermute | solution.py:523
  11.8 3.1 %collective-permute-start.3 = (bf16[8,5,8,128]{3,2,1,0:T(8,128)(2,1)S(1)}, bf16[8,5,8,128]{3,2,1,0:T(8,128)(2,1)S(1)}, u32[]{:S(2)}, u32[]{:S(2)}) collective-permute-start(bf16[8,5,8,128]{3,2,1,0:T(8,128)(2,1)S(1)} %pad_maximum_fusion._), channel_id=1, source_target_pairs={{0,8},{1,9},{2,10},{3,11},{4,12},{5,13},{6,14},{7,15},{8,0},{9,1},... | collective-permute-start | bytes 245768 | tf_op jit(solution)/shard_map/ppermute | solution.py:523
  14.9 1.8 %column_adjoint.1.ca_ref = bf16[48,256,128]{2,1,0:T(8,128)(2,1)S(1)} custom-call(f32[384,128]{1,0:T(8,128)S(1)} %taps.1, bf16[8,5,8,128]{3,2,1,0:T(8,128)(2,1)S(1)} %pad_maximum_fusion._), custom_call_target="tpu_custom_call" | custom-call | tf_op jit(solution)/shard_map/column_adjoint/pallas_call | solution.py:130
  16.7 0.6 %collective-permute-done.3 = bf16[8,5,8,128]{3,2,1,0:T(8,128)(2,1)S(1)} collective-permute-done((bf16[8,5,8,128]{3,2,1,0:T(8,128)(2,1)S(1)}, bf16[8,5,8,128]{3,2,1,0:T(8,128)(2,1)S(1)}, u32[]{:S(2)}, u32[]{:S(2)}) %collective-permute-start.3) | collective-permute-done | bytes 81952 | tf_op jit(solution)/shard_map/ppermute | solution.py:523
  17.3 0.0 copy-start
  17.4 0.0 copy-start.1
  17.4 12.9 %imaging.1 = (f32[64,256]{1,0:T(8,128)}, f32[16,4,8,128]{3,2,1,0:T(8,128)S(1)}) custom-call(bf16[80,8,128]{2,1,0:T(8,128)(2,1)S(1)} %bitcast.5, f32[384,128]{1,0:T(8,128)S(1)} %taps.1, bf16[24,512,128]{2,1,0:T(8,128)(2,1)S(1)} %column_bands.1.cf_ref, bf16[48,256,128]{2,1,0:T(8,128)(2,1)S(1)} %column_adjoint.1.ca_ref, f32[12]{0:T(128)} %weight_hbm.1, ...), custom_call_target="tpu_custom_call" | custom-call | tf_op jit(solution)/shard_map/imaging/pallas_call | solution.py:401
  30.2 0.1 collective-permute-start.4
  30.3 1.3 %collective-permute-done.4 = f32[8,4,8,128]{3,2,1,0:T(8,128)S(1)} collective-permute-done((f32[8,4,8,128]{3,2,1,0:T(8,128)S(1)}, f32[8,4,8,128]{3,2,1,0:T(8,128)S(1)}, u32[]{:S(2)}, u32[]{:S(2)}) %collective-permute-start.4) | collective-permute-done | bytes 131104 | tf_op jit(solution)/shard_map/ppermute | solution.py:523
  31.7 1.9 %collective-permute-start.5 = (f32[4,4,8,128]{3,2,1,0:T(8,128)S(1)}, f32[4,4,8,128]{3,2,1,0:T(8,128)S(1)}, u32[]{:S(2)}, u32[]{:S(2)}) collective-permute-start(f32[4,4,8,128]{3,2,1,0:T(8,128)S(1)} %slice.29), channel_id=1, source_target_pairs={{0,2},{1,3},{2,0},{3,1},{4,6},{5,7},{6,4},{7,5},{8,10},{9,11},{10,... | collective-permute-start | bytes 196616 | tf_op jit(solution)/shard_map/ppermute | solution.py:523
  33.6 2.4 %collective-permute-done.5 = f32[4,4,8,128]{3,2,1,0:T(8,128)S(1)} collective-permute-done((f32[4,4,8,128]{3,2,1,0:T(8,128)S(1)}, f32[4,4,8,128]{3,2,1,0:T(8,128)S(1)}, u32[]{:S(2)}, u32[]{:S(2)}) %collective-permute-start.5) | collective-permute-done | bytes 65568 | tf_op jit(solution)/shard_map/ppermute | solution.py:523
  36.0 2.0 %collective-permute-start.6 = (f32[2,4,8,128]{3,2,1,0:T(8,128)S(1)}, f32[2,4,8,128]{3,2,1,0:T(8,128)S(1)}, u32[]{:S(2)}, u32[]{:S(2)}) collective-permute-start(f32[2,4,8,128]{3,2,1,0:T(8,128)S(1)} %slice.31), channel_id=1, source_target_pairs={{0,4},{1,5},{2,6},{3,7},{4,0},{5,1},{6,2},{7,3},{8,12},{9,13},{10,... | collective-permute-start | bytes 98312 | tf_op jit(solution)/shard_map/ppermute | solution.py:523
  38.0 2.0 %collective-permute-done.6 = f32[2,4,8,128]{3,2,1,0:T(8,128)S(1)} collective-permute-done((f32[2,4,8,128]{3,2,1,0:T(8,128)S(1)}, f32[2,4,8,128]{3,2,1,0:T(8,128)S(1)}, u32[]{:S(2)}, u32[]{:S(2)}) %collective-permute-start.6) | collective-permute-done | bytes 32800 | tf_op jit(solution)/shard_map/ppermute | solution.py:523
  40.0 3.3 %collective-permute-start.7 = (f32[1,4,8,128]{3,2,1,0:T(8,128)S(1)}, f32[1,4,8,128]{3,2,1,0:T(8,128)S(1)}, u32[]{:S(2)}, u32[]{:S(2)}) collective-permute-start(f32[1,4,8,128]{3,2,1,0:T(8,128)S(1)} %slice.32), channel_id=1, source_target_pairs={{0,8},{1,9},{2,10},{3,11},{4,12},{5,13},{6,14},{7,15},{8,0},{9,1},... | collective-permute-start | bytes 49160 | tf_op jit(solution)/shard_map/ppermute | solution.py:523
  43.3 1.7 %collective-permute-done.7.sent_ref = f32[1,4,8,128]{3,2,1,0:T(8,128)S(1)} collective-permute-done((f32[1,4,8,128]{3,2,1,0:T(8,128)S(1)}, f32[1,4,8,128]{3,2,1,0:T(8,128)S(1)}, u32[]{:S(2)}, u32[]{:S(2)}) %collective-permute-start.7) | collective-permute-done | bytes 16416 | tf_op jit(solution)/shard_map/ppermute | solution.py:523
  45.1 0.9 %update.1 = (f32[4,1024]{1,0:T(4,128)}, f32[4,1024]{1,0:T(4,128)}) custom-call(f32[2,4,8,128]{3,2,1,0:T(8,128)S(1)} %slice_add_fusion.2.kept_ref, f32[1,4,8,128]{3,2,1,0:T(8,128)S(1)} %collective-permute-done.7.sent_ref, f32[4,1024]{1,0:T(4,128)S(1)} %copy-done.1, f32[4,1024]{1,0:T(4,128)S(1)} %copy-done), custom_call_target="tpu_custom_call" | custom-call | tf_op jit(solution)/shard_map/update/pallas_call | solution.py:508
  (17 shorter events, 0.1 us)
Async XLA Ops:
  1.7 1.5 %collective-permute-start = (bf16[1,5,8,128]{3,2,1,0:T(8,128)(2,1)S(1)}, bf16[1,5,8,128]{3,2,1,0:T(8,128)(2,1)S(1)}, u32[]{:S(2)}, u32[]{:S(2)}) collective-permute-start(bf16[1,5,8,128]{3,2,1,0:T(8,128)(2,1)S(1)} %pack.1), channel_id=1, source_target_pairs={{0,1},{1,0},{2,3},{3,2},{4,5},{5,4},{6,7},{7,6},{8,9},{9,8},{10,11... | collective-permute-start | bytes 30728 | tf_op jit(solution)/shard_map/ppermute | solution.py:523
  3.2 4.5 %collective-permute-start.1 = (bf16[2,5,8,128]{3,2,1,0:T(8,128)(2,1)S(1)}, bf16[2,5,8,128]{3,2,1,0:T(8,128)(2,1)S(1)}, u32[]{:S(2)}, u32[]{:S(2)}) collective-permute-start(bf16[2,5,8,128]{3,2,1,0:T(8,128)(2,1)S(1)} %pad_maximum_fusion.2._), channel_id=1, source_target_pairs={{0,2},{1,3},{2,0},{3,1},{4,6},{5,7},{6,4},{7,5},{8,10},{9,11},{10,... | collective-permute-start | bytes 61448 | tf_op jit(solution)/shard_map/ppermute | solution.py:523
  7.7 4.1 %collective-permute-start.2 = (bf16[4,5,8,128]{3,2,1,0:T(8,128)(2,1)S(1)}, bf16[4,5,8,128]{3,2,1,0:T(8,128)(2,1)S(1)}, u32[]{:S(2)}, u32[]{:S(2)}) collective-permute-start(bf16[4,5,8,128]{3,2,1,0:T(8,128)(2,1)S(1)} %pad_maximum_fusion.1), channel_id=1, source_target_pairs={{0,4},{1,5},{2,6},{3,7},{4,0},{5,1},{6,2},{7,3},{8,12},{9,13},{10,... | collective-permute-start | bytes 122888 | tf_op jit(solution)/shard_map/ppermute | solution.py:523
  11.8 5.5 %collective-permute-start.3 = (bf16[8,5,8,128]{3,2,1,0:T(8,128)(2,1)S(1)}, bf16[8,5,8,128]{3,2,1,0:T(8,128)(2,1)S(1)}, u32[]{:S(2)}, u32[]{:S(2)}) collective-permute-start(bf16[8,5,8,128]{3,2,1,0:T(8,128)(2,1)S(1)} %pad_maximum_fusion._), channel_id=1, source_target_pairs={{0,8},{1,9},{2,10},{3,11},{4,12},{5,13},{6,14},{7,15},{8,0},{9,1},... | collective-permute-start | bytes 245768 | tf_op jit(solution)/shard_map/ppermute | solution.py:523
  17.3 27.7 %copy-start = (f32[4,1024]{1,0:T(4,128)S(1)}, f32[4,1024]{1,0:T(4,128)}, u32[]{:S(2)}) copy-start(f32[4,1024]{1,0:T(4,128)} %masters_ref.3) | copy-start | bytes 49156
  17.4 27.7 %copy-start.1 = (f32[4,1024]{1,0:T(4,128)S(1)}, f32[4,1024]{1,0:T(4,128)}, u32[]{:S(2)}) copy-start(f32[4,1024]{1,0:T(4,128)} %velocity_ref.1) | copy-start | bytes 49156
  30.2 1.4 %collective-permute-start.4 = (f32[8,4,8,128]{3,2,1,0:T(8,128)S(1)}, f32[8,4,8,128]{3,2,1,0:T(8,128)S(1)}, u32[]{:S(2)}, u32[]{:S(2)}) collective-permute-start(f32[8,4,8,128]{3,2,1,0:T(8,128)S(1)} %slice.22), channel_id=1, source_target_pairs={{0,1},{1,0},{2,3},{3,2},{4,5},{5,4},{6,7},{7,6},{8,9},{9,8},{10,11... | collective-permute-start | bytes 393224 | tf_op jit(solution)/shard_map/ppermute | solution.py:523
  31.7 4.3 %collective-permute-start.5 = (f32[4,4,8,128]{3,2,1,0:T(8,128)S(1)}, f32[4,4,8,128]{3,2,1,0:T(8,128)S(1)}, u32[]{:S(2)}, u32[]{:S(2)}) collective-permute-start(f32[4,4,8,128]{3,2,1,0:T(8,128)S(1)} %slice.29), channel_id=1, source_target_pairs={{0,2},{1,3},{2,0},{3,1},{4,6},{5,7},{6,4},{7,5},{8,10},{9,11},{10,... | collective-permute-start | bytes 196616 | tf_op jit(solution)/shard_map/ppermute | solution.py:523
  36.0 4.0 %collective-permute-start.6 = (f32[2,4,8,128]{3,2,1,0:T(8,128)S(1)}, f32[2,4,8,128]{3,2,1,0:T(8,128)S(1)}, u32[]{:S(2)}, u32[]{:S(2)}) collective-permute-start(f32[2,4,8,128]{3,2,1,0:T(8,128)S(1)} %slice.31), channel_id=1, source_target_pairs={{0,4},{1,5},{2,6},{3,7},{4,0},{5,1},{6,2},{7,3},{8,12},{9,13},{10,... | collective-permute-start | bytes 98312 | tf_op jit(solution)/shard_map/ppermute | solution.py:523
  40.0 5.0 %collective-permute-start.7 = (f32[1,4,8,128]{3,2,1,0:T(8,128)S(1)}, f32[1,4,8,128]{3,2,1,0:T(8,128)S(1)}, u32[]{:S(2)}, u32[]{:S(2)}) collective-permute-start(f32[1,4,8,128]{3,2,1,0:T(8,128)S(1)} %slice.32), channel_id=1, source_target_pairs={{0,8},{1,9},{2,10},{3,11},{4,12},{5,13},{6,14},{7,15},{8,0},{9,1},... | collective-permute-start | bytes 49160 | tf_op jit(solution)/shard_map/ppermute | solution.py:523

commit v9 on v8

--- a/solution.py
+++ b/solution.py
@@ -89,6 +89,22 @@
             cf_ref[n, at + BLK : at + EXT, :] = half_band(jnp.where(low, a_far, b))
             cf_ref[n, at + EXT : at + EXT + BLK, :] = half_band(jnp.where(low, -b, a_far))
             cf_ref[n, at + EXT + BLK : at + 2 * EXT, :] = half_band(jnp.where(low, -b_far, a))
+        return carry
+
+    lax.fori_loop(0, 2 * MODES, step, 0, unroll=3)
+
+
+def row_adjoint_kernel(taps, _, rt_ref):
+    low = low_lanes()
+
+    def step(n, carry):
+        first = 2 * MODES * CH + 4 * n
+        for par in range(2):
+            a, a_far, b, b_far = pair(
+                taps[pl.ds(first + par, 1), :], taps[pl.ds(first + 2 + par, 1), :]
+            )
+            rt_ref[n, par * EXT : par * EXT + BLK, :] = half_band(jnp.where(low, a, b_far))
+            rt_ref[n, par * EXT + BLK : (par + 1) * EXT, :] = half_band(jnp.where(low, a_far, b))
         return carry
 
     lax.fori_loop(0, 2 * MODES, step, 0, unroll=3)
@@ -139,6 +155,7 @@
             stages,
             (
                 (column_bands_kernel, (2 * MODES, CH * EXT // 2, LANES), "column_bands"),
+                (row_adjoint_kernel, (2 * MODES, 2 * EXT, LANES), "row_adjoint"),
                 (column_adjoint_kernel, (4 * MODES, 2 * EXT, LANES), "column_adjoint"),
             ),
         )
@@ -155,22 +172,24 @@
     gathered_ref,
     taps,
     cf_ref,
+    rt_ref,
     ca_ref,
     weight_hbm,
     target_hbm,
-    resid_ref,
+    resid_hbm,
     grads_ref,
     *scratch,
 ):
     canvases, grads, sums = scratch[0:3], scratch[3:6], scratch[6:9]
     window, lhs, fields, slope, gw, gys, table, ids, sem = scratch[9:18]
-    weight_ref, target_ref, r_ref, rt_ref, load_sems = scratch[18:]
+    weight_ref, target_ref, resid_ref, r_ref, load_sems = scratch[18:]
     loads = [
         pltpu.make_async_copy(source, target, load_sems.at[n])
         for n, (source, target) in enumerate(
             (
                 (weight_hbm, weight_ref),
                 (target_hbm, target_ref),
+                (resid_ref, resid_hbm),
             )
         )
     ]
@@ -208,7 +227,7 @@
             )[:, :STEP]
     to_scalar = pltpu.make_async_copy(table, ids, sem)
     to_scalar.start()
-    for load in loads:
+    for load in loads[:2]:
         load.start()
     for canvas in canvases:
         canvas[...] = jnp.zeros_like(canvas)
@@ -268,22 +287,10 @@
     lanes16 = lane_iota((16, LANES))
     before = lanes16 < HALF
     until = lanes16 < HALF + BLK
-    low64 = low_lanes()
-
     def row_bands(k):
         for c in range(CH):
             at = k * CH + c
             r_ref[at * BLK : (at + 1) * BLK, :] = half_band(skew(taps[at : at + 1, :], 0))
-
-    def row_adjoint_bands(k):
-        for n in (2 * k, 2 * k + 1):
-            tap = 2 * MODES * CH + 4 * n
-            for par in range(2):
-                one, two = tap + par, tap + 2 + par
-                a, a_far, b, b_far = pair(taps[one : one + 1, :], taps[two : two + 1, :])
-                at = par * EXT
-                rt_ref[n, at : at + BLK, :] = half_band(jnp.where(low64, a, b_far))
-                rt_ref[n, at + BLK : at + EXT, :] = half_band(jnp.where(low64, a_far, b))
 
     loads[0].wait()
     row_bands(0)
@@ -291,7 +298,6 @@
     for k in range(MODES):
         if k + 1 < MODES:
             row_bands(k + 1)
-        row_adjoint_bands(k)
         field_y = jnp.dot(
             r_ref[k * CH * rows : (k + 1) * CH * rows, :],
             window[...],
@@ -311,20 +317,26 @@
         intensity = intensity + weight_ref[k] * (e * e)
     loads[1].wait()
     low_rows = lane_iota((rows, LANES)) < BLK
-    for b in range(NBLK):
-        inten = intensity[b * rows : (b + 1) * rows]
-        inten = inten + pltpu.roll(inten, BLK, 1)
-        t = target_ref[:, (b // 2) * LANES : (b // 2 + 1) * LANES].astype(jnp.float32)
-        other = pltpu.roll(t, BLK, 1)
-        goal = jnp.where(low_rows, t, other) if b % 2 == 0 else jnp.where(low_rows, other, t)
+
+    def halves(x, first):
+        turned = pltpu.roll(x, BLK, 1)
+        return (jnp.where(low_rows, x, turned), jnp.where(low_rows, turned, x))[first]
+
+    for h in range(2):
+        one = intensity[2 * h * rows : (2 * h + 1) * rows]
+        two = intensity[(2 * h + 1) * rows : (2 * h + 2) * rows]
+        inten = jnp.where(
+            low_rows, one + pltpu.roll(one, BLK, 1), two + pltpu.roll(two, BLK, 1)
+        )
+        at = slice(h * LANES, (h + 1) * LANES)
         resist = jax.nn.sigmoid(steepness * (inten - threshold))
-        resid = resist - goal
-        slope[b * rows : (b + 1) * rows, :] = 2.0 * (resid * steepness * resist * (1.0 - resist))
-        if b % 2 == 0:
-            resid_ref[:, (b // 2) * LANES : (b // 2 + 1) * LANES] = resid
-        else:
-            resid_ref[:, (b // 2) * LANES + BLK : (b // 2 + 1) * LANES] = resid[:, BLK:]
-
+        resid = resist - target_ref[:, at].astype(jnp.float32)
+        resid_ref[:, at] = resid
+        change = 2.0 * (resid * steepness * resist * (1.0 - resist))
+        for n in range(2):
+            slope[(2 * h + n) * rows : (2 * h + n + 1) * rows, :] = halves(change, n)
+
+    loads[2].start()
     nothing = jnp.zeros((16, LANES), jnp.float32)
     for k in range(MODES):
         weight = weight_ref[k]
@@ -392,6 +404,7 @@
             gather(j, u)
 
     grads_ref[...] = (sums[0][...] + sums[1][...] + sums[2][...]).reshape(grads_ref.shape)
+    loads[2].wait()
 
 
 def main_step(weights, gathered, target, bands):
@@ -401,11 +414,11 @@
     return pl.pallas_call(
         functools.partial(main_kernel, devices),
         out_shape=(
-            jax.ShapeDtypeStruct(target.shape, jnp.float32),
+            pltpu.HBM(target.shape, jnp.float32),
             pltpu.VMEM((devices, count, 8, LANES), jnp.float32),
         ),
-        in_specs=[vmem] * 4 + [pl.BlockSpec(memory_space=pl.ANY)] * 2,
-        out_specs=[vmem] * 2,
+        in_specs=[vmem] * 5 + [pl.BlockSpec(memory_space=pl.ANY)] * 2,
+        out_specs=[pl.BlockSpec(memory_space=pl.ANY), vmem],
         scratch_shapes=[
             *[pltpu.VMEM((4 * CROWS, LANES), jnp.float32)] * 3,
             *[pltpu.VMEM((4 * W, LANES), jnp.float32)] * 3,
@@ -421,9 +434,9 @@
             pltpu.SemaphoreType.DMA,
             pltpu.SMEM(weights.shape, jnp.float32),
             pltpu.VMEM(target.shape, jnp.bfloat16),
+            pltpu.VMEM(target.shape, jnp.float32),
             pltpu.VMEM((MODES * CH * BLK, LANES), jnp.bfloat16),
-            pltpu.VMEM((2 * MODES, 2 * EXT, LANES), jnp.bfloat16),
-            pltpu.SemaphoreType.DMA((2,)),
+            pltpu.SemaphoreType.DMA((3,)),
         ],
         compiler_params=pltpu.CompilerParams(vmem_limit_bytes=28 << 20),
         name="imaging",
@@ -542,7 +555,7 @@
     for b in range(bits):
         held = jnp.concatenate([held, swap(held, 1 << b, devices)], axis=0)
         stages.append(held)
-    bands = build_bands(row_taps, col_taps, (stages[0], stages[-2]))
+    bands = build_bands(row_taps, col_taps, stages[-4:-1])
     resid, grads = main_step(mode_weights, held, target, bands)
     for b in range(bits):
         half = grads.shape[0] // 2

time: 46.2 us -> 45.6 us (0.987)
  waiting for transfers between devices: 10.1 us -> 8.71 us
  Pallas kernels: 19.2 us -> 20 us
    ppermute x8, waiting for transfers between devices: 10.1 us -> 8.71 us  [swap(): return lax.ppermute(value, 'tx', [(i, i ^ bit) for i in range(devices)])]
    pallas_call x2 -> x3, Pallas kernels: 3.54 us -> 4.91 us  [build_bands(): pl.pallas_call(kernel, out_shape=pltpu.VMEM(shape, jnp.bfloat16), in_spec...]
    pallas_call x1, Pallas kernels: 12.9 us -> 12.3 us  [main_step(): pl.pallas_call(functools.partial(main_kernel, devices), out_shape=(pltpu....]
  transfers between devices with their start and end apart: 8 -> 8, of which waited for: 6 -> 6; matrix products, arithmetic and copies ran while one was open for 0% -> 0% of each run, Pallas kernels for 10% -> 13%
where the time goes in v9:
time: 45.6 us; the launch traced here: 45.4 us
  Pallas kernels  20 us (44%)
  starting transfers between devices  15.7 us (34%)
  waiting for transfers between devices  8.71 us (19%)
  between operations  0.77 us (2%)
    ppermute x8, starting transfers between devices, swap(): return lax.ppermute(value, 'tx', [(i, i ^ bit) for i in range(devices)])  15.7 us
    pallas_call x1, Pallas kernels, main_step(): pl.pallas_call(functools.partial(main_kernel, devices), out_shape=(pltpu....  12.3 us
    ppermute x8, waiting for transfers between devices, swap(): return lax.ppermute(value, 'tx', [(i, i ^ bit) for i in range(devices)])  8.71 us
    pallas_call x3, Pallas kernels, build_bands(): pl.pallas_call(kernel, out_shape=pltpu.VMEM(shape, jnp.bfloat16), in_spec...  4.91 us
    pallas_call x1, Pallas kernels, pack(): pl.pallas_call(pack_kernel, out_shape=pltpu.VMEM((1, count + 1, 8, LANES)...  1.02 us
    pallas_call x1, Pallas kernels, build_bands(): pl.pallas_call(taps_kernel, out_shape=pltpu.VMEM((4 * MODES * CH, LANES),...  0.93 us
  transfers between devices with their start and end apart: 8, of which 6 were waited for; matrix products, arithmetic and copies ran while one was open for 0% of the time, Pallas kernels for 13%

profile of v9, /device:TPU:0, one launch (start us, length us, event | category | flops | bytes accessed | tf_op | source)
XLA Modules:
  0.0 45.4 jit_solution(4278070949155235017)
XLA Ops:
  0.6 1.0 %pack.1 = bf16[1,5,8,128]{3,2,1,0:T(8,128)(2,1)S(1)} custom-call(f32[4,1024]{1,0:T(4,128)} %masters_ref.3, s32[1,128]{1,0:T(1,128)} %bitcast.6, s32[1,128]{1,0:T(1,128)} %bitcast.7, s32[1,128]{1,0:T(1,128)} %bitcast.8, s32[1,128]{1,0:T(1,128)} %bitcast.9), custom_call_target="tpu_custom_call" | custom-call | tf_op jit(solution)/shard_map/pack/pallas_call | solution.py:490
  1.7 0.6 %collective-permute-start = (bf16[1,5,8,128]{3,2,1,0:T(8,128)(2,1)S(1)}, bf16[1,5,8,128]{3,2,1,0:T(8,128)(2,1)S(1)}, u32[]{:S(2)}, u32[]{:S(2)}) collective-permute-start(bf16[1,5,8,128]{3,2,1,0:T(8,128)(2,1)S(1)} %pack.1), channel_id=1, source_target_pairs={{0,1},{1,0},{2,3},{3,2},{4,5},{5,4},{6,7},{7,6},{8,9},{9,8},{10,11... | collective-permute-start | bytes 30728 | tf_op jit(solution)/shard_map/ppermute | solution.py:536
  2.2 0.9 %taps.1 = f32[384,128]{1,0:T(8,128)S(1)} custom-call(bf16[12,4,2,63]{3,2,1,0:T(2,128)(2,1)} %row_ref.1, bf16[12,4,2,63]{3,2,1,0:T(2,128)(2,1)} %col_ref.1), custom_call_target="tpu_custom_call" | custom-call | tf_op jit(solution)/shard_map/taps/pallas_call | solution.py:136
  3.2 2.7 %collective-permute-start.1 = (bf16[2,5,8,128]{3,2,1,0:T(8,128)(2,1)S(1)}, bf16[2,5,8,128]{3,2,1,0:T(8,128)(2,1)S(1)}, u32[]{:S(2)}, u32[]{:S(2)}) collective-permute-start(bf16[2,5,8,128]{3,2,1,0:T(8,128)(2,1)S(1)} %pad_maximum_fusion.2._), channel_id=1, source_target_pairs={{0,2},{1,3},{2,0},{3,1},{4,6},{5,7},{6,4},{7,5},{8,10},{9,11},{10,... | collective-permute-start | bytes 61448 | tf_op jit(solution)/shard_map/ppermute | solution.py:536
  5.9 1.8 %column_bands.1.cf_ref = bf16[24,512,128]{2,1,0:T(8,128)(2,1)S(1)} custom-call(f32[384,128]{1,0:T(8,128)S(1)} %taps.1, bf16[2,5,8,128]{3,2,1,0:T(8,128)(2,1)S(1)} %pad_maximum_fusion.2._), custom_call_target="tpu_custom_call" | custom-call | tf_op jit(solution)/shard_map/column_bands/pallas_call | solution.py:146
  7.7 0.0 collective-permute-done.1
  7.7 2.1 %collective-permute-start.2 = (bf16[4,5,8,128]{3,2,1,0:T(8,128)(2,1)S(1)}, bf16[4,5,8,128]{3,2,1,0:T(8,128)(2,1)S(1)}, u32[]{:S(2)}, u32[]{:S(2)}) collective-permute-start(bf16[4,5,8,128]{3,2,1,0:T(8,128)(2,1)S(1)} %pad_maximum_fusion.1._), channel_id=1, source_target_pairs={{0,4},{1,5},{2,6},{3,7},{4,0},{5,1},{6,2},{7,3},{8,12},{9,13},{10,... | collective-permute-start | bytes 122888 | tf_op jit(solution)/shard_map/ppermute | solution.py:536
  9.8 1.4 %row_adjoint.1.rt_ref = bf16[24,256,128]{2,1,0:T(8,128)(2,1)S(1)} custom-call(f32[384,128]{1,0:T(8,128)S(1)} %taps.1, bf16[4,5,8,128]{3,2,1,0:T(8,128)(2,1)S(1)} %pad_maximum_fusion.1._), custom_call_target="tpu_custom_call" | custom-call | tf_op jit(solution)/shard_map/row_adjoint/pallas_call | solution.py:146
  11.2 0.6 %collective-permute-done.2 = bf16[4,5,8,128]{3,2,1,0:T(8,128)(2,1)S(1)} collective-permute-done((bf16[4,5,8,128]{3,2,1,0:T(8,128)(2,1)S(1)}, bf16[4,5,8,128]{3,2,1,0:T(8,128)(2,1)S(1)}, u32[]{:S(2)}, u32[]{:S(2)}) %collective-permute-start.2) | collective-permute-done | bytes 40992 | tf_op jit(solution)/shard_map/ppermute | solution.py:536
  11.8 3.1 %collective-permute-start.3 = (bf16[8,5,8,128]{3,2,1,0:T(8,128)(2,1)S(1)}, bf16[8,5,8,128]{3,2,1,0:T(8,128)(2,1)S(1)}, u32[]{:S(2)}, u32[]{:S(2)}) collective-permute-start(bf16[8,5,8,128]{3,2,1,0:T(8,128)(2,1)S(1)} %pad_maximum_fusion._), channel_id=1, source_target_pairs={{0,8},{1,9},{2,10},{3,11},{4,12},{5,13},{6,14},{7,15},{8,0},{9,1},... | collective-permute-start | bytes 245768 | tf_op jit(solution)/shard_map/ppermute | solution.py:536
  14.9 1.8 %column_adjoint.1.ca_ref = bf16[48,256,128]{2,1,0:T(8,128)(2,1)S(1)} custom-call(f32[384,128]{1,0:T(8,128)S(1)} %taps.1, bf16[8,5,8,128]{3,2,1,0:T(8,128)(2,1)S(1)} %pad_maximum_fusion._), custom_call_target="tpu_custom_call" | custom-call | tf_op jit(solution)/shard_map/column_adjoint/pallas_call | solution.py:146
  16.7 0.6 %collective-permute-done.3 = bf16[8,5,8,128]{3,2,1,0:T(8,128)(2,1)S(1)} collective-permute-done((bf16[8,5,8,128]{3,2,1,0:T(8,128)(2,1)S(1)}, bf16[8,5,8,128]{3,2,1,0:T(8,128)(2,1)S(1)}, u32[]{:S(2)}, u32[]{:S(2)}) %collective-permute-start.3) | collective-permute-done | bytes 81952 | tf_op jit(solution)/shard_map/ppermute | solution.py:536
  17.3 0.0 copy-start
  17.4 0.0 copy-start.1
  17.4 12.3 %imaging.1 = (f32[64,256]{1,0:T(8,128)}, f32[16,4,8,128]{3,2,1,0:T(8,128)S(1)}) custom-call(bf16[80,8,128]{2,1,0:T(8,128)(2,1)S(1)} %bitcast.5, f32[384,128]{1,0:T(8,128)S(1)} %taps.1, bf16[24,512,128]{2,1,0:T(8,128)(2,1)S(1)} %column_bands.1.cf_ref, bf16[24,256,128]{2,1,0:T(8,128)(2,1)S(1)} %row_adjoint.1.rt_ref, ...), custom_call_target="tpu_custom_call" | custom-call | tf_op jit(solution)/shard_map/imaging/pallas_call | solution.py:414
  29.7 0.1 collective-permute-start.4
  29.7 1.3 %collective-permute-done.4 = f32[8,4,8,128]{3,2,1,0:T(8,128)S(1)} collective-permute-done((f32[8,4,8,128]{3,2,1,0:T(8,128)S(1)}, f32[8,4,8,128]{3,2,1,0:T(8,128)S(1)}, u32[]{:S(2)}, u32[]{:S(2)}) %collective-permute-start.4) | collective-permute-done | bytes 131104 | tf_op jit(solution)/shard_map/ppermute | solution.py:536
  31.1 1.9 %collective-permute-start.5 = (f32[4,4,8,128]{3,2,1,0:T(8,128)S(1)}, f32[4,4,8,128]{3,2,1,0:T(8,128)S(1)}, u32[]{:S(2)}, u32[]{:S(2)}) collective-permute-start(f32[4,4,8,128]{3,2,1,0:T(8,128)S(1)} %slice.29), channel_id=1, source_target_pairs={{0,2},{1,3},{2,0},{3,1},{4,6},{5,7},{6,4},{7,5},{8,10},{9,11},{10,... | collective-permute-start | bytes 196616 | tf_op jit(solution)/shard_map/ppermute | solution.py:536
  33.0 2.4 %collective-permute-done.5 = f32[4,4,8,128]{3,2,1,0:T(8,128)S(1)} collective-permute-done((f32[4,4,8,128]{3,2,1,0:T(8,128)S(1)}, f32[4,4,8,128]{3,2,1,0:T(8,128)S(1)}, u32[]{:S(2)}, u32[]{:S(2)}) %collective-permute-start.5) | collective-permute-done | bytes 65568 | tf_op jit(solution)/shard_map/ppermute | solution.py:536
  35.5 2.0 %collective-permute-start.6 = (f32[2,4,8,128]{3,2,1,0:T(8,128)S(1)}, f32[2,4,8,128]{3,2,1,0:T(8,128)S(1)}, u32[]{:S(2)}, u32[]{:S(2)}) collective-permute-start(f32[2,4,8,128]{3,2,1,0:T(8,128)S(1)} %slice.31), channel_id=1, source_target_pairs={{0,4},{1,5},{2,6},{3,7},{4,0},{5,1},{6,2},{7,3},{8,12},{9,13},{10,... | collective-permute-start | bytes 98312 | tf_op jit(solution)/shard_map/ppermute | solution.py:536
  37.4 2.0 %collective-permute-done.6 = f32[2,4,8,128]{3,2,1,0:T(8,128)S(1)} collective-permute-done((f32[2,4,8,128]{3,2,1,0:T(8,128)S(1)}, f32[2,4,8,128]{3,2,1,0:T(8,128)S(1)}, u32[]{:S(2)}, u32[]{:S(2)}) %collective-permute-start.6) | collective-permute-done | bytes 32800 | tf_op jit(solution)/shard_map/ppermute | solution.py:536
  39.5 3.3 %collective-permute-start.7 = (f32[1,4,8,128]{3,2,1,0:T(8,128)S(1)}, f32[1,4,8,128]{3,2,1,0:T(8,128)S(1)}, u32[]{:S(2)}, u32[]{:S(2)}) collective-permute-start(f32[1,4,8,128]{3,2,1,0:T(8,128)S(1)} %slice.32), channel_id=1, source_target_pairs={{0,8},{1,9},{2,10},{3,11},{4,12},{5,13},{6,14},{7,15},{8,0},{9,1},... | collective-permute-start | bytes 49160 | tf_op jit(solution)/shard_map/ppermute | solution.py:536
  42.8 1.7 %collective-permute-done.7.sent_ref = f32[1,4,8,128]{3,2,1,0:T(8,128)S(1)} collective-permute-done((f32[1,4,8,128]{3,2,1,0:T(8,128)S(1)}, f32[1,4,8,128]{3,2,1,0:T(8,128)S(1)}, u32[]{:S(2)}, u32[]{:S(2)}) %collective-permute-start.7) | collective-permute-done | bytes 16416 | tf_op jit(solution)/shard_map/ppermute | solution.py:536
  44.5 0.9 %update.1 = (f32[4,1024]{1,0:T(4,128)}, f32[4,1024]{1,0:T(4,128)}) custom-call(f32[2,4,8,128]{3,2,1,0:T(8,128)S(1)} %slice_add_fusion.2.kept_ref, f32[1,4,8,128]{3,2,1,0:T(8,128)S(1)} %collective-permute-done.7.sent_ref, f32[4,1024]{1,0:T(4,128)S(1)} %copy-done.1, f32[4,1024]{1,0:T(4,128)S(1)} %copy-done), custom_call_target="tpu_custom_call" | custom-call | tf_op jit(solution)/shard_map/update/pallas_call | solution.py:521
  (18 shorter events, 0.1 us)
Async XLA Ops:
  1.7 1.5 %collective-permute-start = (bf16[1,5,8,128]{3,2,1,0:T(8,128)(2,1)S(1)}, bf16[1,5,8,128]{3,2,1,0:T(8,128)(2,1)S(1)}, u32[]{:S(2)}, u32[]{:S(2)}) collective-permute-start(bf16[1,5,8,128]{3,2,1,0:T(8,128)(2,1)S(1)} %pack.1), channel_id=1, source_target_pairs={{0,1},{1,0},{2,3},{3,2},{4,5},{5,4},{6,7},{7,6},{8,9},{9,8},{10,11... | collective-permute-start | bytes 30728 | tf_op jit(solution)/shard_map/ppermute | solution.py:536
  3.2 4.5 %collective-permute-start.1 = (bf16[2,5,8,128]{3,2,1,0:T(8,128)(2,1)S(1)}, bf16[2,5,8,128]{3,2,1,0:T(8,128)(2,1)S(1)}, u32[]{:S(2)}, u32[]{:S(2)}) collective-permute-start(bf16[2,5,8,128]{3,2,1,0:T(8,128)(2,1)S(1)} %pad_maximum_fusion.2._), channel_id=1, source_target_pairs={{0,2},{1,3},{2,0},{3,1},{4,6},{5,7},{6,4},{7,5},{8,10},{9,11},{10,... | collective-permute-start | bytes 61448 | tf_op jit(solution)/shard_map/ppermute | solution.py:536
  7.7 4.1 %collective-permute-start.2 = (bf16[4,5,8,128]{3,2,1,0:T(8,128)(2,1)S(1)}, bf16[4,5,8,128]{3,2,1,0:T(8,128)(2,1)S(1)}, u32[]{:S(2)}, u32[]{:S(2)}) collective-permute-start(bf16[4,5,8,128]{3,2,1,0:T(8,128)(2,1)S(1)} %pad_maximum_fusion.1._), channel_id=1, source_target_pairs={{0,4},{1,5},{2,6},{3,7},{4,0},{5,1},{6,2},{7,3},{8,12},{9,13},{10,... | collective-permute-start | bytes 122888 | tf_op jit(solution)/shard_map/ppermute | solution.py:536
  11.8 5.5 %collective-permute-start.3 = (bf16[8,5,8,128]{3,2,1,0:T(8,128)(2,1)S(1)}, bf16[8,5,8,128]{3,2,1,0:T(8,128)(2,1)S(1)}, u32[]{:S(2)}, u32[]{:S(2)}) collective-permute-start(bf16[8,5,8,128]{3,2,1,0:T(8,128)(2,1)S(1)} %pad_maximum_fusion._), channel_id=1, source_target_pairs={{0,8},{1,9},{2,10},{3,11},{4,12},{5,13},{6,14},{7,15},{8,0},{9,1},... | collective-permute-start | bytes 245768 | tf_op jit(solution)/shard_map/ppermute | solution.py:536
  17.3 27.1 %copy-start = (f32[4,1024]{1,0:T(4,128)S(1)}, f32[4,1024]{1,0:T(4,128)}, u32[]{:S(2)}) copy-start(f32[4,1024]{1,0:T(4,128)} %masters_ref.3) | copy-start | bytes 49156
  17.4 27.1 %copy-start.1 = (f32[4,1024]{1,0:T(4,128)S(1)}, f32[4,1024]{1,0:T(4,128)}, u32[]{:S(2)}) copy-start(f32[4,1024]{1,0:T(4,128)} %velocity_ref.1) | copy-start | bytes 49156
  29.7 1.4 %collective-permute-start.4 = (f32[8,4,8,128]{3,2,1,0:T(8,128)S(1)}, f32[8,4,8,128]{3,2,1,0:T(8,128)S(1)}, u32[]{:S(2)}, u32[]{:S(2)}) collective-permute-start(f32[8,4,8,128]{3,2,1,0:T(8,128)S(1)} %slice.22), channel_id=1, source_target_pairs={{0,1},{1,0},{2,3},{3,2},{4,5},{5,4},{6,7},{7,6},{8,9},{9,8},{10,11... | collective-permute-start | bytes 393224 | tf_op jit(solution)/shard_map/ppermute | solution.py:536
  31.1 4.3 %collective-permute-start.5 = (f32[4,4,8,128]{3,2,1,0:T(8,128)S(1)}, f32[4,4,8,128]{3,2,1,0:T(8,128)S(1)}, u32[]{:S(2)}, u32[]{:S(2)}) collective-permute-start(f32[4,4,8,128]{3,2,1,0:T(8,128)S(1)} %slice.29), channel_id=1, source_target_pairs={{0,2},{1,3},{2,0},{3,1},{4,6},{5,7},{6,4},{7,5},{8,10},{9,11},{10,... | collective-permute-start | bytes 196616 | tf_op jit(solution)/shard_map/ppermute | solution.py:536
  35.5 4.0 %collective-permute-start.6 = (f32[2,4,8,128]{3,2,1,0:T(8,128)S(1)}, f32[2,4,8,128]{3,2,1,0:T(8,128)S(1)}, u32[]{:S(2)}, u32[]{:S(2)}) collective-permute-start(f32[2,4,8,128]{3,2,1,0:T(8,128)S(1)} %slice.31), channel_id=1, source_target_pairs={{0,4},{1,5},{2,6},{3,7},{4,0},{5,1},{6,2},{7,3},{8,12},{9,13},{10,... | collective-permute-start | bytes 98312 | tf_op jit(solution)/shard_map/ppermute | solution.py:536
  39.5 5.0 %collective-permute-start.7 = (f32[1,4,8,128]{3,2,1,0:T(8,128)S(1)}, f32[1,4,8,128]{3,2,1,0:T(8,128)S(1)}, u32[]{:S(2)}, u32[]{:S(2)}) collective-permute-start(f32[1,4,8,128]{3,2,1,0:T(8,128)S(1)} %slice.32), channel_id=1, source_target_pairs={{0,8},{1,9},{2,10},{3,11},{4,12},{5,13},{6,14},{7,15},{8,0},{9,1},... | collective-permute-start | bytes 49160 | tf_op jit(solution)/shard_map/ppermute | solution.py:536

commit v10 on v9

--- a/solution.py
+++ b/solution.py
@@ -89,22 +89,6 @@
             cf_ref[n, at + BLK : at + EXT, :] = half_band(jnp.where(low, a_far, b))
             cf_ref[n, at + EXT : at + EXT + BLK, :] = half_band(jnp.where(low, -b, a_far))
             cf_ref[n, at + EXT + BLK : at + 2 * EXT, :] = half_band(jnp.where(low, -b_far, a))
-        return carry
-
-    lax.fori_loop(0, 2 * MODES, step, 0, unroll=3)
-
-
-def row_adjoint_kernel(taps, _, rt_ref):
-    low = low_lanes()
-
-    def step(n, carry):
-        first = 2 * MODES * CH + 4 * n
-        for par in range(2):
-            a, a_far, b, b_far = pair(
-                taps[pl.ds(first + par, 1), :], taps[pl.ds(first + 2 + par, 1), :]
-            )
-            rt_ref[n, par * EXT : par * EXT + BLK, :] = half_band(jnp.where(low, a, b_far))
-            rt_ref[n, par * EXT + BLK : (par + 1) * EXT, :] = half_band(jnp.where(low, a_far, b))
         return carry
 
     lax.fori_loop(0, 2 * MODES, step, 0, unroll=3)
@@ -155,7 +139,6 @@
             stages,
             (
                 (column_bands_kernel, (2 * MODES, CH * EXT // 2, LANES), "column_bands"),
-                (row_adjoint_kernel, (2 * MODES, 2 * EXT, LANES), "row_adjoint"),
                 (column_adjoint_kernel, (4 * MODES, 2 * EXT, LANES), "column_adjoint"),
             ),
         )
@@ -172,7 +155,6 @@
     gathered_ref,
     taps,
     cf_ref,
-    rt_ref,
     ca_ref,
     weight_hbm,
     target_hbm,
@@ -182,7 +164,7 @@
 ):
     canvases, grads, sums = scratch[0:3], scratch[3:6], scratch[6:9]
     window, lhs, fields, slope, gw, gys, table, ids, sem = scratch[9:18]
-    weight_ref, target_ref, resid_ref, r_ref, load_sems = scratch[18:]
+    weight_ref, target_ref, resid_ref, r_ref, rt_ref, load_sems = scratch[18:]
     loads = [
         pltpu.make_async_copy(source, target, load_sems.at[n])
         for n, (source, target) in enumerate(
@@ -203,15 +185,15 @@
     for n, (other, missing) in enumerate(
         ((me, 0), (jnp.maximum(me - 1, 0), 0), (jnp.minimum(me + 1, devices - 1), BLK - MS))
     ):
-        slab = gathered_ref[(other ^ me) * slabs + count].astype(jnp.float32).astype(jnp.int32)
-        owner, local, row, col = slab[0:1] ^ me, slab[1:2], slab[2:3], slab[3:4]
+        slab = gathered_ref[reversed_bits(other ^ me, bits) * slabs + count].astype(jnp.float32).astype(jnp.int32)
+        owner, local, row, col = reversed_bits(slab[0:1] ^ me, bits), slab[1:2], slab[2:3], slab[3:4]
         if n:
             row = jnp.where(other == me, missing, row)
         first_lane = (row + bases[n]) & 127
         lines = jnp.concatenate(
             [
                 owner * slabs + local,
-                reversed_bits(owner, bits) * count + local,
+                owner * count + local,
                 col + HALF,
                 first_lane,
                 col,
@@ -292,12 +274,25 @@
             at = k * CH + c
             r_ref[at * BLK : (at + 1) * BLK, :] = half_band(skew(taps[at : at + 1, :], 0))
 
+    low64 = low_lanes()
+
+    def row_adjoint_bands(k):
+        for n in (2 * k, 2 * k + 1):
+            tap = 2 * MODES * CH + 4 * n
+            for par in range(2):
+                one, two = tap + par, tap + 2 + par
+                a, a_far, b, b_far = pair(taps[one : one + 1, :], taps[two : two + 1, :])
+                at = par * EXT
+                rt_ref[n, at : at + BLK, :] = half_band(jnp.where(low64, a, b_far))
+                rt_ref[n, at + BLK : at + EXT, :] = half_band(jnp.where(low64, a_far, b))
+
     loads[0].wait()
     row_bands(0)
     intensity = jnp.zeros((NBLK * rows, LANES), jnp.float32)
     for k in range(MODES):
         if k + 1 < MODES:
             row_bands(k + 1)
+        row_adjoint_bands(k)
         field_y = jnp.dot(
             r_ref[k * CH * rows : (k + 1) * CH * rows, :],
             window[...],
@@ -417,7 +412,7 @@
             pltpu.HBM(target.shape, jnp.float32),
             pltpu.VMEM((devices, count, 8, LANES), jnp.float32),
         ),
-        in_specs=[vmem] * 5 + [pl.BlockSpec(memory_space=pl.ANY)] * 2,
+        in_specs=[vmem] * 4 + [pl.BlockSpec(memory_space=pl.ANY)] * 2,
         out_specs=[pl.BlockSpec(memory_space=pl.ANY), vmem],
         scratch_shapes=[
             *[pltpu.VMEM((4 * CROWS, LANES), jnp.float32)] * 3,
@@ -436,6 +431,7 @@
             pltpu.VMEM(target.shape, jnp.bfloat16),
             pltpu.VMEM(target.shape, jnp.float32),
             pltpu.VMEM((MODES * CH * BLK, LANES), jnp.bfloat16),
+            pltpu.VMEM((2 * MODES, 2 * EXT, LANES), jnp.bfloat16),
             pltpu.SemaphoreType.DMA((3,)),
         ],
         compiler_params=pltpu.CompilerParams(vmem_limit_bytes=28 << 20),
@@ -552,10 +548,10 @@
     bits = devices.bit_length() - 1
     held = pack(masters, place_owner, place_local, place_row, place_col)
     stages = []
-    for b in range(bits):
+    for b in reversed(range(bits)):
         held = jnp.concatenate([held, swap(held, 1 << b, devices)], axis=0)
         stages.append(held)
-    bands = build_bands(row_taps, col_taps, stages[-4:-1])
+    bands = build_bands(row_taps, col_taps, stages[-4:-2])
     resid, grads = main_step(mode_weights, held, target, bands)
     for b in range(bits):
         half = grads.shape[0] // 2

time: 45.6 us -> 44.7 us (0.980)
  Pallas kernels: 20 us -> 18.7 us
  waiting for transfers between devices: 8.71 us -> 9.77 us
  starting transfers between devices: 15.7 us -> 15.1 us
    pallas_call x3 -> x2, Pallas kernels: 4.91 us -> 3.54 us  [build_bands(): pl.pallas_call(kernel, out_shape=pltpu.VMEM(shape, jnp.bfloat16), in_spec...]
    ppermute x8, waiting for transfers between devices: 8.71 us -> 9.77 us  [swap(): return lax.ppermute(value, 'tx', [(i, i ^ bit) for i in range(devices)])]
    ppermute x8, starting transfers between devices: 15.7 us -> 15.1 us  [swap(): return lax.ppermute(value, 'tx', [(i, i ^ bit) for i in range(devices)])]
  transfers between devices with their start and end apart: 8 -> 8, of which waited for: 6 -> 8; matrix products, arithmetic and copies ran while one was open for 0% -> 0% of each run, Pallas kernels for 13% -> 10%
where the time goes in v10:
time: 44.7 us; the launch traced here: 44.4 us
  Pallas kernels  18.7 us (42%)
  starting transfers between devices  15.1 us (34%)
  waiting for transfers between devices  9.77 us (22%)
  between operations  0.74 us (2%)
    ppermute x8, starting transfers between devices, swap(): return lax.ppermute(value, 'tx', [(i, i ^ bit) for i in range(devices)])  15.1 us
    pallas_call x1, Pallas kernels, main_step(): pl.pallas_call(functools.partial(main_kernel, devices), out_shape=(pltpu....  12.3 us
    ppermute x8, waiting for transfers between devices, swap(): return lax.ppermute(value, 'tx', [(i, i ^ bit) for i in range(devices)])  9.77 us
    pallas_call x2, Pallas kernels, build_bands(): pl.pallas_call(kernel, out_shape=pltpu.VMEM(shape, jnp.bfloat16), in_spec...  3.54 us
    pallas_call x1, Pallas kernels, pack(): pl.pallas_call(pack_kernel, out_shape=pltpu.VMEM((1, count + 1, 8, LANES)...  1.02 us
    pallas_call x1, Pallas kernels, build_bands(): pl.pallas_call(taps_kernel, out_shape=pltpu.VMEM((4 * MODES * CH, LANES),...  0.93 us
  transfers between devices with their start and end apart: 8, of which 8 were waited for; matrix products, arithmetic and copies ran while one was open for 0% of the time, Pallas kernels for 10%

profile of v10, /device:TPU:0, one launch (start us, length us, event | category | flops | bytes accessed | tf_op | source)
XLA Modules:
  0.0 44.4 jit_solution(7670084750985229368)
XLA Ops:
  0.6 1.0 %pack.1 = bf16[1,5,8,128]{3,2,1,0:T(8,128)(2,1)S(1)} custom-call(f32[4,1024]{1,0:T(4,128)} %masters_ref.3, s32[1,128]{1,0:T(1,128)} %bitcast.6, s32[1,128]{1,0:T(1,128)} %bitcast.7, s32[1,128]{1,0:T(1,128)} %bitcast.8, s32[1,128]{1,0:T(1,128)} %bitcast.9), custom_call_target="tpu_custom_call" | custom-call | tf_op jit(solution)/shard_map/pack/pallas_call | solution.py:486
  1.7 4.1 %collective-permute-start = (bf16[1,5,8,128]{3,2,1,0:T(8,128)(2,1)S(1)}, bf16[1,5,8,128]{3,2,1,0:T(8,128)(2,1)S(1)}, u32[]{:S(2)}, u32[]{:S(2)}) collective-permute-start(bf16[1,5,8,128]{3,2,1,0:T(8,128)(2,1)S(1)} %pack.1), channel_id=1, source_target_pairs={{0,8},{1,9},{2,10},{3,11},{4,12},{5,13},{6,14},{7,15},{8,0},{9,1},... | collective-permute-start | bytes 30728 | tf_op jit(solution)/shard_map/ppermute | solution.py:532
  5.8 0.9 %taps.1 = f32[384,128]{1,0:T(8,128)S(1)} custom-call(bf16[12,4,2,63]{3,2,1,0:T(2,128)(2,1)} %row_ref.1, bf16[12,4,2,63]{3,2,1,0:T(2,128)(2,1)} %col_ref.1), custom_call_target="tpu_custom_call" | custom-call | tf_op jit(solution)/shard_map/taps/pallas_call | solution.py:120
  6.7 0.7 %collective-permute-done = bf16[1,5,8,128]{3,2,1,0:T(8,128)(2,1)S(1)} collective-permute-done((bf16[1,5,8,128]{3,2,1,0:T(8,128)(2,1)S(1)}, bf16[1,5,8,128]{3,2,1,0:T(8,128)(2,1)S(1)}, u32[]{:S(2)}, u32[]{:S(2)}) %collective-permute-start) | collective-permute-done | bytes 10272 | tf_op jit(solution)/shard_map/ppermute | solution.py:532
  7.4 1.9 %collective-permute-start.1 = (bf16[2,5,8,128]{3,2,1,0:T(8,128)(2,1)S(1)}, bf16[2,5,8,128]{3,2,1,0:T(8,128)(2,1)S(1)}, u32[]{:S(2)}, u32[]{:S(2)}) collective-permute-start(bf16[2,5,8,128]{3,2,1,0:T(8,128)(2,1)S(1)} %pad_maximum_fusion.2._), channel_id=1, source_target_pairs={{0,4},{1,5},{2,6},{3,7},{4,0},{5,1},{6,2},{7,3},{8,12},{9,13},{10,... | collective-permute-start | bytes 61448 | tf_op jit(solution)/shard_map/ppermute | solution.py:532
  9.4 1.8 %column_bands.1.cf_ref = bf16[24,512,128]{2,1,0:T(8,128)(2,1)S(1)} custom-call(f32[384,128]{1,0:T(8,128)S(1)} %taps.1, bf16[2,5,8,128]{3,2,1,0:T(8,128)(2,1)S(1)} %pad_maximum_fusion.2._), custom_call_target="tpu_custom_call" | custom-call | tf_op jit(solution)/shard_map/column_bands/pallas_call | solution.py:130
  11.1 0.1 collective-permute-done.1
  11.2 1.9 %collective-permute-start.2 = (bf16[4,5,8,128]{3,2,1,0:T(8,128)(2,1)S(1)}, bf16[4,5,8,128]{3,2,1,0:T(8,128)(2,1)S(1)}, u32[]{:S(2)}, u32[]{:S(2)}) collective-permute-start(bf16[4,5,8,128]{3,2,1,0:T(8,128)(2,1)S(1)} %pad_maximum_fusion.1._), channel_id=1, source_target_pairs={{0,2},{1,3},{2,0},{3,1},{4,6},{5,7},{6,4},{7,5},{8,10},{9,11},{10,... | collective-permute-start | bytes 122888 | tf_op jit(solution)/shard_map/ppermute | solution.py:532
  13.2 1.8 %column_adjoint.1.ca_ref = bf16[48,256,128]{2,1,0:T(8,128)(2,1)S(1)} custom-call(f32[384,128]{1,0:T(8,128)S(1)} %taps.1, bf16[4,5,8,128]{3,2,1,0:T(8,128)(2,1)S(1)} %pad_maximum_fusion.1._), custom_call_target="tpu_custom_call" | custom-call | tf_op jit(solution)/shard_map/column_adjoint/pallas_call | solution.py:130
  14.9 0.4 collective-permute-done.2
  15.3 0.1 collective-permute-start.3
  15.4 1.2 %collective-permute-done.3 = bf16[8,5,8,128]{3,2,1,0:T(8,128)(2,1)S(1)} collective-permute-done((bf16[8,5,8,128]{3,2,1,0:T(8,128)(2,1)S(1)}, bf16[8,5,8,128]{3,2,1,0:T(8,128)(2,1)S(1)}, u32[]{:S(2)}, u32[]{:S(2)}) %collective-permute-start.3) | collective-permute-done | bytes 81952 | tf_op jit(solution)/shard_map/ppermute | solution.py:532
  16.7 0.0 copy-start
  16.7 0.0 copy-start.1
  16.7 12.3 %imaging.1 = (f32[64,256]{1,0:T(8,128)}, f32[16,4,8,128]{3,2,1,0:T(8,128)S(1)}) custom-call(bf16[80,8,128]{2,1,0:T(8,128)(2,1)S(1)} %bitcast.5, f32[384,128]{1,0:T(8,128)S(1)} %taps.1, bf16[24,512,128]{2,1,0:T(8,128)(2,1)S(1)} %column_bands.1.cf_ref, bf16[48,256,128]{2,1,0:T(8,128)(2,1)S(1)} %column_adjoint.1.ca_ref, f32[12]{0:T(128)} %weight_hbm.1, ...), custom_call_target="tpu_custom_call" | custom-call | tf_op jit(solution)/shard_map/imaging/pallas_call | solution.py:409
  29.0 0.2 collective-permute-start.4
  29.2 1.2 %collective-permute-done.4 = f32[8,4,8,128]{3,2,1,0:T(8,128)S(1)} collective-permute-done((f32[8,4,8,128]{3,2,1,0:T(8,128)S(1)}, f32[8,4,8,128]{3,2,1,0:T(8,128)S(1)}, u32[]{:S(2)}, u32[]{:S(2)}) %collective-permute-start.4) | collective-permute-done | bytes 131104 | tf_op jit(solution)/shard_map/ppermute | solution.py:532
  30.5 1.9 %collective-permute-start.5 = (f32[4,4,8,128]{3,2,1,0:T(8,128)S(1)}, f32[4,4,8,128]{3,2,1,0:T(8,128)S(1)}, u32[]{:S(2)}, u32[]{:S(2)}) collective-permute-start(f32[4,4,8,128]{3,2,1,0:T(8,128)S(1)} %slice.29), channel_id=1, source_target_pairs={{0,2},{1,3},{2,0},{3,1},{4,6},{5,7},{6,4},{7,5},{8,10},{9,11},{10,... | collective-permute-start | bytes 196616 | tf_op jit(solution)/shard_map/ppermute | solution.py:532
  32.4 2.4 %collective-permute-done.5 = f32[4,4,8,128]{3,2,1,0:T(8,128)S(1)} collective-permute-done((f32[4,4,8,128]{3,2,1,0:T(8,128)S(1)}, f32[4,4,8,128]{3,2,1,0:T(8,128)S(1)}, u32[]{:S(2)}, u32[]{:S(2)}) %collective-permute-start.5) | collective-permute-done | bytes 65568 | tf_op jit(solution)/shard_map/ppermute | solution.py:532
  34.8 2.0 %collective-permute-start.6 = (f32[2,4,8,128]{3,2,1,0:T(8,128)S(1)}, f32[2,4,8,128]{3,2,1,0:T(8,128)S(1)}, u32[]{:S(2)}, u32[]{:S(2)}) collective-permute-start(f32[2,4,8,128]{3,2,1,0:T(8,128)S(1)} %slice.31), channel_id=1, source_target_pairs={{0,4},{1,5},{2,6},{3,7},{4,0},{5,1},{6,2},{7,3},{8,12},{9,13},{10,... | collective-permute-start | bytes 98312 | tf_op jit(solution)/shard_map/ppermute | solution.py:532
  36.8 2.0 %collective-permute-done.6 = f32[2,4,8,128]{3,2,1,0:T(8,128)S(1)} collective-permute-done((f32[2,4,8,128]{3,2,1,0:T(8,128)S(1)}, f32[2,4,8,128]{3,2,1,0:T(8,128)S(1)}, u32[]{:S(2)}, u32[]{:S(2)}) %collective-permute-start.6) | collective-permute-done | bytes 32800 | tf_op jit(solution)/shard_map/ppermute | solution.py:532
  38.8 3.0 %collective-permute-start.7 = (f32[1,4,8,128]{3,2,1,0:T(8,128)S(1)}, f32[1,4,8,128]{3,2,1,0:T(8,128)S(1)}, u32[]{:S(2)}, u32[]{:S(2)}) collective-permute-start(f32[1,4,8,128]{3,2,1,0:T(8,128)S(1)} %slice.32), channel_id=1, source_target_pairs={{0,8},{1,9},{2,10},{3,11},{4,12},{5,13},{6,14},{7,15},{8,0},{9,1},... | collective-permute-start | bytes 49160 | tf_op jit(solution)/shard_map/ppermute | solution.py:532
  41.8 1.7 %collective-permute-done.7.sent_ref = f32[1,4,8,128]{3,2,1,0:T(8,128)S(1)} collective-permute-done((f32[1,4,8,128]{3,2,1,0:T(8,128)S(1)}, f32[1,4,8,128]{3,2,1,0:T(8,128)S(1)}, u32[]{:S(2)}, u32[]{:S(2)}) %collective-permute-start.7) | collective-permute-done | bytes 16416 | tf_op jit(solution)/shard_map/ppermute | solution.py:532
  43.5 0.9 %update.1 = (f32[4,1024]{1,0:T(4,128)}, f32[4,1024]{1,0:T(4,128)}) custom-call(f32[2,4,8,128]{3,2,1,0:T(8,128)S(1)} %slice_add_fusion.2.kept_ref, f32[1,4,8,128]{3,2,1,0:T(8,128)S(1)} %collective-permute-done.7.sent_ref, f32[4,1024]{1,0:T(4,128)S(1)} %copy-done.1, f32[4,1024]{1,0:T(4,128)S(1)} %copy-done), custom_call_target="tpu_custom_call" | custom-call | tf_op jit(solution)/shard_map/update/pallas_call | solution.py:517
  (17 shorter events, 0.1 us)
Async XLA Ops:
  1.7 5.8 %collective-permute-start = (bf16[1,5,8,128]{3,2,1,0:T(8,128)(2,1)S(1)}, bf16[1,5,8,128]{3,2,1,0:T(8,128)(2,1)S(1)}, u32[]{:S(2)}, u32[]{:S(2)}) collective-permute-start(bf16[1,5,8,128]{3,2,1,0:T(8,128)(2,1)S(1)} %pack.1), channel_id=1, source_target_pairs={{0,8},{1,9},{2,10},{3,11},{4,12},{5,13},{6,14},{7,15},{8,0},{9,1},... | collective-permute-start | bytes 30728 | tf_op jit(solution)/shard_map/ppermute | solution.py:532
  7.4 3.8 %collective-permute-start.1 = (bf16[2,5,8,128]{3,2,1,0:T(8,128)(2,1)S(1)}, bf16[2,5,8,128]{3,2,1,0:T(8,128)(2,1)S(1)}, u32[]{:S(2)}, u32[]{:S(2)}) collective-permute-start(bf16[2,5,8,128]{3,2,1,0:T(8,128)(2,1)S(1)} %pad_maximum_fusion.2._), channel_id=1, source_target_pairs={{0,4},{1,5},{2,6},{3,7},{4,0},{5,1},{6,2},{7,3},{8,12},{9,13},{10,... | collective-permute-start | bytes 61448 | tf_op jit(solution)/shard_map/ppermute | solution.py:532
  11.2 4.1 %collective-permute-start.2 = (bf16[4,5,8,128]{3,2,1,0:T(8,128)(2,1)S(1)}, bf16[4,5,8,128]{3,2,1,0:T(8,128)(2,1)S(1)}, u32[]{:S(2)}, u32[]{:S(2)}) collective-permute-start(bf16[4,5,8,128]{3,2,1,0:T(8,128)(2,1)S(1)} %pad_maximum_fusion.1._), channel_id=1, source_target_pairs={{0,2},{1,3},{2,0},{3,1},{4,6},{5,7},{6,4},{7,5},{8,10},{9,11},{10,... | collective-permute-start | bytes 122888 | tf_op jit(solution)/shard_map/ppermute | solution.py:532
  15.3 1.3 %collective-permute-start.3 = (bf16[8,5,8,128]{3,2,1,0:T(8,128)(2,1)S(1)}, bf16[8,5,8,128]{3,2,1,0:T(8,128)(2,1)S(1)}, u32[]{:S(2)}, u32[]{:S(2)}) collective-permute-start(bf16[8,5,8,128]{3,2,1,0:T(8,128)(2,1)S(1)} %pad_maximum_fusion), channel_id=1, source_target_pairs={{0,1},{1,0},{2,3},{3,2},{4,5},{5,4},{6,7},{7,6},{8,9},{9,8},{10,11... | collective-permute-start | bytes 245768 | tf_op jit(solution)/shard_map/ppermute | solution.py:532
  16.7 26.9 %copy-start = (f32[4,1024]{1,0:T(4,128)S(1)}, f32[4,1024]{1,0:T(4,128)}, u32[]{:S(2)}) copy-start(f32[4,1024]{1,0:T(4,128)} %masters_ref.3) | copy-start | bytes 49156
  16.7 26.8 %copy-start.1 = (f32[4,1024]{1,0:T(4,128)S(1)}, f32[4,1024]{1,0:T(4,128)}, u32[]{:S(2)}) copy-start(f32[4,1024]{1,0:T(4,128)} %velocity_ref.1) | copy-start | bytes 49156
  29.0 1.4 %collective-permute-start.4 = (f32[8,4,8,128]{3,2,1,0:T(8,128)S(1)}, f32[8,4,8,128]{3,2,1,0:T(8,128)S(1)}, u32[]{:S(2)}, u32[]{:S(2)}) collective-permute-start(f32[8,4,8,128]{3,2,1,0:T(8,128)S(1)} %slice.22), channel_id=1, source_target_pairs={{0,1},{1,0},{2,3},{3,2},{4,5},{5,4},{6,7},{7,6},{8,9},{9,8},{10,11... | collective-permute-start | bytes 393224 | tf_op jit(solution)/shard_map/ppermute | solution.py:532
  30.5 4.3 %collective-permute-start.5 = (f32[4,4,8,128]{3,2,1,0:T(8,128)S(1)}, f32[4,4,8,128]{3,2,1,0:T(8,128)S(1)}, u32[]{:S(2)}, u32[]{:S(2)}) collective-permute-start(f32[4,4,8,128]{3,2,1,0:T(8,128)S(1)} %slice.29), channel_id=1, source_target_pairs={{0,2},{1,3},{2,0},{3,1},{4,6},{5,7},{6,4},{7,5},{8,10},{9,11},{10,... | collective-permute-start | bytes 196616 | tf_op jit(solution)/shard_map/ppermute | solution.py:532
  34.8 4.0 %collective-permute-start.6 = (f32[2,4,8,128]{3,2,1,0:T(8,128)S(1)}, f32[2,4,8,128]{3,2,1,0:T(8,128)S(1)}, u32[]{:S(2)}, u32[]{:S(2)}) collective-permute-start(f32[2,4,8,128]{3,2,1,0:T(8,128)S(1)} %slice.31), channel_id=1, source_target_pairs={{0,4},{1,5},{2,6},{3,7},{4,0},{5,1},{6,2},{7,3},{8,12},{9,13},{10,... | collective-permute-start | bytes 98312 | tf_op jit(solution)/shard_map/ppermute | solution.py:532
  38.8 4.7 %collective-permute-start.7 = (f32[1,4,8,128]{3,2,1,0:T(8,128)S(1)}, f32[1,4,8,128]{3,2,1,0:T(8,128)S(1)}, u32[]{:S(2)}, u32[]{:S(2)}) collective-permute-start(f32[1,4,8,128]{3,2,1,0:T(8,128)S(1)} %slice.32), channel_id=1, source_target_pairs={{0,8},{1,9},{2,10},{3,11},{4,12},{5,13},{6,14},{7,15},{8,0},{9,1},... | collective-permute-start | bytes 49160 | tf_op jit(solution)/shard_map/ppermute | solution.py:532
